TPU v7x, 32 devices: a whole 2x2x4 slice. The times are simulated.
32 devices in a mesh: dp: 2 (over x), ctx: 4 (over z), tp: 4 (over y, core).
Axes of the slice: x: 2, y: 2, z: 4, core: 2. Of those that a mesh axis runs over, the one named last changes fastest.
Arguments:
- tokens: bfloat16 [2, 2048, 4096], P('dp', 'ctx'), may hold values from -6 to 6
- norm_gain: float32 [4096], replicated, may hold values from 0.25 to 1.75
- zx_weight: bfloat16 [4096, 2, 8192], P(('dp', 'ctx'), None, 'tp'), may hold values from -0.09375 to 0.09375
- bc_weight: bfloat16 [4096, 2, 1024], P(('dp', 'ctx'), None, 'tp'), may hold values from -0.09375 to 0.09375
- dt_weight: bfloat16 [4096, 128], P(('dp', 'ctx'), 'tp'), may hold values from -0.09375 to 0.09375
- conv_x: float32 [5, 8192], P(None, 'tp'), may hold values from -3 to 3
- conv_bc: float32 [5, 2, 1024], P(None, None, 'tp'), may hold values from -3 to 3
- head_params: float32 [3, 128], P(None, 'tp'), may hold values from -12 to 4
- gate_gain: float32 [8192], P('tp'), may hold values from 0.25 to 1.75
- out_weight: bfloat16 [4096, 8192], P(('dp', 'ctx'), 'tp'), may hold values from -0.0625 to 0.0625
- cotangent: bfloat16 [2, 2048, 4096], P('dp', 'ctx'), may hold values from -6 to 6
Outputs:
- mixed: bfloat16 [2, 2048, 4096], P('dp', 'ctx')
- tokens_grad: float32 [2, 2048, 4096], P('dp', 'ctx')
- norm_gain_grad: float32 [4096], replicated
- zx_weight_grad: float32 [4096, 2, 8192], P(('dp', 'ctx'), None, 'tp')
- bc_weight_grad: float32 [4096, 2, 1024], P(('dp', 'ctx'), None, 'tp')
- dt_weight_grad: float32 [4096, 128], P(('dp', 'ctx'), 'tp')
- conv_x_grad: float32 [5, 8192], P(None, 'tp')
- conv_bc_grad: float32 [5, 2, 1024], P(None, None, 'tp')
- head_params_grad: float32 [3, 128], P(None, 'tp')
- gate_gain_grad: float32 [8192], P('tp')
- out_weight_grad: float32 [4096, 8192], P(('dp', 'ctx'), 'tp')
All inputs are finite; a program needn't handle non-finite values.
Results may differ from a plain program's by a relative error of at most 0.0049.
The roundings to bfloat16 on the way count: a program that leaves them out, or rounds other values in their place, can miss the bound.
Values may be sent and summed in bfloat16 or wider, within the bound.
A program may use at most 448 MiB of HBM per device.

v0:
```python
import jax
import jax.numpy as jnp
from jax import lax
from jax.sharding import PartitionSpec as P

P_SIZE = 64
N = 128
STRETCH = 256


EPS = 1e-05
HIGH = lax.Precision.HIGHEST


def shifted(value, axis, by):
    devices = lax.axis_size(axis)
    pairs = [(i, i + by) for i in range(devices) if 0 <= i + by < devices]
    return lax.ppermute(value, axis, pairs)


def carried_in(part, axis, combine, identity, reverse):
    count = lax.axis_size(axis)
    place = lax.axis_index(axis)
    ahead = count - 1 - place if reverse else place
    gathered = jax.tree.map(lambda a: lax.all_gather(a, axis), part)
    state = jax.tree.map(lambda a, e: jnp.zeros_like(a) + jnp.asarray(e, a.dtype), part, identity)

    def one(turn, state):
        source = count - 1 - turn if reverse else turn
        return combine(
            state, jax.tree.map(lambda a: lax.dynamic_index_in_dim(a, source, 0, False), gathered)
        )

    return lax.fori_loop(0, ahead, one, state)


def dot_last(left_side, right_side):
    return lax.dot_general(
        left_side, right_side, (((1,), (1,)), ((), ())), preferred_element_type=jnp.float32
    )


def dot_first(left_side, right_side):
    return lax.dot_general(
        left_side, right_side, (((0,), (0,)), ((), ())), preferred_element_type=jnp.float32
    )


def conv_silu(padded, kernel):
    tap_count = kernel.shape[0] - 1
    length = padded.shape[1] - tap_count + 1
    running = kernel[tap_count] + kernel[0] * padded[:, 0:length]
    for offset in range(1, tap_count):
        running = running + kernel[offset] * padded[:, offset : offset + length]
    return jax.nn.silu(running)


def block_step(memory, pieces, log_decay):
    x_heads, step_sizes, inject, readout = pieces
    block_len = x_heads.shape[0]
    groups = inject.shape[1]
    per_group = x_heads.shape[1] // groups
    head_dim = x_heads.shape[2]
    cumulative = jnp.cumsum(step_sizes * log_decay, axis=0)
    gap_matrix = cumulative[:, None, :] - cumulative[None, :, :]
    causal = jnp.tril(jnp.ones((block_len, block_len), jnp.float32))
    decays = jnp.exp(jnp.minimum(gap_matrix, 0.0)) * causal[:, :, None]
    scores = jnp.einsum("ign,jgn->ijg", readout, inject, precision=HIGH)
    mixing = decays.reshape(block_len, block_len, groups, per_group) * scores[:, :, :, None]
    scaled = (x_heads * step_sizes[:, :, None]).reshape(block_len, groups, per_group, head_dim)
    local_out = jnp.einsum("ijgh,jghp->ighp", mixing, scaled, precision=HIGH)
    carried = jnp.einsum("ign,ghpn->ighp", readout, memory, precision=HIGH)
    carried = carried * jnp.exp(cumulative).reshape(block_len, groups, per_group)[:, :, :, None]
    to_end = jnp.exp(cumulative[-1] - cumulative).reshape(block_len, groups, per_group)
    new_memory = memory * jnp.exp(cumulative[-1]).reshape(groups, per_group)[:, :, None, None]
    new_memory = new_memory + jnp.einsum(
        "jgn,jghp->ghpn", inject, scaled * to_end[:, :, :, None], precision=HIGH
    )
    return (new_memory, (local_out + carried).reshape(block_len, groups * per_group, head_dim))


def ssd_scan(x_heads, step_sizes, log_decay, inject, readout):
    length, head_count, head_dim = x_heads.shape
    groups, state_dim = (inject.shape[1], inject.shape[2])
    block_count = length // STRETCH
    pieces = (
        x_heads.reshape(block_count, STRETCH, head_count, head_dim),
        step_sizes.reshape(block_count, STRETCH, head_count),
        inject.reshape(block_count, STRETCH, groups, state_dim),
        readout.reshape(block_count, STRETCH, groups, state_dim),
    )
    zero_memory = jnp.zeros((groups, head_count // groups, head_dim, state_dim), jnp.float32)
    advance = jax.checkpoint(lambda memory, piece_set: block_step(memory, piece_set, log_decay))
    last_memory, outputs = lax.scan(advance, zero_memory, pieces)
    return (
        outputs.reshape(length, head_count, head_dim),
        last_memory.reshape(head_count, head_dim, state_dim),
    )


def local_states(x_flat, state_maps, raw_dt, head_params):
    seq_count, length, inner_width = x_flat.shape
    head_count = head_params.shape[1]
    groups = state_maps.shape[2] // (2 * N)
    step_sizes = jax.nn.softplus(raw_dt + head_params[0])
    log_decay = -jnp.exp(head_params[1])
    x_heads = x_flat.reshape(seq_count, length, head_count, P_SIZE)
    inject = state_maps[:, :, : groups * N].reshape(seq_count, length, groups, N)
    readout = state_maps[:, :, groups * N :].reshape(seq_count, length, groups, N)

    def single_seq(x_one, step_one, inject_one, readout_one):
        return ssd_scan(x_one, step_one, log_decay, inject_one, readout_one)

    outputs, last_memory = jax.vmap(single_seq)(x_heads, step_sizes, inject, readout)
    cumulative = jnp.cumsum(step_sizes * log_decay, axis=1)
    return (outputs, jnp.exp(cumulative[:, -1]), last_memory, cumulative)


def finish_heads(
    outputs, x_flat, state_maps, cumulative, start_state, gate_pre, head_params, gate_gain
):
    seq_count, length, inner_width = x_flat.shape
    head_count = head_params.shape[1]
    groups = state_maps.shape[2] // (2 * N)
    per_group = head_count // groups
    readout = state_maps[:, :, groups * N :].reshape(seq_count, length, groups, N)
    start_grouped = start_state.reshape(seq_count, groups, per_group, P_SIZE, N)
    carried = jnp.einsum("slgn,sghpn->slghp", readout, start_grouped, precision=HIGH)
    carried = carried * jnp.exp(cumulative).reshape(seq_count, length, groups, per_group)[..., None]
    x_heads = x_flat.reshape(seq_count, length, head_count, P_SIZE)
    total_out = (
        outputs
        + carried.reshape(seq_count, length, head_count, P_SIZE)
        + head_params[2][:, None] * x_heads
    )
    gated = total_out.reshape(seq_count, length, inner_width) * jax.nn.silu(gate_pre)
    grouped = gated.reshape(seq_count, length, groups, inner_width // groups)
    grouped = grouped * lax.rsqrt(jnp.mean(grouped * grouped, axis=-1, keepdims=True) + EPS)
    return grouped.reshape(seq_count, length, inner_width) * gate_gain


def combine_maps(earlier, later):
    return (later[0] * earlier[0], later[0][:, :, None, None] * earlier[1] + later[1])


def shards(
    tokens,
    norm_gain,
    zx_weight,
    bc_weight,
    dt_weight,
    conv_x,
    conv_bc,
    head_params,
    gate_gain,
    out_weight,
    cotangent,
):
    seq_count, length, model_width = tokens.shape
    row_count = seq_count * length
    inner_width = conv_x.shape[1]
    pair_width = bc_weight.shape[2]
    head_count = dt_weight.shape[1]
    shard_rows = dt_weight.shape[0]
    tap_count = conv_x.shape[0] - 1
    edge_rows = tap_count - 1
    hidden = tokens.astype(jnp.float32)
    rscale = lax.rsqrt(jnp.mean(hidden * hidden, axis=-1, keepdims=True) + EPS)
    normed = (hidden * rscale * norm_gain).astype(jnp.bfloat16).reshape(row_count, model_width)
    pieces = (
        lax.all_gather(zx_weight, ("dp", "ctx"), axis=0, tiled=True),
        lax.all_gather(bc_weight, ("dp", "ctx"), axis=0, tiled=True),
        lax.all_gather(dt_weight, ("dp", "ctx"), axis=0, tiled=True),
    )
    row_span = pieces[0].shape[0]
    columns = normed
    proj_zx = jnp.dot(
        columns, pieces[0].reshape(row_span, 2 * inner_width), preferred_element_type=jnp.float32
    )
    proj_bc = jnp.dot(
        columns, pieces[1].reshape(row_span, 2 * pair_width), preferred_element_type=jnp.float32
    )
    raw_dt = jnp.dot(columns, pieces[2], preferred_element_type=jnp.float32)
    gate_pre = proj_zx[:, :inner_width].reshape(seq_count, length, inner_width)
    conv_input = jnp.concatenate([proj_zx[:, inner_width:], proj_bc], axis=1).astype(jnp.bfloat16)
    conv_input = conv_input.reshape(seq_count, length, inner_width + 2 * pair_width)
    before_rows = shifted(conv_input[:, length - edge_rows :], "ctx", 1)
    padded = jnp.concatenate([before_rows, conv_input], axis=1).astype(jnp.float32)
    kernel = jnp.concatenate([conv_x, conv_bc.reshape(tap_count + 1, 2 * pair_width)], axis=1)
    conv_out, conv_back = jax.vjp(conv_silu, padded, kernel)
    conv_low = lax.optimization_barrier(conv_out.astype(jnp.bfloat16)).astype(jnp.float32)
    x_flat = conv_low[:, :, :inner_width]
    state_maps = conv_low[:, :, inner_width:]
    step_raw = raw_dt.reshape(seq_count, length, head_count)
    summary, states_back = jax.vjp(local_states, x_flat, state_maps, step_raw, head_params)
    outputs, span_decay, last_memory, cumulative = summary
    identity_pair = (jnp.ones_like(span_decay), jnp.zeros_like(last_memory))
    start_state = carried_in((span_decay, last_memory), "ctx", combine_maps, identity_pair, False)[
        1
    ]
    gated_full, finish_back = jax.vjp(
        finish_heads,
        outputs,
        x_flat,
        state_maps,
        cumulative,
        start_state,
        gate_pre,
        head_params,
        gate_gain,
    )
    gated_norm = gated_full.astype(jnp.bfloat16).reshape(row_count, inner_width)
    branch_out = dot_last(gated_norm, lax.all_gather(out_weight, ("dp", "ctx"), axis=0, tiled=True))
    flat_hidden = hidden.reshape(row_count, model_width)
    branch_total = lax.psum(branch_out, "tp")
    mixed = (flat_hidden + branch_total).astype(jnp.bfloat16)
    mixed = mixed.reshape(seq_count, length, model_width)
    flat_cot = cotangent.reshape(row_count, model_width)
    columns = flat_cot
    grad_gated = jnp.dot(
        columns,
        lax.all_gather(out_weight, ("dp", "ctx"), axis=0, tiled=True),
        preferred_element_type=jnp.float32,
    )
    (
        grad_outputs,
        grad_x_one,
        grad_maps_one,
        grad_cumul,
        grad_start,
        grad_gate,
        grad_head_one,
        gate_gain_grad,
    ) = finish_back(grad_gated.reshape(seq_count, length, inner_width))
    later_grad = carried_in((span_decay, grad_start), "ctx", combine_maps, identity_pair, True)[1]
    grad_decay = jnp.sum(later_grad * start_state, axis=(2, 3))
    grad_x_two, grad_maps_two, grad_step, grad_head_two = states_back(
        (grad_outputs, grad_decay, later_grad, grad_cumul)
    )
    grad_conv_out = jnp.concatenate(
        [grad_x_one + grad_x_two, grad_maps_one + grad_maps_two], axis=2
    )
    grad_padded, grad_kernel = conv_back(grad_conv_out)
    returned_rows = shifted(grad_padded[:, :edge_rows], "ctx", -1)
    grad_input = grad_padded[:, edge_rows:]
    grad_input = jnp.concatenate(
        [grad_input[:, : length - edge_rows], grad_input[:, length - edge_rows :] + returned_rows],
        axis=1,
    )
    grad_input = grad_input.reshape(row_count, inner_width + 2 * pair_width)
    grad_zx = jnp.concatenate(
        [grad_gate.reshape(row_count, inner_width), grad_input[:, :inner_width]], axis=1
    ).astype(jnp.bfloat16)
    grad_bc = grad_input[:, inner_width:].astype(jnp.bfloat16)
    grad_dt = grad_step.reshape(row_count, head_count).astype(jnp.bfloat16)
    pieces = (
        lax.all_gather(zx_weight, ("dp", "ctx"), axis=0, tiled=True),
        lax.all_gather(bc_weight, ("dp", "ctx"), axis=0, tiled=True),
        lax.all_gather(dt_weight, ("dp", "ctx"), axis=0, tiled=True),
    )
    row_span = pieces[0].shape[0]
    contrib = dot_last(grad_zx, pieces[0].reshape(row_span, 2 * inner_width))
    contrib = contrib + dot_last(grad_bc, pieces[1].reshape(row_span, 2 * pair_width))
    contrib = contrib + dot_last(grad_dt, pieces[2])
    grad_normed = contrib
    grad_normed = lax.psum(grad_normed, "tp")
    flat_scale = rscale.reshape(row_count, 1)
    grad_hat = grad_normed * norm_gain
    norm_gain_grad = jnp.sum(grad_normed * flat_hidden * flat_scale, axis=0)
    grad_hidden = flat_scale * grad_hat - flat_hidden * (
        flat_scale * flat_scale * flat_scale
    ) * jnp.mean(grad_hat * flat_hidden, axis=1, keepdims=True)
    tokens_grad = (flat_cot.astype(jnp.float32) + grad_hidden).reshape(
        seq_count, length, model_width
    )
    zx_end = 2 * inner_width
    bc_end = zx_end + 2 * pair_width
    dt_end = bc_end + head_count
    weight_sum = lax.psum_scatter(
        jnp.concatenate(
            [
                jnp.concatenate(
                    [
                        dot_first(normed, grad_zx),
                        dot_first(normed, grad_bc),
                        dot_first(normed, grad_dt),
                    ],
                    axis=1,
                ),
                dot_first(flat_cot, gated_norm),
            ],
            axis=1,
        ),
        ("dp", "ctx"),
        scatter_dimension=0,
        tiled=True,
    )
    out_weight_grad = weight_sum[:, dt_end:]
    zx_weight_grad = weight_sum[:, :zx_end].reshape(shard_rows, 2, inner_width)
    bc_weight_grad = weight_sum[:, zx_end:bc_end].reshape(shard_rows, 2, pair_width)
    dt_weight_grad = weight_sum[:, bc_end:dt_end]
    small_sums = lax.psum(
        (
            norm_gain_grad,
            grad_kernel[:, :inner_width],
            grad_kernel[:, inner_width:].reshape(tap_count + 1, 2, pair_width),
            grad_head_one + grad_head_two,
            gate_gain_grad,
        ),
        ("dp", "ctx"),
    )
    return (
        mixed,
        tokens_grad,
        small_sums[0],
        zx_weight_grad,
        bc_weight_grad,
        dt_weight_grad,
        small_sums[1],
        small_sums[2],
        small_sums[3],
        small_sums[4],
        out_weight_grad,
    )


def solution(mesh):
    return jax.shard_map(
        shards,
        mesh=mesh,
        in_specs=(
            P("dp", "ctx", None),
            P(),
            P(("dp", "ctx"), None, "tp"),
            P(("dp", "ctx"), None, "tp"),
            P(("dp", "ctx"), "tp"),
            P(None, "tp"),
            P(None, None, "tp"),
            P(None, "tp"),
            P("tp"),
            P(("dp", "ctx"), "tp"),
            P("dp", "ctx", None),
        ),
        out_specs=(
            P("dp", "ctx", None),
            P("dp", "ctx", None),
            P(),
            P(("dp", "ctx"), None, "tp"),
            P(("dp", "ctx"), None, "tp"),
            P(("dp", "ctx"), "tp"),
            P(None, "tp"),
            P(None, None, "tp"),
            P(None, "tp"),
            P("tp"),
            P(("dp", "ctx"), "tp"),
        ),
        check_vma=False,
    )
```

profile of v0, /device:TPU:0, one launch (start us, length us, event | category | flops | bytes accessed | tf_op | source)
XLA Modules:
  0.0 3656.5 jit_solution(2228593473752931483)
XLA Ops:
  8.8 34.3 all_gather.28
  50.5 38.7 %all-gather.8.cloned.1.call-done = bf16[4096,2,256]{2,1,0:T(2,128)(2,1)} async-done(((bf16[512,2,256]{2,1,0:T(2,128)(2,1)}), bf16[4096,2,256]{2,1,0:T(2,128)(2,1)}) %all-gather.8.cloned.1.call-update) | async-done | bytes 4194320 | tf_op jit(solution)/shard_map/all_gather | solution.py:172
  96.7 630.1 %all-gather.6.cloned.1.call-done = bf16[4096,2,2048]{2,1,0:T(2,128)(2,1)} async-done(((bf16[512,2,2048]{2,1,0:T(2,128)(2,1)}), bf16[4096,2,2048]{2,1,0:T(2,128)(2,1)}) %all-gather.6.cloned.1.call-update) | async-done | bytes 33554448 | tf_op jit(solution)/shard_map/all_gather | solution.py:171
  726.8 23.2 copy.526
  750.0 22.8 fusion.190
  807.3 44.8 %while.68 = (s32[]{:T(128)}, f32[1,2,16,64,128]{4,3,2,1,0:T(8,128)S(1)}, f32[2,1,256,32,64]{2,4,3,1,0:T(8,128)}, f32[2,1,2,16,64,128]{5,4,3,2,1,0:T(8,128)}, f32...) while((s32[]{:T(128)}, ...), condition=%wide.region_4.5_spmd.clone, body=%wide.region_1.4_spmd.clone.sunk | while | flops 3436068864 | bytes 62821912 | solution.py:94
  859.1 12.9 all_gather.31
  892.1 44.2 %all-gather.10.cloned.1.call-done = f32[4,1,32,64,128]{4,3,2,1,0:T(8,128)} async-done(((f32[1,1,32,64,128]{4,3,2,1,0:T(8,128)}), f32[4,1,32,64,128]{4,3,2,1,0:T(8,128)}) %all-gather.10.cloned.1.call-update) | async-done | bytes 4194320 | tf_op jit(solution)/shard_map/all_gather | solution.py:25
  947.2 217.2 %all-gather.12.cloned.1.call-done = bf16[4096,2048]{1,0:T(8,128)(2,1)} async-done(((bf16[512,2048]{1,0:T(8,128)(2,1)}), bf16[4096,2048]{1,0:T(8,128)(2,1)}) %all-gather.12.cloned.1.call-update) | async-done | bytes 16777232 | tf_op jit(solution)/shard_map/all_gather | solution.py:213
  1164.4 21.4 multiply_multiply_fusion
  1270.1 12.2 multiply_reduce_fusion.6
  1282.3 15.4 convolution_bitcast_fusion.3
  1297.7 14.9 fusion.201
  1338.5 164.0 %while.69 = (s32[]{:T(128)}, f32[32]{0:T(128)}, f32[1,2,16,64,128]{4,3,2,1,0:T(8,128)S(1)}, f32[2,1,256,32,64]{2,4,3,1,0:T(8,128)}, f32[2,1,256,32]{2,0,3,1:T(2,...) while((s32[]{:T(128)}, f32[32]{0:T(128)}, ...), condition=%wide.region_28.29_spmd.clone, body=%wide.region_14.28_spmd.clone.sunk | while | flops 7901773824 | bytes 110699288 | solution.py:94
  1369.3 14.5 fusion.297
  1450.7 14.5 fusion.297
  1571.0 22.9 fusion.158
  1605.0 30.2 fusion.157
  1642.3 74.9 %pad_maximum_fusion = f32[4096,6688]{0,1:T(8,128)} fusion(f32[4096,2048]{0,1:T(8,128)} %convolution_bitcast_fusion.3, f32[4096,32]{0,1:T(8,128)S(1)} %fusion.177, f32[4096,512]{0,1:T(8,128)} %fusion.164, f32[4096,4096]{0,1:T(8,128)} %fusion.157), kind=kLoop, calls=%fused_computation.166 | loop fusion | flops 82182144 | bytes 219152384 | tf_op jit(solution)/shard_map/concatenate | solution.py:280
  1720.8 170.7 %all-reduce.25.cloned.1.call-done = (f32[512,4096]{1,0:T(8,128)}, f32[512,4096]{1,0:T(8,128)}) async-done(((f32[512,4096]{1,0:T(8,128)}, f32[512,4096]{1,0:T(8,128)}), (f32[512,4096]{1,0:T(8,128)}, f32[512,4096]{1,0:T(8,128)})) %all-reduce.25.cloned.1.call-update) | async-done | bytes 16777232 | tf_op jit(solution)/shard_map/psum | solution.py:215
  1898.9 15.8 fusion.130
  1914.8 1653.0 %reduce-scatter.2.cloned.1.call-done = f32[512,6688]{0,1:T(8,128)} async-done(((f32[4096,6688]{0,1:T(8,128)}), f32[512,6688]{0,1:T(8,128)}) %reduce-scatter.2.cloned.1.call-update) | async-done | bytes 13697040 | tf_op jit(solution)/shard_map/reduce_scatter | solution.py:279
  3578.0 13.3 copy.448
  3602.6 40.1 %all-reduce.23.cloned.1.call-done = (f32[4096]{0:T(1024)}, f32[5,2048]{1,0:T(8,128)}, f32[5,2,256]{2,1,0:T(2,128)}, f32[3,32]{1,0:T(4,128)}, f32[2048]{0:T(1024)}) async-done(((f32[4096]{0:T(1024)}, f32[5,2048]{1,0:T(8,128)}, f32[5,2,256]{2,1,0:T(2,128)}, f32[3,32]{1,0:T(4,128)}, f32[2048]{0:T(1024)}), (f32[4096]{0:T(1024)}, f32[5,2048]{1,0:T(8,128)}, f32[5,2,256]{2,1,0:T(2,128)}, f32[3,32]{1,0:T(4,128)}, ...) | async-done | bytes 76176 | tf_op jit(solution)/shard_map/psum | solution.py:302
  (525 shorter events, 506.6 us)
Async XLA Ops:
  7.2 35.9 copy-start.77
  7.2 82.0 %all-gather.8.cloned.1.call-start = ((), (), s32[]{:S(2)}) async-start(), calls=%async_computation.2 | async-start | bytes 4718592 | tf_op jit(solution)/shard_map/all_gather | solution.py:172
  7.9 39.5 %copy-start.56 = (f32[4096]{0:T(1024)S(1)}, f32[4096]{0:T(1024)}, u32[]{:S(2)}) copy-start(f32[4096]{0:T(1024)} %param.20) | copy-start | bytes 49156
  8.0 718.8 %all-gather.6.cloned.1.call-start = ((), (), s32[]{:S(2)}) async-start(), calls=%async_computation.1 | async-start | bytes 37748736 | tf_op jit(solution)/shard_map/all_gather | solution.py:171
  8.7 927.6 %all-gather.10.cloned.1.call-start = ((), (), s32[]{:S(2)}) async-start(), calls=%async_computation.3 | async-start | bytes 5242880 | tf_op jit(solution)/shard_map/all_gather | solution.py:25
  8.8 38.7 %copy-start.19 = (bf16[1,512,4096]{2,1,0:T(8,128)(2,1)S(1)}, bf16[1,512,4096]{2,1,0:T(8,128)(2,1)}, u32[]{:S(2)}) copy-start(bf16[1,512,4096]{2,1,0:T(8,128)(2,1)} %param.19) | copy-start | bytes 12582916
  47.4 702.5 %copy-start.70 = (f32[512]{0:T(512)}, f32[512]{0:T(512)S(1)}, u32[]{:S(2)}) copy-start(f32[512]{0:T(512)S(1)} %get-tuple-element.1004) | copy-start | bytes 6148
  50.5 728.6 %copy-start.48 = (f32[2560]{0:T(1024)}, f32[2560]{0:T(1024)S(1)}, u32[]{:S(2)}) copy-start(f32[2560]{0:T(1024)S(1)} %get-tuple-element.881) | copy-start | bytes 30724
  50.5 728.6 %copy-start.50 = (f32[2560]{0:T(1024)}, f32[2560]{0:T(1024)S(1)}, u32[]{:S(2)}) copy-start(f32[2560]{0:T(1024)S(1)} %get-tuple-element.882) | copy-start | bytes 30724
  50.5 728.6 %copy-start.52 = (f32[2560]{0:T(1024)}, f32[2560]{0:T(1024)S(1)}, u32[]{:S(2)}) copy-start(f32[2560]{0:T(1024)S(1)} %get-tuple-element.883) | copy-start | bytes 30724
  50.5 728.6 %copy-start.54 = (f32[2560]{0:T(1024)}, f32[2560]{0:T(1024)S(1)}, u32[]{:S(2)}) copy-start(f32[2560]{0:T(1024)S(1)} %get-tuple-element.884) | copy-start | bytes 30724
  773.5 4.9 collective-permute-start
  853.3 18.7 copy-start.13
  853.3 311.1 %all-gather.12.cloned.1.call-start = ((), (), s32[]{:S(2)}) async-start(), calls=%async_computation.4 | async-start | bytes 18874368 | tf_op jit(solution)/shard_map/all_gather | solution.py:213
  853.9 468.3 %all-gather.14.cloned.1.call-start = ((), (), s32[]{:S(2)}) async-start(), calls=%async_computation.5 | async-start | bytes 5242880 | tf_op jit(solution)/shard_map/all_gather | solution.py:25
  854.1 310.3 %copy-start.68 = (f32[2048]{0:T(1024)}, f32[2048]{0:T(1024)S(1)}, u32[]{:S(2)}) copy-start(f32[2048]{0:T(1024)S(1)} %mul.940) | copy-start | bytes 24580
  941.6 222.8 %copy-start.65 = (f32[2048]{0:T(1024)S(1)}, f32[2048]{0:T(1024)}, u32[]{:S(2)}) copy-start(f32[2048]{0:T(1024)} %param.27) | copy-start | bytes 24580
  1243.1 648.4 %all-reduce.25.cloned.1.call-start = ((), (), s32[]{:S(2)}) async-start(), calls=%async_computation.8 | async-start | bytes 33554432 | tf_op jit(solution)/shard_map/psum | solution.py:215
  1369.3 15.7 copy-start.40
  1552.7 9.5 collective-permute-start.1
  1571.0 22.9 copy-start.44
  1604.3 1963.4 %reduce-scatter.2.cloned.1.call-start = ((), (), s32[]{:S(2)}) async-start(), calls=%async_computation.6 | async-start | bytes 123273216 | tf_op jit(solution)/shard_map/reduce_scatter | solution.py:279
  1605.0 30.2 copy-start.21
  1717.3 1925.5 %all-reduce.23.cloned.1.call-start = ((), (), s32[]{:S(2)}) async-start(), calls=%async_computation.7 | async-start | bytes 204800 | tf_op jit(solution)/shard_map/psum | solution.py:302
  (87 other events, 419.5 us)
Sparse Core Ops, SparseCore 0:
  10.2 79.0 all-gather.7
  90.8 635.9 all-gather.5
  853.4 82.7 all-gather.9
  938.2 226.1 all-gather.11
  1243.2 78.9 all-gather.13
  1604.5 287.0 all-reduce.24
  1895.4 1672.3 reduce-scatter.1
  3573.3 69.3 all-reduce.22
where the time goes:
time: 3670 us; the launch traced here: 3660 us
  waiting for transfers between devices  2810 us (77%)
  matrix products  286 us (8%)
  local copies, waits for them, and re-layouts  263 us (7%)
  other arithmetic  231 us (6%)
  blocking collectives  47.2 us (1%)
    reduce_scatter x1, waiting for transfers between devices, shards(): lax.psum_scatter(jnp.concatenate([jnp.concatenate([dot_first(normed, grad...  1650 us
    all_gather x1, waiting for transfers between devices, shards(): lax.all_gather(zx_weight, ('dp', 'ctx'), axis=0, tiled=True)  630 us
    all_gather x1, waiting for transfers between devices, shards(): lax.all_gather(out_weight, ('dp', 'ctx'), axis=0, tiled=True)  217 us
    psum x1, waiting for transfers between devices, shards(): branch_total = lax.psum(branch_out, 'tp')  171 us
    unnamed x144, local copies, waits for them, and re-layouts  87.5 us
    concatenate x1, other arithmetic, shards(): jnp.concatenate([jnp.concatenate([dot_first(normed, grad_zx), dot_first(n...  74.9 us
  transfers between devices with their start and end apart: 10, of which 9 were waited for; matrix products, arithmetic and copies ran while one was open for 8% of the time, Pallas kernels for 0%

commit v1 on v0

v1 whole, which is shorter than its diff:
```python
import jax
import jax.numpy as jnp
from jax import lax
from jax.sharding import PartitionSpec as P

P_SIZE = 64
N = 128
STRETCH = 256
EPS = 1e-05
HIGH = lax.Precision.HIGHEST
F32 = jnp.float32
BF16 = jnp.bfloat16


def dot_last(left_side, right_side):
    return lax.dot_general(left_side, right_side, (((1,), (1,)), ((), ())), preferred_element_type=F32)


def dot_first(left_side, right_side):
    return lax.dot_general(left_side, right_side, (((0,), (0,)), ((), ())), preferred_element_type=F32)


def conv_silu(padded, kernel):
    tap_count = kernel.shape[0] - 1
    length = padded.shape[0] - tap_count + 1
    running = kernel[tap_count] + kernel[0] * padded[0:length]
    for offset in range(1, tap_count):
        running = running + kernel[offset] * padded[offset : offset + length]
    return jax.nn.silu(running)


def block_step(memory, pieces, log_decay):
    x_heads, step_sizes, inject, readout = pieces
    block_len = x_heads.shape[0]
    cumulative = jnp.cumsum(step_sizes * log_decay, axis=0)
    gap_matrix = cumulative[:, None, :] - cumulative[None, :, :]
    causal = jnp.tril(jnp.ones((block_len, block_len), F32))
    decays = jnp.exp(jnp.minimum(gap_matrix, 0.0)) * causal[:, :, None]
    scores = jnp.einsum("in,jn->ij", readout, inject, precision=HIGH)
    mixing = decays * scores[:, :, None]
    scaled = x_heads * step_sizes[:, :, None]
    local_out = jnp.einsum("ijh,jhp->ihp", mixing, scaled, precision=HIGH)
    carried = jnp.einsum("in,hpn->ihp", readout, memory, precision=HIGH)
    carried = carried * jnp.exp(cumulative)[:, :, None]
    to_end = jnp.exp(cumulative[-1] - cumulative)
    new_memory = memory * jnp.exp(cumulative[-1])[:, None, None]
    new_memory = new_memory + jnp.einsum("jn,jhp->hpn", inject, scaled * to_end[:, :, None], precision=HIGH)
    return (new_memory, local_out + carried)


def mixer(x_flat, maps, raw_dt, head_params):
    length, width = x_flat.shape
    heads = head_params.shape[1]
    count = length // STRETCH
    step_sizes = jax.nn.softplus(raw_dt + head_params[0])
    log_decay = -jnp.exp(head_params[1])
    x_heads = x_flat.reshape(length, heads, P_SIZE)
    pieces = (
        x_heads.reshape(count, STRETCH, heads, P_SIZE),
        step_sizes.reshape(count, STRETCH, heads),
        maps[:, :N].reshape(count, STRETCH, N),
        maps[:, N:].reshape(count, STRETCH, N),
    )
    zero_memory = jnp.zeros((heads, P_SIZE, N), F32)
    advance = jax.checkpoint(lambda memory, piece_set: block_step(memory, piece_set, log_decay))
    _, outputs = lax.scan(advance, zero_memory, pieces)
    outputs = outputs.reshape(length, heads, P_SIZE) + head_params[2][:, None] * x_heads
    return outputs.reshape(length, width)


def spread_rows(value):
    part = value.shape[0] // lax.axis_size("tp")
    mine = lax.dynamic_slice_in_dim(value, lax.axis_index("tp") * part, part, 0)
    along = lax.all_gather(mine, "ctx", axis=0)
    return lax.all_gather(along, "tp", axis=1).reshape(-1, value.shape[1])


def fetch_weight(packed):
    mine = lax.all_to_all(packed, "ctx", 0, 0, tiled=True)
    return lax.all_gather(mine.reshape(-1, packed.shape[2]), "dp", axis=0, tiled=True)


def return_grad(grad, rows):
    ndp, nctx = lax.axis_size("dp"), lax.axis_size("ctx")
    parts = grad.astype(BF16).reshape(ndp, nctx * rows, grad.shape[1])
    summed = jnp.sum(lax.all_to_all(parts, "dp", 0, 0, tiled=True).astype(F32), axis=0)
    back = lax.all_to_all(summed.astype(BF16).reshape(nctx, rows, grad.shape[1]), "ctx", 0, 0, tiled=True)
    return back.astype(F32)


def sum_rows(partial):
    return lax.psum_scatter(partial.astype(BF16), ("ctx", "tp"), scatter_dimension=0, tiled=True).astype(F32)


def shards(tokens, norm_gain, zx_weight, bc_weight, dt_weight, conv_x, conv_bc, head_params, gate_gain, out_weight, cotangent):
    seq_count, length, model_width = tokens.shape
    assert seq_count == 1
    nctx, ntp, ndp = lax.axis_size("ctx"), lax.axis_size("tp"), lax.axis_size("dp")
    ctx = lax.axis_index("ctx")
    rows = dt_weight.shape[0]
    inner = conv_x.shape[1]
    groups = bc_weight.shape[2] // N
    share = nctx // groups
    assert share == 2 and groups * share == nctx
    width = inner // nctx
    heads = dt_weight.shape[1] // nctx
    taps = conv_x.shape[0] - 1
    group_width = inner // groups

    def mine(value):
        return lax.dynamic_index_in_dim(value, ctx, 0, False)

    def partner(value):
        return lax.ppermute(value, "ctx", [(i, i ^ 1) for i in range(nctx)])

    hidden = tokens.astype(F32).reshape(length, model_width)
    cot = cotangent.reshape(length, model_width)
    rscale = lax.rsqrt(jnp.mean(hidden * hidden, axis=-1, keepdims=True) + EPS)
    normed = (hidden * rscale * norm_gain).astype(BF16)

    zx = zx_weight.reshape(rows, 2, nctx, width)
    bc = jnp.repeat(bc_weight.reshape(rows, 2, groups, N), share, axis=2)
    packed = jnp.concatenate(
        [zx[:, 0], zx[:, 1], bc[:, 0], bc[:, 1], dt_weight.reshape(rows, nctx, heads)], axis=2
    ).transpose(1, 0, 2)
    weight_in = fetch_weight(packed)
    weight_out = fetch_weight(out_weight.reshape(rows, nctx, width).transpose(1, 0, 2))
    normed_all = spread_rows(normed)
    cot_all = spread_rows(cot)

    proj = jnp.dot(normed_all, weight_in, preferred_element_type=F32)
    gate_pre = proj[:, :width]
    conv_width = width + 2 * N
    conv_input = proj[:, width : width + conv_width].astype(BF16)
    raw_dt = proj[:, width + conv_width :]
    padded = jnp.concatenate([jnp.zeros((taps - 1, conv_width), BF16), conv_input], axis=0).astype(F32)
    kernel_x = mine(conv_x.reshape(taps + 1, nctx, width).transpose(1, 0, 2))
    kernel_bc = conv_bc.reshape(taps + 1, 2, groups, N)
    kernel_bc = lax.dynamic_index_in_dim(kernel_bc, ctx // share, 2, False)
    kernel = jnp.concatenate([kernel_x, kernel_bc.reshape(taps + 1, 2 * N)], axis=1)
    conv_out = conv_silu(padded, kernel)
    conv_low = lax.optimization_barrier(conv_out.astype(BF16)).astype(F32)
    heads_mine = mine(head_params.reshape(3, nctx, heads).transpose(1, 0, 2))
    gain = mine(gate_gain.reshape(nctx, width))
    ssd, mixer_back = jax.vjp(mixer, conv_low[:, :width], conv_low[:, width:], raw_dt, heads_mine)

    sig = jax.nn.sigmoid(gate_pre)
    gate = gate_pre * sig
    gated = ssd * gate
    grad_gated = jnp.dot(cot_all, weight_out, preferred_element_type=F32)
    grad_scaled = grad_gated * gain
    sums = jnp.stack([jnp.sum(gated * gated, axis=1), jnp.sum(grad_scaled * gated, axis=1)])
    sums = (sums + partner(sums)) / group_width
    inverse = lax.rsqrt(sums[0] + EPS)[:, None]
    gated_norm = (gated * inverse * gain).astype(BF16)
    branch = sum_rows(dot_last(gated_norm, weight_out))
    part = length // ntp
    hidden_part = lax.dynamic_slice_in_dim(hidden, lax.axis_index("tp") * part, part, 0)
    mixed = lax.all_gather((hidden_part + branch).astype(BF16), "tp", axis=0, tiled=True)
    grad_out = return_grad(dot_first(cot_all, gated_norm), rows)

    gate_gain_grad = jnp.sum(grad_gated * gated * inverse, axis=0)
    grad_pre = inverse * grad_scaled - gated * (inverse * inverse * inverse * sums[1][:, None])
    grad_ssd = grad_pre * gate
    grad_gate = (grad_pre * ssd * (sig * (1.0 + gate_pre * (1.0 - sig)))).astype(BF16)
    grad_x, grad_maps, grad_dt, grad_heads = mixer_back(grad_ssd)

    odd = ctx % 2
    own_maps = lax.dynamic_slice_in_dim(grad_maps, odd * N, N, 1)
    send_maps = lax.dynamic_slice_in_dim(grad_maps, (1 - odd) * N, N, 1)
    own_maps = own_maps + partner(send_maps)
    own_padded = jnp.concatenate([padded[:, :width], lax.dynamic_slice_in_dim(padded, width + odd * N, N, 1)], axis=1)
    own_kernel = jnp.concatenate([kernel[:, :width], lax.dynamic_slice_in_dim(kernel, width + odd * N, N, 1)], axis=1)
    _, conv_back = jax.vjp(conv_silu, own_padded, own_kernel)
    grad_padded, grad_kernel = conv_back(jnp.concatenate([grad_x, own_maps], axis=1))
    grad_input = grad_padded[taps - 1 :].astype(BF16)
    grad_all = jnp.concatenate([grad_gate, grad_input, grad_dt.astype(BF16)], axis=1)
    own_weight = jnp.concatenate(
        [
            weight_in[:, : 2 * width],
            lax.dynamic_slice_in_dim(weight_in, 2 * width + odd * N, N, 1),
            weight_in[:, 2 * width + 2 * N :],
        ],
        axis=1,
    )
    normed_part = sum_rows(dot_last(grad_all, own_weight))
    grad_normed = lax.all_gather(normed_part.astype(BF16), "tp", axis=0, tiled=True).astype(F32)
    grad_in = return_grad(dot_first(normed_all, grad_all), rows)

    grad_hat = grad_normed * norm_gain
    norm_gain_grad = jnp.sum(grad_normed * hidden * rscale, axis=0)
    grad_hidden = rscale * grad_hat - hidden * (rscale * rscale * rscale) * jnp.mean(
        grad_hat * hidden, axis=1, keepdims=True
    )
    tokens_grad = cot.astype(F32) + grad_hidden

    zx_weight_grad = jnp.stack([grad_in[:, :, :width], grad_in[:, :, width : 2 * width]], axis=2)
    zx_weight_grad = zx_weight_grad.transpose(1, 2, 0, 3).reshape(rows, 2, inner)
    bc_weight_grad = grad_in[:, :, 2 * width : 2 * width + N].reshape(groups, 2, rows, N)
    bc_weight_grad = bc_weight_grad.transpose(2, 1, 0, 3).reshape(rows, 2, groups * N)
    dt_weight_grad = grad_in[:, :, 2 * width + N :].transpose(1, 0, 2).reshape(rows, nctx * heads)
    out_weight_grad = grad_out.transpose(1, 0, 2).reshape(rows, inner)

    small = jnp.concatenate([grad_kernel.reshape(-1), grad_heads.reshape(-1), gate_gain_grad])
    table = lax.dynamic_update_slice(jnp.zeros((nctx, small.shape[0]), F32), small[None], (ctx, 0))
    table, norm_gain_grad = lax.psum((table, norm_gain_grad), ("dp", "ctx"))
    kernel_end = (taps + 1) * (width + N)
    heads_end = kernel_end + 3 * heads
    kernels = table[:, :kernel_end].reshape(nctx, taps + 1, width + N)
    conv_x_grad = kernels[:, :, :width].transpose(1, 0, 2).reshape(taps + 1, inner)
    conv_bc_grad = kernels[:, :, width:].reshape(groups, 2, taps + 1, N).transpose(2, 1, 0, 3)
    conv_bc_grad = conv_bc_grad.reshape(taps + 1, 2, groups * N)
    head_grad = table[:, kernel_end:heads_end].reshape(nctx, 3, heads).transpose(1, 0, 2).reshape(3, nctx * heads)
    gate_gain_grad = table[:, heads_end:].reshape(inner)
    return (
        mixed.reshape(tokens.shape),
        tokens_grad.reshape(tokens.shape),
        norm_gain_grad,
        zx_weight_grad,
        bc_weight_grad,
        dt_weight_grad,
        conv_x_grad,
        conv_bc_grad,
        head_grad,
        gate_gain_grad,
        out_weight_grad,
    )


def solution(mesh):
    wide = P(("dp", "ctx"), None, "tp")
    flat = P(("dp", "ctx"), "tp")
    rows = P("dp", "ctx", None)
    return jax.shard_map(
        shards,
        mesh=mesh,
        in_specs=(rows, P(), wide, wide, flat, P(None, "tp"), P(None, None, "tp"), P(None, "tp"), P("tp"), flat, rows),
        out_specs=(rows, rows, P(), wide, wide, flat, P(None, "tp"), P(None, None, "tp"), P(None, "tp"), P("tp"), flat),
        check_vma=False,
    )
```

time: 3670 us -> 1670 us (0.46)
  waiting for transfers between devices: 2810 us -> 711 us
  local copies, waits for them, and re-layouts: 263 us -> 412 us
  other arithmetic: 231 us -> 159 us
    reduce_scatter x1 -> x2, waiting for transfers between devices: 1650 us -> 0.03 us  [sum_rows(): lax.psum_scatter(partial.astype(BF16), ('ctx', 'tp'), scatter_dimension=0...]
    all_gather x5 -> x8, waiting for transfers between devices: 940 us -> 178 us  [the longest x2 107 us: spread_rows(): return lax.all_gather(along, 'tp', axis=1).reshape(-1, value.shape[1])]
    all_to_all x0 -> x5, waiting for transfers between devices: none -> 457 us  [the longest x1 231 us: fetch_weight(): mine = lax.all_to_all(packed, 'ctx', 0, 0, tiled=True)]
    dynamic_update_slice x10 -> x33, local copies, waits for them, and re-layouts: 11.2 us -> 213 us  [the longest x32 213 us: mixer(): _, outputs = lax.scan(advance, zero_memory, pieces)]
    psum x2 -> x1, waiting for transfers between devices: 211 us -> 57.9 us  [shards(): table, norm_gain_grad = lax.psum((table, norm_gain_grad), ('dp', 'ctx'))]
    concatenate x3 -> x1, other arithmetic: 75.1 us -> 0.01 us  [shards(): jnp.concatenate([kernel_x, kernel_bc.reshape(taps + 1, 2 * N)], axis=1)]
    all_to_all x0 -> x1, blocking collectives: none -> 52.3 us  [fetch_weight(): mine = lax.all_to_all(packed, 'ctx', 0, 0, tiled=True)]
    all_gather x2 -> x0, blocking collectives: 47.2 us -> none  [the longest x1 34.3 us: shards(): lax.all_gather(dt_weight, ('dp', 'ctx'), axis=0, tiled=True)]
  transfers between devices with their start and end apart: 10 -> 18, of which waited for: 9 -> 9; matrix products, arithmetic and copies ran while one was open for 8% -> 45% of each run, Pallas kernels for 0% -> 0%
where the time goes in v1:
time: 1670 us; the launch traced here: 1660 us
  waiting for transfers between devices  711 us (43%)
  local copies, waits for them, and re-layouts  412 us (25%)
  matrix products  274 us (16%)
  other arithmetic  159 us (10%)
  blocking collectives  52.3 us (3%)
  starting transfers between devices  31.1 us (2%)
    all_to_all x1, waiting for transfers between devices, fetch_weight(): mine = lax.all_to_all(packed, 'ctx', 0, 0, tiled=True)  231 us
    dynamic_update_slice x32, local copies, waits for them, and re-layouts, mixer(): _, outputs = lax.scan(advance, zero_memory, pieces)  213 us
    all_to_all x2, waiting for transfers between devices, return_grad(): lax.all_to_all(summed.astype(BF16).reshape(nctx, rows, grad.shape[1]), 'c...  119 us
    all_gather x2, waiting for transfers between devices, spread_rows(): return lax.all_gather(along, 'tp', axis=1).reshape(-1, value.shape[1])  107 us
    all_to_all x2, waiting for transfers between devices, return_grad(): lax.all_to_all(parts, 'dp', 0, 0, tiled=True).astype(F32)  107 us
    unnamed x101, local copies, waits for them, and re-layouts  77.8 us
    dot_general x24, matrix products, block_step(): local_out = jnp.einsum('ijh,jhp->ihp', mixing, scaled, precision=HIGH)  71.3 us
    all_gather x2, waiting for transfers between devices, fetch_weight(): lax.all_gather(mine.reshape(-1, packed.shape[2]), 'dp', axis=0, tiled=True)  70.5 us
  transfers between devices with their start and end apart: 18, of which 9 were waited for; matrix products, arithmetic and copies ran while one was open for 45% of the time, Pallas kernels for 0%

profile of v1, /device:TPU:0, one launch (start us, length us, event | category | flops | bytes accessed | tf_op | source)
XLA Modules:
  0.0 1657.0 jit_solution(5033758154530576964)
XLA Ops:
  49.2 230.9 %all-to-all-done = bf16[4,512,1288]{1,2,0:T(8,128)(2,1)} async-done(((bf16[4,512,1288]{1,2,0:T(8,128)(2,1)}), bf16[4,512,1288]{1,2,0:T(8,128)(2,1)}, u32[]{:S(2)}, u32[]{:S(2)}) %all-to-all-start) | async-done | bytes 5275680 | tf_op jit(solution)/shard_map/all_to_all | solution.py:79
  289.8 52.3 %all_to_all.30 = bf16[4,512,512]{1,2,0:T(8,128)(2,1)S(1)} all-to-all(bf16[4,512,512]{1,2,0:T(8,128)(2,1)} %bitcast.402), channel_id=1, replica_groups=mesh['dp'=2,'ctx'=4,'tp'=4] {'ctx'}, dimensions={0} | all-to-all | bytes 4194304 | tf_op jit(solution)/shard_map/all_to_all | solution.py:79
  346.6 70.5 %all-gather.12.cloned.1.call-done = bf16[4096,1288]{0,1:T(8,128)(2,1)} async-done(((bf16[2048,1288]{0,1:T(8,128)(2,1)}), bf16[4096,1288]{0,1:T(8,128)(2,1)}) %all-gather.12.cloned.1.call-update) | async-done | bytes 10551312 | tf_op jit(solution)/shard_map/all_gather | solution.py:80
  417.1 107.4 %all-gather.24.cloned.1.call-done = bf16[4,512,4096]{2,1,0:T(8,128)(2,1)} async-done(((bf16[4,128,4096]{2,1,0:T(8,128)(2,1)}), bf16[4,512,4096]{2,1,0:T(8,128)(2,1)}) %all-gather.24.cloned.1.call-update) | async-done | bytes 16777232 | tf_op jit(solution)/shard_map/all_gather | solution.py:75
  524.5 26.9 %fusion.166 = f32[2048,1288]{0,1:T(8,128)S(1)} fusion(bf16[2048,4096]{1,0:T(8,128)(2,1)} %bitcast.442, bf16[4096,1288]{0,1:T(8,128)(2,1)} %all-gather.12.cloned.1.call-done), kind=kOutput, calls=%fused_computation.308 | convolution fusion | flops 21609054208 | bytes 37879808 | tf_op jit(solution)/shard_map/dot_general | solution.py:131
  581.7 171.9 %while.40 = (s32[]{:T(128)}, f32[8,64,128]{2,1,0:T(8,128)S(1)}, f32[8,256,8,64]{1,0,3,2:T(8,128)}, f32[8,8,64,128]{3,2,1,0:T(8,128)}, f32[8,256,8]{1,2,0:T(8,128...) while((s32[]{:T(128)}, f32[8,64,128]{2,1,0:T(8,128)S(1)}, ...), condition=%wide.region_4.5_spmd.clone, body=%wide.region_1.4_spmd.clone.sunk | while | flops 909447168 | bytes 7737156 | solution.py:66
  590.4 13.1 dynamic_update_slice.67
  760.5 19.1 %multiply_reduce_fusion.12 = (f32[2048]{0:T(1024)S(1)}, f32[2048]{0:T(1024)S(1)}, f32[2048,512]{0,1:T(8,128)}, f32[2048,512]{0,1:T(8,128)}) fusion(f32[512]{0:T(512)S(1)} %bitcast.435, f32[2048,1288]{0,1:T(8,128)} %copy-done.10, f32[2048,512]{0,1:T(8,128)} %bitcast.393, f32[2048,768]{0,1:T(8,128)} %convert_element_type.67, f32[512]{0:T(512)S(1)} %mul.749, ...), kind=kOutput, calls=%fused_computation.200 | convolution fusion | flops 8602513408 | bytes 41963520 | tf_op jit(solution)/shard_map/dot_general | solution.py:150
  807.1 15.0 convolution_convert_fusion.2
  826.7 286.7 %while.41 = (s32[]{:T(128)}, f32[8]{0:T(128)S(1)}, f32[8,64,128]{2,1,0:T(8,128)S(1)}, f32[8,256,8,64]{1,0,3,2:T(8,128)}, f32[8,256,8]{1,2,0:T(8,128)S(1)}, /*ind...) while((s32[]{:T(128)}, f32[8]{0:T(128)S(1)}, ...), condition=%wide.region_22.23_spmd.clone, body=%wide.region_8.22_spmd.clone.sunk | while | flops 2126870528 | bytes 19074456 | solution.py:66
  850.8 12.8 dynamic_update_slice.71
  886.5 12.8 dynamic_update_slice.71
  922.1 12.8 dynamic_update_slice.71
  957.9 12.8 dynamic_update_slice.71
  1124.6 17.4 %collective-permute-done.1 = f32[2048,128]{0,1:T(8,128)S(1)} collective-permute-done((f32[2048,128]{0,1:T(8,128)S(1)}, f32[2048,128]{0,1:T(8,128)S(1)}, u32[]{:S(2)}, u32[]{:S(2)}) %collective-permute-start.1) | collective-permute-done | bytes 1048608 | tf_op jit(solution)/shard_map/ppermute | solution.py:114
  1142.4 16.0 multiply_reduce_fusion.8
  1167.9 26.7 %convolution_convert_fusion.1 = bf16[2048,4096]{1,0:T(8,128)(2,1)} fusion(bf16[4096,8]{0,1:T(8,128)(2,1)S(1)} %slice-done.3, bf16[4096,128]{0,1:T(8,128)(2,1)S(1)} %copy-done.14, bf16[4096,1024]{0,1:T(8,128)(2,1)} %slice.297, bf16[2048,8]{0,1:T(8,128)(2,1)S(1)} %get-tuple-element.705, bf16[2048,640]{0,1:T(8,128)(2,1)S(1)} %fusion.116, ...), kind=kOutput, calls=%fused_computation.135 | convolution fusion | flops 19512721408 | bytes 31031296 | tf_op jit(solution)/shard_map/dot_general | solution.py:16
  1194.6 16.0 convolution_convert_fusion.3
  1216.7 26.1 %convolution_convert_fusion = bf16[4096,1160]{0,1:T(8,128)(2,1)} fusion(bf16[2048,4096]{1,0:T(8,128)(2,1)} %bitcast.443, bf16[2048,8]{0,1:T(8,128)(2,1)S(1)} %get-tuple-element.705, bf16[2048,640]{0,1:T(8,128)(2,1)S(1)} %fusion.116, bf16[2048,512]{0,1:T(8,128)(2,1)} %get-tuple-element.715), kind=kOutput, calls=%fused_computation.134 | convolution fusion | flops 19480576000 | bytes 31031296 | tf_op jit(solution)/shard_map/dot_general | solution.py:20
  1279.7 94.9 %all-to-all-done.2 = bf16[2,2048,1160]{1,2,0:T(8,128)(2,1)} async-done(((bf16[2,2048,1160]{1,2,0:T(8,128)(2,1)}), bf16[2,2048,1160]{1,2,0:T(8,128)(2,1)}, u32[]{:S(2)}, u32[]{:S(2)}) %all-to-all-start.2) | async-done | bytes 9502752 | tf_op jit(solution)/shard_map/all_to_all | solution.py:86
  1394.3 30.1 %all-to-all-done.5 = bf16[4,512,512]{2,1,0:T(8,128)(2,1)S(1)} async-done(((bf16[4,512,512]{2,1,0:T(8,128)(2,1)}), bf16[4,512,512]{2,1,0:T(8,128)(2,1)S(1)}, u32[]{:S(2)}, u32[]{:S(2)}) %all-to-all-start.5) | async-done | bytes 2097184 | tf_op jit(solution)/shard_map/all_to_all | solution.py:87
  1445.2 88.9 %all-to-all-done.3 = bf16[4,512,1160]{1,2,0:T(8,128)(2,1)} async-done(((bf16[4,512,1160]{1,2,0:T(8,128)(2,1)}), bf16[4,512,1160]{1,2,0:T(8,128)(2,1)}, u32[]{:S(2)}, u32[]{:S(2)}) %all-to-all-start.3) | async-done | bytes 4751392 | tf_op jit(solution)/shard_map/all_to_all | solution.py:87
  1550.6 13.3 copy.180
  1581.8 57.9 %all-reduce.20.cloned.1.call-done = (f32[4096]{0:T(1024)}, f32[4,3736]{1,0:T(4,128)}) async-done(((f32[4096]{0:T(1024)}, f32[4,3736]{1,0:T(4,128)}), (f32[4096]{0:T(1024)}, f32[4,3736]{1,0:T(4,128)})) %all-reduce.20.cloned.1.call-update) | async-done | bytes 76176 | tf_op jit(solution)/shard_map/psum | solution.py:206
  (695 shorter events, 666.2 us)
Async XLA Ops:
  7.2 278.6 %all-gather.22.cloned.1.call-start = ((), (), s32[]{:S(2)}) async-start(), calls=%async_computation.15 | async-start | bytes 5242880 | tf_op jit(solution)/shard_map/all_gather | solution.py:74
  40.7 239.3 %all-to-all-start = ((bf16[4,512,1288]{1,2,0:T(8,128)(2,1)}), bf16[4,512,1288]{1,2,0:T(8,128)(2,1)}, u32[]{:S(2)}, u32[]{:S(2)}) async-start(bf16[4,512,1288]{1,2,0:T(8,128)(2,1)} %bitcast.396), calls=%async_computation | async-start | bytes 10551296 | tf_op jit(solution)/shard_map/all_to_all | solution.py:79
  46.8 297.8 %all-gather.14.cloned.1.call-start = ((), (), s32[]{:S(2)}) async-start(), calls=%async_computation.9 | async-start | bytes 5242880 | tf_op jit(solution)/shard_map/all_gather | solution.py:74
  49.1 368.0 %all-gather.12.cloned.1.call-start = ((), (), s32[]{:S(2)}) async-start(), calls=%async_computation.8 | async-start | bytes 15826944 | tf_op jit(solution)/shard_map/all_gather | solution.py:80
  285.7 238.7 %all-gather.24.cloned.1.call-start = ((), (), s32[]{:S(2)}) async-start(), calls=%async_computation.16 | async-start | bytes 20971520 | tf_op jit(solution)/shard_map/all_gather | solution.py:75
  286.3 474.2 %all-gather.16.cloned.1.call-start = ((), (), s32[]{:S(2)}) async-start(), calls=%async_computation.10 | async-start | bytes 6291456 | tf_op jit(solution)/shard_map/all_gather | solution.py:80
  344.5 416.0 %all-gather.26.cloned.1.call-start = ((), (), s32[]{:S(2)}) async-start(), calls=%async_computation.17 | async-start | bytes 20971520 | tf_op jit(solution)/shard_map/all_gather | solution.py:75
  345.1 926.5 %reduce-scatter.3.cloned.1.call-start = ((), (), s32[]{:S(2)}) async-start(), calls=%async_computation.11 | async-start | bytes 17825792 | tf_op jit(solution)/shard_map/reduce_scatter | solution.py:92
  345.5 205.9 %copy-start.36 = (f32[1,3,8]{2,0,1:T(1,128)}, f32[1,3,8]{2,0,1:T(1,128)S(1)}, u32[]{:S(2)}) copy-start(f32[1,3,8]{2,0,1:T(1,128)S(1)} %fusion.147) | copy-start | bytes 292
  753.6 26.0 %copy-start.8 = (f32[8,256,128]{2,1,0:T(8,128)}, f32[8,256,128]{2,1,0:T(8,128)S(1)}, u32[]{:S(2)}) copy-start(f32[8,256,128]{2,1,0:T(8,128)S(1)} %get-tuple-element.1069) | copy-start | bytes 3145732
  753.6 26.0 %copy-start.9 = (f32[8,256,128]{2,1,0:T(8,128)}, f32[8,256,128]{2,1,0:T(8,128)S(1)}, u32[]{:S(2)}) copy-start(f32[8,256,128]{2,1,0:T(8,128)S(1)} %get-tuple-element.1070) | copy-start | bytes 3145732
  779.7 12.0 collective-permute-start
  822.1 607.4 %reduce-scatter.5.cloned.1.call-start = ((), (), s32[]{:S(2)}) async-start(), calls=%async_computation.13 | async-start | bytes 17825792 | tf_op jit(solution)/shard_map/reduce_scatter | solution.py:92
  1116.8 25.2 %collective-permute-start.1 = (f32[2048,128]{0,1:T(8,128)S(1)}, f32[2048,128]{0,1:T(8,128)S(1)}, u32[]{:S(2)}, u32[]{:S(2)}) collective-permute-start(f32[2048,128]{0,1:T(8,128)S(1)} %fusion.123), channel_id=1, source_target_pairs={{0,4},{4,0},{8,12},{12,8},{1,5},{5,1},{9,13},{13,9},{2,6},{6,2},{1... | collective-permute-start | bytes 3145736 | tf_op jit(solution)/shard_map/ppermute | solution.py:114
  1123.9 18.4 %slice-start = ((f32[2051,768]{0,1:T(8,128)}), f32[2051,512]{0,1:T(8,128)S(1)}, s32[]{:S(2)}) async-start(f32[2051,768]{0,1:T(8,128)} %copy-done), calls=%async_computation.19 | async-start | bytes 8912896 | tf_op jit(solution)/shard_map/slice | solution.py:172
  1123.9 18.4 %copy-start.20 = (f32[640]{0:T(1024)S(1)}, f32[640]{0:T(1024)}, u32[]{:S(2)}) copy-start(f32[640]{0:T(1024)} %get-tuple-element.643) | copy-start | bytes 7684
  1123.9 18.4 %copy-start.21 = (f32[640]{0:T(1024)S(1)}, f32[640]{0:T(1024)}, u32[]{:S(2)}) copy-start(f32[640]{0:T(1024)} %get-tuple-element.644) | copy-start | bytes 7684
  1210.6 53.3 %all-to-all-start.4 = ((bf16[2,2048,512]{2,1,0:T(8,128)(2,1)}), bf16[2,2048,512]{2,1,0:T(8,128)(2,1)}, u32[]{:S(2)}, u32[]{:S(2)}) async-start(bf16[2,2048,512]{2,1,0:T(8,128)(2,1)} %bitcast.407), calls=%async_computation.6 | async-start | bytes 8388608 | tf_op jit(solution)/shard_map/all_to_all | solution.py:86
  1263.9 110.8 %all-to-all-start.2 = ((bf16[2,2048,1160]{1,2,0:T(8,128)(2,1)}), bf16[2,2048,1160]{1,2,0:T(8,128)(2,1)}, u32[]{:S(2)}, u32[]{:S(2)}) async-start(bf16[2,2048,1160]{1,2,0:T(8,128)(2,1)} %bitcast.377), calls=%async_computation.4 | async-start | bytes 19005440 | tf_op jit(solution)/shard_map/all_to_all | solution.py:86
  1271.5 293.9 %all-gather.18.cloned.1.call-start = ((), (), s32[]{:S(2)}) async-start(), calls=%async_computation.12 | async-start | bytes 5242880 | tf_op jit(solution)/shard_map/all_gather | solution.py:159
  1374.6 49.7 %all-to-all-start.5 = ((bf16[4,512,512]{2,1,0:T(8,128)(2,1)}), bf16[4,512,512]{2,1,0:T(8,128)(2,1)S(1)}, u32[]{:S(2)}, u32[]{:S(2)}) async-start(bf16[4,512,512]{2,1,0:T(8,128)(2,1)} %bitcast.400), calls=%async_computation.7 | async-start | bytes 4194304 | tf_op jit(solution)/shard_map/all_to_all | solution.py:87
  1424.4 109.7 %all-to-all-start.3 = ((bf16[4,512,1160]{1,2,0:T(8,128)(2,1)}), bf16[4,512,1160]{1,2,0:T(8,128)(2,1)}, u32[]{:S(2)}, u32[]{:S(2)}) async-start(bf16[4,512,1160]{1,2,0:T(8,128)(2,1)} %bitcast.381), calls=%async_computation.5 | async-start | bytes 9502720 | tf_op jit(solution)/shard_map/all_to_all | solution.py:87
  1429.4 136.0 %all-gather.20.cloned.1.call-start = ((), (), s32[]{:S(2)}) async-start(), calls=%async_computation.14 | async-start | bytes 5242880 | tf_op jit(solution)/shard_map/all_gather | solution.py:187
  1430.0 209.7 %all-reduce.20.cloned.1.call-start = ((), (), s32[]{:S(2)}) async-start(), calls=%async_computation.18 | async-start | bytes 155648 | tf_op jit(solution)/shard_map/psum | solution.py:206
  (36 other events, 253.0 us)
Sparse Core Ops, SparseCore 0:
  22.7 139.2 all-gather.21
  164.1 122.1 all-gather.13
  288.4 128.6 all-gather.11
  418.5 105.9 all-gather.23
  525.9 56.7 all-gather.15
  584.1 105.9 all-gather.25
  822.2 177.6 reduce-scatter.2
  1194.7 177.7 reduce-scatter.4
  1374.1 33.4 all-gather.17
  1431.5 34.0 all-gather.19
  1573.6 66.1 all-reduce.19

commit v2 on v1

--- a/solution.py
+++ b/solution.py
@@ -1,15 +1,359 @@
+import functools
+
 import jax
 import jax.numpy as jnp
 from jax import lax
+from jax.experimental import pallas as pl
+from jax.experimental.pallas import tpu as pltpu
 from jax.sharding import PartitionSpec as P
 
 P_SIZE = 64
 N = 128
-STRETCH = 256
+BLOCK = 256
+EDGE = 8
 EPS = 1e-05
 HIGH = lax.Precision.HIGHEST
 F32 = jnp.float32
 BF16 = jnp.bfloat16
+
+
+def dot_on(left_side, right_side, left_dim, right_dim, precision=None):
+    return lax.dot_general(
+        left_side, right_side, (((left_dim,), (right_dim,)), ((), ())), precision=precision, preferred_element_type=F32
+    )
+
+
+def split(v):
+    high = v.astype(BF16)
+    return high, (v - high.astype(F32)).astype(BF16)
+
+
+def dot_two(parts, other, part_dim, other_dim):
+    return dot_on(parts[0], other, part_dim, other_dim) + dot_on(parts[1], other, part_dim, other_dim)
+
+
+def dot_three(left_side, right_side, left_dim, right_dim):
+    high = dot_two(left_side, right_side[0], left_dim, right_dim)
+    return high + dot_on(left_side[0], right_side[1], left_dim, right_dim)
+
+
+def softplus(v):
+    return jnp.maximum(v, 0.0) + jnp.log1p(jnp.exp(-jnp.abs(v)))
+
+
+def sigmoid(v):
+    return 1.0 / (1.0 + jnp.exp(-v))
+
+
+def order_mask(transposed):
+    row = lax.broadcasted_iota(jnp.int32, (BLOCK, BLOCK), 0)
+    col = lax.broadcasted_iota(jnp.int32, (BLOCK, BLOCK), 1)
+    return row <= col if transposed else row >= col
+
+
+def first_half(rows):
+    return lax.broadcasted_iota(jnp.int32, (rows, 2 * P_SIZE), 1) < P_SIZE
+
+
+def over_pair(value, pair):
+    shape = (value.shape[0], P_SIZE * 2)
+    left = jnp.broadcast_to(value[:, 2 * pair : 2 * pair + 1], shape)
+    right = jnp.broadcast_to(value[:, 2 * pair + 1 : 2 * pair + 2], shape)
+    return jnp.where(first_half(shape[0]), left, right)
+
+
+def over_heads(value):
+    return jnp.concatenate([over_pair(value, pair) for pair in range(value.shape[1] // 2)], axis=1)
+
+
+def head_sums(value):
+    columns = []
+    for pair in range(value.shape[1] // (2 * P_SIZE)):
+        part = value[:, pair * 2 * P_SIZE : (pair + 1) * 2 * P_SIZE]
+        left = jnp.where(first_half(part.shape[0]), part, 0.0)
+        columns += [jnp.sum(left, axis=1, keepdims=True), jnp.sum(part - left, axis=1, keepdims=True)]
+    heads = len(columns)
+    lane = lax.broadcasted_iota(jnp.int32, (value.shape[0], heads), 1)
+    total = jnp.broadcast_to(columns[0], lane.shape)
+    for head in range(1, heads):
+        total = jnp.where(lane == head, columns[head], total)
+    return total
+
+
+def convolve(buffer, kernel_ref, start, width):
+    taps = kernel_ref.shape[0] - 1
+    total = kernel_ref[taps : taps + 1, start : start + width]
+    for tap in range(taps):
+        low = EDGE - taps + 1 + tap
+        total = total + kernel_ref[tap : tap + 1, start : start + width] * buffer[low : low + BLOCK, start : start + width]
+    return total
+
+
+def block_steps(raw_ref, head_ref):
+    dt = softplus(raw_ref[...] + head_ref[0:1, :])
+    decay = -jnp.exp(head_ref[1:2, :])
+    log_step = dt * decay
+    lower = order_mask(False).astype(F32)
+    total = dot_on(lower, log_step, 1, 0, HIGH)
+    total_t = dot_on(log_step, lower, 0, 1, HIGH)
+    return dt, decay, total, total_t
+
+
+def forward_body(conv_ref, raw_ref, gate_ref, up_ref, kernel_ref, head_ref, gain_ref, low_ref, ssd_ref, state_ref, sums_ref, state, buffer):
+    width = gate_ref.shape[1]
+    first = pl.program_id(0) == 0
+
+    @pl.when(first)
+    def _():
+        state[...] = jnp.zeros_like(state)
+        buffer[0:EDGE, :] = jnp.zeros((EDGE, buffer.shape[1]), F32)
+
+    @pl.when(jnp.logical_not(first))
+    def _():
+        buffer[0:EDGE, :] = buffer[BLOCK : BLOCK + EDGE, :]
+
+    buffer[EDGE : EDGE + BLOCK, :] = conv_ref[...].astype(F32)
+    before = convolve(buffer, kernel_ref, 0, buffer.shape[1])
+    low_ref[...] = (before * sigmoid(before)).astype(BF16)
+    dt, _, total, total_t = block_steps(raw_ref, head_ref)
+    state_ref[0] = state[...]
+    inject = low_ref[:, width : width + N]
+    readout = low_ref[:, width + N : width + 2 * N]
+    scores = dot_on(readout, inject, 1, 1)
+    mask = order_mask(False)
+    half = first_half(BLOCK)
+    skip = over_heads(head_ref[2:3, :])
+    squares = []
+    for pair in range(width // (2 * P_SIZE)):
+        cols = slice(pair * 2 * P_SIZE, (pair + 1) * 2 * P_SIZE)
+        x = low_ref[:, cols].astype(F32)
+        total_p = over_pair(total, pair)
+        scaled = x * over_pair(dt, pair)
+        scaled_two = split(scaled)
+        local = []
+        for head in (2 * pair, 2 * pair + 1):
+            gap = total[:, head : head + 1] - total_t[head : head + 1, :]
+            mixing = jnp.exp(jnp.where(mask, gap, -1e30)) * scores
+            local.append(dot_three(split(mixing), scaled_two, 1, 0))
+        held = state[:, cols]
+        held_two = split(held)
+        carried = jnp.exp(total_p) * (dot_on(readout, held_two[0], 1, 0) + dot_on(readout, held_two[1], 1, 0))
+        ssd = jnp.where(half, local[0], local[1]) + carried + skip[:, cols] * x
+        ssd_ref[:, cols] = ssd
+        moved = split(scaled * jnp.exp(total_p[BLOCK - 1 : BLOCK, :] - total_p))
+        state[:, cols] = held * jnp.exp(total_p[BLOCK - 1 : BLOCK, :]) + (
+            dot_on(inject, moved[0], 0, 0) + dot_on(inject, moved[1], 0, 0)
+        )
+        gate_pre = gate_ref[:, cols]
+        gated = ssd * (gate_pre * sigmoid(gate_pre))
+        squares.append((gated * gated, gated * (up_ref[:, cols] * gain_ref[0:1, cols])))
+    ones = jnp.ones((8, 2 * P_SIZE), F32)
+    square = functools.reduce(jnp.add, [s[0] for s in squares])
+    cross = functools.reduce(jnp.add, [s[1] for s in squares])
+    sums_ref[0:1, :] = dot_on(ones, square, 1, 1, HIGH)[0:1, :]
+    sums_ref[1:2, :] = dot_on(ones, cross, 1, 1, HIGH)[0:1, :]
+
+
+def mixer_forward(conv_input, raw_dt, gate_pre, grad_gated, kernel, heads, gain):
+    length, width = gate_pre.shape
+    wide = conv_input.shape[1]
+    count = length // BLOCK
+    rows = lambda i: (i, 0)
+    whole = lambda i: (0, 0)
+    return pl.pallas_call(
+        forward_body,
+        grid=(count,),
+        in_specs=[
+            pl.BlockSpec((BLOCK, wide), rows),
+            pl.BlockSpec((BLOCK, raw_dt.shape[1]), rows),
+            pl.BlockSpec((BLOCK, width), rows),
+            pl.BlockSpec((BLOCK, width), rows),
+            pl.BlockSpec(kernel.shape, whole),
+            pl.BlockSpec(heads.shape, whole),
+            pl.BlockSpec(gain.shape, whole),
+        ],
+        out_specs=[
+            pl.BlockSpec((BLOCK, wide), rows),
+            pl.BlockSpec((BLOCK, width), rows),
+            pl.BlockSpec((1, N, width), lambda i: (i, 0, 0)),
+            pl.BlockSpec((2, BLOCK), lambda i: (0, i)),
+        ],
+        out_shape=[
+            jax.ShapeDtypeStruct((length, wide), BF16),
+            jax.ShapeDtypeStruct((length, width), F32),
+            jax.ShapeDtypeStruct((count, N, width), F32),
+            jax.ShapeDtypeStruct((2, length), F32),
+        ],
+        scratch_shapes=[pltpu.VMEM((N, width), F32), pltpu.VMEM((BLOCK + EDGE, wide), F32)],
+        compiler_params=pltpu.CompilerParams(vmem_limit_bytes=48 << 20),
+        name="mixer_forward",
+    )(conv_input, raw_dt, gate_pre, grad_gated, kernel, heads, gain)
+
+
+def backward_body(
+    conv_ref, edge_ref, low_ref, raw_ref, gate_ref, up_ref, ssd_ref, state_ref, norm_ref, kernel_ref, head_ref, gain_ref,
+    grad_gate_ref, grad_in_ref, grad_maps_ref, grad_dt_ref, grad_kernel_ref, grad_head_ref, grad_gain_ref,
+    adjoint, buffer, grads, next_state,
+):
+    width = gate_ref.shape[1]
+    taps = kernel_ref.shape[0] - 1
+    count = pl.num_programs(0)
+    step = pl.program_id(0)
+
+    @pl.when(step == 0)
+    def _():
+        adjoint[...] = jnp.zeros_like(adjoint)
+        next_state[...] = jnp.zeros_like(next_state)
+        grads[BLOCK : BLOCK + EDGE, :] = jnp.zeros((EDGE, width), F32)
+        grad_kernel_ref[...] = jnp.zeros_like(grad_kernel_ref)
+        grad_head_ref[...] = jnp.zeros_like(grad_head_ref)
+        grad_gain_ref[...] = jnp.zeros_like(grad_gain_ref)
+
+    @pl.when(step > 0)
+    def _():
+        grads[BLOCK : BLOCK + EDGE, :] = grads[0:EDGE, :]
+
+    edge = edge_ref[edge_ref.shape[0] - EDGE :, 0:width].astype(F32)
+    buffer[0:EDGE, :] = jnp.where(step == count - 1, 0.0, edge)
+    buffer[EDGE : EDGE + BLOCK, :] = conv_ref[:, 0:width].astype(F32)
+    dt, decay, total, total_t = block_steps(raw_ref, head_ref)
+    inject = low_ref[:, width : width + N]
+    readout = low_ref[:, width + N : width + 2 * N]
+    scores_t = dot_on(inject, readout, 1, 1)
+    mask_t = order_mask(True)
+    half = first_half(BLOCK)
+    skip = over_heads(head_ref[2:3, :])
+    inverse = norm_ref[:, 0:1]
+    pull = norm_ref[:, 1:2]
+    grad_scores_t = jnp.zeros((BLOCK, BLOCK), F32)
+    grad_inject = jnp.zeros((BLOCK, N), F32)
+    grad_readout = jnp.zeros((BLOCK, N), F32)
+    decay_parts, step_parts, skip_parts, end_parts = [], [], [], []
+    for pair in range(width // (2 * P_SIZE)):
+        cols = slice(pair * 2 * P_SIZE, (pair + 1) * 2 * P_SIZE)
+        x = low_ref[:, cols].astype(F32)
+        gate_pre = gate_ref[:, cols]
+        ssd = ssd_ref[:, cols]
+        sig = sigmoid(gate_pre)
+        gate = gate_pre * sig
+        up = up_ref[:, cols]
+        gated = ssd * gate
+        grad_gain_ref[0:1, cols] += jnp.sum(up * gated * inverse, axis=0, keepdims=True)
+        grad_pre = inverse * (up * gain_ref[0:1, cols]) - gated * pull
+        grad_gate_ref[:, cols] = (grad_pre * ssd * (sig * (1.0 + gate_pre * (1.0 - sig)))).astype(BF16)
+        grad_ssd = grad_pre * gate
+        grad_two = split(grad_ssd)
+        total_p = over_pair(total, pair)
+        dt_p = over_pair(dt, pair)
+        to_end = jnp.exp(total_p[BLOCK - 1 : BLOCK, :] - total_p)
+        scaled = x * dt_p
+        scaled_two = split(scaled)
+        local = []
+        for index, head in enumerate((2 * pair, 2 * pair + 1)):
+            gap = total_t[head : head + 1, :] - total[:, head : head + 1]
+            decays = jnp.exp(jnp.where(mask_t, gap, -1e30))
+            own = half if index == 0 else jnp.logical_not(half)
+            mine = [jnp.where(own, part, jnp.zeros_like(part)) for part in grad_two]
+            grad_scores_t += decays * dot_three(scaled_two, mine, 1, 1)
+            local.append(dot_three(split(decays * scores_t), grad_two, 1, 0))
+        local = jnp.where(half, local[0], local[1])
+        lam = adjoint[:, cols]
+        lam_two = split(lam)
+        held = state_ref[0, :, cols]
+        far = dot_on(inject, lam_two[0], 1, 0) + dot_on(inject, lam_two[1], 1, 0)
+        moved = scaled * to_end
+        grad_inject += dot_three(split(moved), lam_two, 1, 1)
+        rising = split(grad_ssd * jnp.exp(total_p))
+        grad_readout += dot_three(rising, split(held), 1, 1)
+        end_parts.append(jnp.sum(lam * next_state[:, cols], axis=0, keepdims=True))
+        adjoint[:, cols] = lam * jnp.exp(total_p[BLOCK - 1 : BLOCK, :]) + (
+            dot_on(readout, rising[0], 0, 0) + dot_on(readout, rising[1], 0, 0)
+        )
+        next_state[:, cols] = held
+        pure = ssd - skip[:, cols] * x
+        decay_parts.append(grad_ssd * pure - scaled * local - moved * far)
+        grad_scaled = local + to_end * far
+        step_parts.append(x * grad_scaled)
+        skip_parts.append(jnp.sum(grad_ssd * x, axis=0, keepdims=True))
+        grad_x = dt_p * grad_scaled + skip[:, cols] * grad_ssd
+        before = convolve(buffer, kernel_ref, pair * 2 * P_SIZE, 2 * P_SIZE)
+        sig = sigmoid(before)
+        grads[0:BLOCK, cols] = grad_x * (sig * (1.0 + before * (1.0 - sig)))
+    row_grads = head_sums(jnp.concatenate(decay_parts, axis=1))
+    upper = order_mask(True).astype(F32)
+    ends = head_sums(jnp.concatenate(end_parts, axis=1))
+    grad_log = dot_on(upper, row_grads, 1, 0, HIGH) + ends
+    grad_dt = head_sums(jnp.concatenate(step_parts, axis=1)) + decay * grad_log
+    grad_raw = grad_dt * sigmoid(raw_ref[...] + head_ref[0:1, :])
+    grad_dt_ref[...] = grad_raw
+    grad_head_ref[0:1, :] += jnp.sum(grad_raw, axis=0, keepdims=True)
+    grad_head_ref[1:2, :] += decay * jnp.sum(dt * grad_log, axis=0, keepdims=True)
+    grad_head_ref[2:3, :] += head_sums(jnp.concatenate(skip_parts, axis=1))
+    scores_two = split(grad_scores_t)
+    grad_maps_ref[:, 0:N] = grad_inject + dot_two(scores_two, readout, 1, 0)
+    grad_maps_ref[:, N : 2 * N] = grad_readout + dot_two(scores_two, inject, 0, 0)
+    here = grads[0:BLOCK, :]
+    grad_kernel_ref[taps : taps + 1, :] += jnp.sum(here, axis=0, keepdims=True)
+    total_in = jnp.zeros((BLOCK, width), F32)
+    for tap in range(taps):
+        low = EDGE - taps + 1 + tap
+        grad_kernel_ref[tap : tap + 1, :] += jnp.sum(here * buffer[low : low + BLOCK, :], axis=0, keepdims=True)
+        ahead = taps - 1 - tap
+        total_in = total_in + kernel_ref[tap : tap + 1, 0:width] * grads[ahead : ahead + BLOCK, :]
+    grad_in_ref[...] = total_in.astype(BF16)
+
+
+def mixer_backward(conv_input, low, raw_dt, gate_pre, grad_gated, ssd, states, norms, kernel, heads, gain):
+    length, width = gate_pre.shape
+    wide = conv_input.shape[1]
+    count = length // BLOCK
+    edge = 16
+    back = lambda i: (count - 1 - i, 0)
+    whole = lambda i: (0, 0)
+    return pl.pallas_call(
+        backward_body,
+        grid=(count,),
+        in_specs=[
+            pl.BlockSpec((BLOCK, wide), back),
+            pl.BlockSpec((edge, wide), lambda i: (jnp.maximum((count - 1 - i) * (BLOCK // edge) - 1, 0), 0)),
+            pl.BlockSpec((BLOCK, wide), back),
+            pl.BlockSpec((BLOCK, raw_dt.shape[1]), back),
+            pl.BlockSpec((BLOCK, width), back),
+            pl.BlockSpec((BLOCK, width), back),
+            pl.BlockSpec((BLOCK, width), back),
+            pl.BlockSpec((1, N, width), lambda i: (count - 1 - i, 0, 0)),
+            pl.BlockSpec((BLOCK, norms.shape[1]), back),
+            pl.BlockSpec(kernel.shape, whole),
+            pl.BlockSpec(heads.shape, whole),
+            pl.BlockSpec(gain.shape, whole),
+        ],
+        out_specs=[
+            pl.BlockSpec((BLOCK, width), back),
+            pl.BlockSpec((BLOCK, width), back),
+            pl.BlockSpec((BLOCK, 2 * N), back),
+            pl.BlockSpec((BLOCK, raw_dt.shape[1]), back),
+            pl.BlockSpec((kernel.shape[0], width), whole),
+            pl.BlockSpec(heads.shape, whole),
+            pl.BlockSpec(gain.shape, whole),
+        ],
+        out_shape=[
+            jax.ShapeDtypeStruct((length, width), BF16),
+            jax.ShapeDtypeStruct((length, width), BF16),
+            jax.ShapeDtypeStruct((length, 2 * N), F32),
+            jax.ShapeDtypeStruct(raw_dt.shape, F32),
+            jax.ShapeDtypeStruct((kernel.shape[0], width), F32),
+            jax.ShapeDtypeStruct(heads.shape, F32),
+            jax.ShapeDtypeStruct(gain.shape, F32),
+        ],
+        scratch_shapes=[
+            pltpu.VMEM((N, width), F32),
+            pltpu.VMEM((BLOCK + EDGE, width), F32),
+            pltpu.VMEM((BLOCK + EDGE, width), F32),
+            pltpu.VMEM((N, width), F32),
+        ],
+        compiler_params=pltpu.CompilerParams(vmem_limit_bytes=56 << 20),
+        name="mixer_backward",
+    )(conv_input, conv_input, low, raw_dt, gate_pre, grad_gated, ssd, states, norms, kernel, heads, gain)
 
 
 def dot_last(left_side, right_side):
@@ -27,45 +371,6 @@
     for offset in range(1, tap_count):
         running = running + kernel[offset] * padded[offset : offset + length]
     return jax.nn.silu(running)
-
-
-def block_step(memory, pieces, log_decay):
-    x_heads, step_sizes, inject, readout = pieces
-    block_len = x_heads.shape[0]
-    cumulative = jnp.cumsum(step_sizes * log_decay, axis=0)
-    gap_matrix = cumulative[:, None, :] - cumulative[None, :, :]
-    causal = jnp.tril(jnp.ones((block_len, block_len), F32))
-    decays = jnp.exp(jnp.minimum(gap_matrix, 0.0)) * causal[:, :, None]
-    scores = jnp.einsum("in,jn->ij", readout, inject, precision=HIGH)
-    mixing = decays * scores[:, :, None]
-    scaled = x_heads * step_sizes[:, :, None]
-    local_out = jnp.einsum("ijh,jhp->ihp", mixing, scaled, precision=HIGH)
-    carried = jnp.einsum("in,hpn->ihp", readout, memory, precision=HIGH)
-    carried = carried * jnp.exp(cumulative)[:, :, None]
-    to_end = jnp.exp(cumulative[-1] - cumulative)
-    new_memory = memory * jnp.exp(cumulative[-1])[:, None, None]
-    new_memory = new_memory + jnp.einsum("jn,jhp->hpn", inject, scaled * to_end[:, :, None], precision=HIGH)
-    return (new_memory, local_out + carried)
-
-
-def mixer(x_flat, maps, raw_dt, head_params):
-    length, width = x_flat.shape
-    heads = head_params.shape[1]
-    count = length // STRETCH
-    step_sizes = jax.nn.softplus(raw_dt + head_params[0])
-    log_decay = -jnp.exp(head_params[1])
-    x_heads = x_flat.reshape(length, heads, P_SIZE)
-    pieces = (
-        x_heads.reshape(count, STRETCH, heads, P_SIZE),
-        step_sizes.reshape(count, STRETCH, heads),
-        maps[:, :N].reshape(count, STRETCH, N),
-        maps[:, N:].reshape(count, STRETCH, N),
-    )
-    zero_memory = jnp.zeros((heads, P_SIZE, N), F32)
-    advance = jax.checkpoint(lambda memory, piece_set: block_step(memory, piece_set, log_decay))
-    _, outputs = lax.scan(advance, zero_memory, pieces)
-    outputs = outputs.reshape(length, heads, P_SIZE) + head_params[2][:, None] * x_heads
-    return outputs.reshape(length, width)
 
 
 def spread_rows(value):
@@ -128,53 +433,43 @@
     normed_all = spread_rows(normed)
     cot_all = spread_rows(cot)
 
-    proj = jnp.dot(normed_all, weight_in, preferred_element_type=F32)
-    gate_pre = proj[:, :width]
     conv_width = width + 2 * N
-    conv_input = proj[:, width : width + conv_width].astype(BF16)
-    raw_dt = proj[:, width + conv_width :]
-    padded = jnp.concatenate([jnp.zeros((taps - 1, conv_width), BF16), conv_input], axis=0).astype(F32)
+    grad_gated = jnp.dot(cot_all, weight_out, preferred_element_type=F32)
+    gate_pre = jnp.dot(normed_all, weight_in[:, :width], preferred_element_type=F32)
+    conv_input = jnp.dot(normed_all, weight_in[:, width : width + conv_width], preferred_element_type=F32).astype(BF16)
+    raw_dt = jnp.dot(normed_all, weight_in[:, width + conv_width :], preferred_element_type=F32)
     kernel_x = mine(conv_x.reshape(taps + 1, nctx, width).transpose(1, 0, 2))
     kernel_bc = conv_bc.reshape(taps + 1, 2, groups, N)
     kernel_bc = lax.dynamic_index_in_dim(kernel_bc, ctx // share, 2, False)
     kernel = jnp.concatenate([kernel_x, kernel_bc.reshape(taps + 1, 2 * N)], axis=1)
-    conv_out = conv_silu(padded, kernel)
-    conv_low = lax.optimization_barrier(conv_out.astype(BF16)).astype(F32)
     heads_mine = mine(head_params.reshape(3, nctx, heads).transpose(1, 0, 2))
-    gain = mine(gate_gain.reshape(nctx, width))
-    ssd, mixer_back = jax.vjp(mixer, conv_low[:, :width], conv_low[:, width:], raw_dt, heads_mine)
-
-    sig = jax.nn.sigmoid(gate_pre)
-    gate = gate_pre * sig
-    gated = ssd * gate
-    grad_gated = jnp.dot(cot_all, weight_out, preferred_element_type=F32)
-    grad_scaled = grad_gated * gain
-    sums = jnp.stack([jnp.sum(gated * gated, axis=1), jnp.sum(grad_scaled * gated, axis=1)])
+    gain = mine(gate_gain.reshape(nctx, 1, width))
+    low, ssd, states, sums = mixer_forward(conv_input, raw_dt, gate_pre, grad_gated, kernel, heads_mine, gain)
     sums = (sums + partner(sums)) / group_width
-    inverse = lax.rsqrt(sums[0] + EPS)[:, None]
-    gated_norm = (gated * inverse * gain).astype(BF16)
+    inverse = lax.rsqrt(sums[0] + EPS)
+    norms = jnp.stack([inverse, inverse * inverse * inverse * sums[1]], axis=1)
+    gated_norm = (ssd * (gate_pre * jax.nn.sigmoid(gate_pre)) * norms[:, 0:1] * gain).astype(BF16)
     branch = sum_rows(dot_last(gated_norm, weight_out))
     part = length // ntp
     hidden_part = lax.dynamic_slice_in_dim(hidden, lax.axis_index("tp") * part, part, 0)
     mixed = lax.all_gather((hidden_part + branch).astype(BF16), "tp", axis=0, tiled=True)
     grad_out = return_grad(dot_first(cot_all, gated_norm), rows)
-
-    gate_gain_grad = jnp.sum(grad_gated * gated * inverse, axis=0)
-    grad_pre = inverse * grad_scaled - gated * (inverse * inverse * inverse * sums[1][:, None])
-    grad_ssd = grad_pre * gate
-    grad_gate = (grad_pre * ssd * (sig * (1.0 + gate_pre * (1.0 - sig)))).astype(BF16)
-    grad_x, grad_maps, grad_dt, grad_heads = mixer_back(grad_ssd)
+    grad_gate, grad_x, grad_maps, grad_dt, grad_kernel_x, grad_heads, gate_gain_grad = mixer_backward(
+        conv_input, low, raw_dt, gate_pre, grad_gated, ssd, states, norms, kernel, heads_mine, gain
+    )
 
     odd = ctx % 2
     own_maps = lax.dynamic_slice_in_dim(grad_maps, odd * N, N, 1)
     send_maps = lax.dynamic_slice_in_dim(grad_maps, (1 - odd) * N, N, 1)
     own_maps = own_maps + partner(send_maps)
-    own_padded = jnp.concatenate([padded[:, :width], lax.dynamic_slice_in_dim(padded, width + odd * N, N, 1)], axis=1)
-    own_kernel = jnp.concatenate([kernel[:, :width], lax.dynamic_slice_in_dim(kernel, width + odd * N, N, 1)], axis=1)
+    own_input = lax.dynamic_slice_in_dim(conv_input, width + odd * N, N, 1)
+    own_padded = jnp.concatenate([jnp.zeros((taps - 1, N), BF16), own_input], axis=0).astype(F32)
+    own_kernel = lax.dynamic_slice_in_dim(kernel, width + odd * N, N, 1)
     _, conv_back = jax.vjp(conv_silu, own_padded, own_kernel)
-    grad_padded, grad_kernel = conv_back(jnp.concatenate([grad_x, own_maps], axis=1))
-    grad_input = grad_padded[taps - 1 :].astype(BF16)
-    grad_all = jnp.concatenate([grad_gate, grad_input, grad_dt.astype(BF16)], axis=1)
+    grad_padded, grad_kernel_bc = conv_back(own_maps)
+    grad_kernel = jnp.concatenate([grad_kernel_x, grad_kernel_bc], axis=1)
+    grad_bc = grad_padded[taps - 1 :].astype(BF16)
+    grad_all = jnp.concatenate([grad_gate, grad_x, grad_bc, grad_dt.astype(BF16)], axis=1)
     own_weight = jnp.concatenate(
         [
             weight_in[:, : 2 * width],
@@ -201,7 +496,7 @@
     dt_weight_grad = grad_in[:, :, 2 * width + N :].transpose(1, 0, 2).reshape(rows, nctx * heads)
     out_weight_grad = grad_out.transpose(1, 0, 2).reshape(rows, inner)
 
-    small = jnp.concatenate([grad_kernel.reshape(-1), grad_heads.reshape(-1), gate_gain_grad])
+    small = jnp.concatenate([grad_kernel.reshape(-1), grad_heads.reshape(-1), gate_gain_grad.reshape(-1)])
     table = lax.dynamic_update_slice(jnp.zeros((nctx, small.shape[0]), F32), small[None], (ctx, 0))
     table, norm_gain_grad = lax.psum((table, norm_gain_grad), ("dp", "ctx"))
     kernel_end = (taps + 1) * (width + N)

time: 1670 us -> 1410 us (0.84)
  local copies, waits for them, and re-layouts: 412 us -> 102 us
  waiting for transfers between devices: 711 us -> 927 us
  matrix products: 274 us -> 133 us
  other arithmetic: 159 us -> 67.2 us
  Pallas kernels: 0 us -> 71.3 us
    dynamic_update_slice x32 -> x0, local copies, waits for them, and re-layouts: 213 us -> none  [mixer(): _, outputs = lax.scan(advance, zero_memory, pieces)]
    dot_general x113 -> x3, matrix products: 171 us -> 40.7 us  [the longest x1 17.5 us: shards(): jnp.dot(normed_all, weight_in[:, width:width + conv_width], preferred_ele...]
    all_gather x2, waiting for transfers between devices: 107 us -> 215 us  [spread_rows(): return lax.all_gather(along, 'tp', axis=1).reshape(-1, value.shape[1])]
    pallas_call x0 -> x2, Pallas kernels: none -> 71.3 us  [the longest x1 43.6 us: mixer_backward(): pl.pallas_call(backward_body, grid=(count,), in_specs=[pl.BlockSpec((BLOC...]
    ppermute x2, waiting for transfers between devices: 17.4 us -> 71 us  [partner(): return lax.ppermute(value, 'ctx', [(i, i ^ 1) for i in range(nctx)])]
    another operation x74 -> x2, other arithmetic: 37.7 us -> 0.36 us
    all_to_all x2, waiting for transfers between devices: 119 us -> 155 us  [return_grad(): lax.all_to_all(summed.astype(BF16).reshape(nctx, rows, grad.shape[1]), 'c...]
    unnamed x101 -> x92, local copies, waits for them, and re-layouts: 77.8 us -> 51.3 us
  transfers between devices with their start and end apart: 18 -> 18, of which waited for: 9 -> 12; matrix products, arithmetic and copies ran while one was open for 45% -> 16% of each run, Pallas kernels for 0% -> 3%
where the time goes in v2:
time: 1410 us; the launch traced here: 1400 us
  waiting for transfers between devices  927 us (66%)
  matrix products  133 us (9%)
  local copies, waits for them, and re-layouts  102 us (7%)
  Pallas kernels  71.3 us (5%)
  other arithmetic  67.2 us (5%)
  blocking collectives  52.3 us (4%)
  starting transfers between devices  35.2 us (2%)
  between operations  14.8 us (1%)
    all_to_all x1, waiting for transfers between devices, fetch_weight(): mine = lax.all_to_all(packed, 'ctx', 0, 0, tiled=True)  231 us
    all_gather x2, waiting for transfers between devices, spread_rows(): return lax.all_gather(along, 'tp', axis=1).reshape(-1, value.shape[1])  215 us
    all_to_all x2, waiting for transfers between devices, return_grad(): lax.all_to_all(summed.astype(BF16).reshape(nctx, rows, grad.shape[1]), 'c...  155 us
    all_to_all x2, waiting for transfers between devices, return_grad(): lax.all_to_all(parts, 'dp', 0, 0, tiled=True).astype(F32)  104 us
    all_gather x2, waiting for transfers between devices, fetch_weight(): lax.all_gather(mine.reshape(-1, packed.shape[2]), 'dp', axis=0, tiled=True)  88.5 us
    ppermute x2, waiting for transfers between devices, partner(): return lax.ppermute(value, 'ctx', [(i, i ^ 1) for i in range(nctx)])  71 us
    psum x1, waiting for transfers between devices, shards(): table, norm_gain_grad = lax.psum((table, norm_gain_grad), ('dp', 'ctx'))  59.9 us
    all_to_all x1, blocking collectives, fetch_weight(): mine = lax.all_to_all(packed, 'ctx', 0, 0, tiled=True)  52.3 us
  transfers between devices with their start and end apart: 18, of which 12 were waited for; matrix products, arithmetic and copies ran while one was open for 16% of the time, Pallas kernels for 3%

profile of v2, /device:TPU:0, one launch (start us, length us, event | category | flops | bytes accessed | tf_op | source)
XLA Modules:
  0.0 1401.7 jit_solution(17759013143516782664)
XLA Ops:
  22.6 11.2 copy.72
  48.9 231.2 %all-to-all-done = bf16[4,512,1288]{1,2,0:T(8,128)(2,1)} async-done(((bf16[4,512,1288]{1,2,0:T(8,128)(2,1)}), bf16[4,512,1288]{1,2,0:T(8,128)(2,1)}, u32[]{:S(2)}, u32[]{:S(2)}) %all-to-all-start) | async-done | bytes 5275680 | tf_op jit(solution)/shard_map/all_to_all | solution.py:384
  289.8 52.3 %all_to_all.30 = bf16[4,512,512]{1,2,0:T(8,128)(2,1)S(1)} all-to-all(bf16[4,512,512]{1,2,0:T(8,128)(2,1)} %bitcast.155), channel_id=1, replica_groups=mesh['dp'=2,'ctx'=4,'tp'=4] {'ctx'}, dimensions={0} | all-to-all | bytes 4194304 | tf_op jit(solution)/shard_map/all_to_all | solution.py:384
  345.7 71.4 %all-gather.12.cloned.1.call-done = bf16[4096,1288]{0,1:T(8,128)(2,1)} async-done(((bf16[2048,1288]{0,1:T(8,128)(2,1)}), bf16[4096,1288]{0,1:T(8,128)(2,1)}) %all-gather.12.cloned.1.call-update) | async-done | bytes 10551312 | tf_op jit(solution)/shard_map/all_gather | solution.py:385
  417.1 107.4 %all-gather.24.cloned.1.call-done = bf16[4,512,4096]{2,1,0:T(8,128)(2,1)} async-done(((bf16[4,128,4096]{2,1,0:T(8,128)(2,1)}), bf16[4,512,4096]{2,1,0:T(8,128)(2,1)}) %all-gather.24.cloned.1.call-update) | async-done | bytes 16777232 | tf_op jit(solution)/shard_map/all_gather | solution.py:380
  533.7 15.0 %fusion.15.gate_ref = f32[2048,512]{1,0:T(8,128)} fusion(bf16[2048,4096]{1,0:T(8,128)(2,1)} %bitcast.182, bf16[4096,1288]{0,1:T(8,128)(2,1)S(1)} %copy-done.12), kind=kOutput, calls=%fused_computation.28 | convolution fusion | flops 8589934592 | bytes 25165824 | tf_op jit(solution)/shard_map/dot_general | solution.py:438
  548.7 17.5 %fusion.17.conv_ref.edge_ref = bf16[2048,768]{1,0:T(8,128)(2,1)} fusion(bf16[2048,4096]{1,0:T(8,128)(2,1)} %bitcast.183, bf16[4096,1288]{0,1:T(8,128)(2,1)S(1)} %copy-done.12), kind=kOutput, calls=%fused_computation.32 | convolution fusion | flops 12886474752 | bytes 26214400 | tf_op jit(solution)/shard_map/dot_general | solution.py:439
  566.1 17.1 %all-gather.16.cloned.1.call-done = bf16[4096,512]{1,0:T(8,128)(2,1)} async-done(((bf16[2048,512]{1,0:T(8,128)(2,1)}), bf16[4096,512]{1,0:T(8,128)(2,1)}) %all-gather.16.cloned.1.call-update) | async-done | bytes 4194320 | tf_op jit(solution)/shard_map/all_gather | solution.py:385
  583.2 107.4 %all-gather.26.cloned.1.call-done = bf16[4,512,4096]{2,1,0:T(8,128)(2,1)} async-done(((bf16[4,128,4096]{2,1,0:T(8,128)(2,1)}), bf16[4,512,4096]{2,1,0:T(8,128)(2,1)}) %all-gather.26.cloned.1.call-update) | async-done | bytes 16777232 | tf_op jit(solution)/shard_map/all_gather | solution.py:380
  690.6 15.4 %fusion.40.up_ref = f32[2048,512]{1,0:T(8,128)} fusion(bf16[2048,4096]{1,0:T(8,128)(2,1)} %bitcast.185, bf16[4096,512]{1,0:T(8,128)(2,1)} %all-gather.16.cloned.1.call-done), kind=kOutput, calls=%fused_computation.102 | convolution fusion | flops 8589934592 | bytes 25165824 | tf_op jit(solution)/shard_map/dot_general | solution.py:437
  706.0 27.7 %mixer_forward.1 = (bf16[2048,768]{1,0:T(8,128)(2,1)}, f32[2048,512]{1,0:T(8,128)}, f32[8,128,512]{2,1,0:T(8,128)S(1)}, f32[2,2048]{1,0:T(2,128)S(1)}) custom-call(bf16[2048,768]{1,0:T(8,128)(2,1)} %fusion.17.conv_ref.edge_ref, f32[2048,8]{1,0:T(8,128)S(1)} %fusion.35.raw_ref, f32[2048,512]{1,0:T(8,128)} %fusion.15.gate_ref, f32[2048,512]{1,0:T(8,128)} %fusion.40.up_ref, ...), custom_call_target="tpu_custom_call" | custom-call | tf_op jit(solution)/shard_map/mixer_forward/pallas_call | solution.py:163
  742.3 11.7 convolution_convert_fusion.1
  755.7 43.6 %mixer_backward.1 = (bf16[2048,512]{1,0:T(8,128)(2,1)}, bf16[2048,512]{1,0:T(8,128)(2,1)}, f32[2048,256]{1,0:T(8,128)}, f32[2048,8]{1,0:T(8,128)}, f32[5,512]{1,...) custom-call(bf16[2048,768]{1,0:T(8,128)(2,1)} %fusion.17.conv_ref.edge_ref, bf16[2048,768]{1,0:T(8,128)(2,1)} %fusion.17.conv_ref.edge_ref, ...), custom_call_target="tpu_custom_call" | custom-call | tf_op jit(solution)/shard_map/mixer_backward/pallas_call | solution.py:313
  804.9 68.8 %collective-permute-done.1 = f32[2048,128]{1,0:T(8,128)S(1)} collective-permute-done((f32[2048,128]{1,0:T(8,128)S(1)}, f32[2048,128]{1,0:T(8,128)S(1)}, u32[]{:S(2)}, u32[]{:S(2)}) %collective-permute-start.1) | collective-permute-done | bytes 1048608 | tf_op jit(solution)/shard_map/ppermute | solution.py:419
  878.9 25.7 %convolution_convert_fusion = bf16[2048,4096]{1,0:T(8,128)(2,1)} fusion(bf16[4096,8]{0,1:T(8,128)(2,1)S(1)} %slice-done.1, bf16[4096,128]{0,1:T(8,128)(2,1)S(1)} %constant_dynamic-slice_fusion, bf16[4096,1024]{0,1:T(8,128)(2,1)S(1)} %slice-done, bf16[2048,8]{1,0:T(8,128)(2,1)S(1)} %convert_element_type.66, bf16[2048,128]{1,0:T(8,128)(2,1)S(1)} %fusion.27, ...), kind=kOutput, calls=%fused_computation | convolution fusion | flops 19517472768 | bytes 31031296 | tf_op jit(solution)/shard_map/dot_general | solution.py:360
  904.6 14.1 %convolution_convert_fusion.3 = bf16[4096,512]{1,0:T(8,128)(2,1)} fusion(bf16[2048,4096]{1,0:T(8,128)(2,1)} %bitcast.186, bf16[2048,512]{1,0:T(8,128)(2,1)S(1)} %multiply_convert_fusion), kind=kOutput, calls=%fused_computation.23 | convolution fusion | flops 8592031744 | bytes 23068672 | tf_op jit(solution)/shard_map/dot_general | solution.py:364
  924.5 25.0 %convolution_convert_fusion.2 = bf16[4096,1160]{0,1:T(8,128)(2,1)} fusion(bf16[2048,4096]{1,0:T(8,128)(2,1)} %bitcast.184, bf16[2048,8]{1,0:T(8,128)(2,1)S(1)} %convert_element_type.66, bf16[2048,128]{1,0:T(8,128)(2,1)S(1)} %fusion.27, bf16[2048,512]{1,0:T(8,128)(2,1)} %get-tuple-element.27, bf16[2048,512]{1,0:T(8,128)(2,1)S(1)} %copy-done.38), kind=kOutput, calls=%fused_computation.2 | convolution fusion | flops 19485327360 | bytes 31031296 | tf_op jit(solution)/shard_map/dot_general | solution.py:364
  958.9 11.9 all-to-all-done.4
  989.4 92.4 %all-to-all-done.2 = bf16[2,2048,1160]{1,2,0:T(8,128)(2,1)} async-done(((bf16[2,2048,1160]{1,2,0:T(8,128)(2,1)}), bf16[2,2048,1160]{1,2,0:T(8,128)(2,1)}, u32[]{:S(2)}, u32[]{:S(2)}) %all-to-all-start.2) | async-done | bytes 9502752 | tf_op jit(solution)/shard_map/all_to_all | solution.py:391
  1087.2 9.9 reduce_sum.104
  1101.9 65.3 %all-to-all-done.5 = bf16[4,512,512]{2,1,0:T(8,128)(2,1)S(1)} async-done(((bf16[4,512,512]{2,1,0:T(8,128)(2,1)}), bf16[4,512,512]{2,1,0:T(8,128)(2,1)S(1)}, u32[]{:S(2)}, u32[]{:S(2)}) %all-to-all-start.5) | async-done | bytes 2097184 | tf_op jit(solution)/shard_map/all_to_all | solution.py:392
  1187.2 89.9 %all-to-all-done.3 = bf16[4,512,1160]{1,2,0:T(8,128)(2,1)} async-done(((bf16[4,512,1160]{1,2,0:T(8,128)(2,1)}), bf16[4,512,1160]{1,2,0:T(8,128)(2,1)}, u32[]{:S(2)}, u32[]{:S(2)}) %all-to-all-start.3) | async-done | bytes 4751392 | tf_op jit(solution)/shard_map/all_to_all | solution.py:392
  1289.5 13.3 copy.88
  1324.8 59.9 %all-reduce.13.cloned.1.call-done = (f32[4096]{0:T(1024)}, f32[4,3736]{1,0:T(4,128)}) async-done(((f32[4096]{0:T(1024)}, f32[4,3736]{1,0:T(4,128)}), (f32[4096]{0:T(1024)}, f32[4,3736]{1,0:T(4,128)})) %all-reduce.13.cloned.1.call-update) | async-done | bytes 76176 | tf_op jit(solution)/shard_map/psum | solution.py:501
  (198 shorter events, 181.8 us)
Async XLA Ops:
  7.2 338.5 %copy-start = (f32[5,2048]{1,0:T(8,128)S(1)}, f32[5,2048]{1,0:T(8,128)}, u32[]{:S(2)}) copy-start(f32[5,2048]{1,0:T(8,128)} %param.16) | copy-start | bytes 122884
  7.2 278.6 %all-gather.22.cloned.1.call-start = ((), (), s32[]{:S(2)}) async-start(), calls=%async_computation.15 | async-start | bytes 5242880 | tf_op jit(solution)/shard_map/all_gather | solution.py:379
  40.4 239.7 %all-to-all-start = ((bf16[4,512,1288]{1,2,0:T(8,128)(2,1)}), bf16[4,512,1288]{1,2,0:T(8,128)(2,1)}, u32[]{:S(2)}, u32[]{:S(2)}) async-start(bf16[4,512,1288]{1,2,0:T(8,128)(2,1)} %bitcast.151), calls=%async_computation | async-start | bytes 10551296 | tf_op jit(solution)/shard_map/all_to_all | solution.py:384
  46.5 298.1 %all-gather.14.cloned.1.call-start = ((), (), s32[]{:S(2)}) async-start(), calls=%async_computation.9 | async-start | bytes 5242880 | tf_op jit(solution)/shard_map/all_gather | solution.py:379
  48.8 368.3 %all-gather.12.cloned.1.call-start = ((), (), s32[]{:S(2)}) async-start(), calls=%async_computation.8 | async-start | bytes 15826944 | tf_op jit(solution)/shard_map/all_gather | solution.py:385
  285.8 238.7 %all-gather.24.cloned.1.call-start = ((), (), s32[]{:S(2)}) async-start(), calls=%async_computation.16 | async-start | bytes 20971520 | tf_op jit(solution)/shard_map/all_gather | solution.py:380
  286.3 296.9 %all-gather.16.cloned.1.call-start = ((), (), s32[]{:S(2)}) async-start(), calls=%async_computation.10 | async-start | bytes 6291456 | tf_op jit(solution)/shard_map/all_gather | solution.py:385
  344.5 346.1 %all-gather.26.cloned.1.call-start = ((), (), s32[]{:S(2)}) async-start(), calls=%async_computation.17 | async-start | bytes 20971520 | tf_op jit(solution)/shard_map/all_gather | solution.py:380
  345.1 634.8 %reduce-scatter.3.cloned.1.call-start = ((), (), s32[]{:S(2)}) async-start(), calls=%async_computation.11 | async-start | bytes 17825792 | tf_op jit(solution)/shard_map/reduce_scatter | solution.py:397
  345.6 360.3 %copy-start.5 = (f32[3,1,8]{2,0,1:T(4,128)}, f32[3,1,8]{2,0,1:T(4,128)S(1)}, u32[]{:S(2)}) copy-start(f32[3,1,8]{2,0,1:T(4,128)S(1)} %copy.106) | copy-start | bytes 292
  345.7 360.3 %copy-start.6 = (f32[1,512]{1,0:T(1,128)}, f32[1,512]{1,0:T(1,128)S(1)}, u32[]{:S(2)}) copy-start(f32[1,512]{1,0:T(1,128)S(1)} %fusion.51.gain_ref) | copy-start | bytes 6148
  345.7 360.3 %copy-start.4 = (f32[5,768]{1,0:T(8,128)}, f32[5,768]{1,0:T(8,128)S(1)}, u32[]{:S(2)}) copy-start(f32[5,768]{1,0:T(8,128)S(1)} %pad_maximum_fusion.4.kernel_ref) | copy-start | bytes 46084
  533.7 172.3 %copy-start.2 = (f32[2048,8]{1,0:T(8,128)}, f32[2048,8]{1,0:T(8,128)S(1)}, u32[]{:S(2)}) copy-start(f32[2048,8]{1,0:T(8,128)S(1)} %fusion.35.raw_ref) | copy-start | bytes 196612
  735.1 3.7 collective-permute-start
  754.1 418.4 %reduce-scatter.5.cloned.1.call-start = ((), (), s32[]{:S(2)}) async-start(), calls=%async_computation.13 | async-start | bytes 17825792 | tf_op jit(solution)/shard_map/reduce_scatter | solution.py:397
  800.7 73.0 %collective-permute-start.1 = (f32[2048,128]{1,0:T(8,128)S(1)}, f32[2048,128]{1,0:T(8,128)S(1)}, u32[]{:S(2)}, u32[]{:S(2)}) collective-permute-start(f32[2048,128]{1,0:T(8,128)S(1)} %constant_dynamic-slice_fusion.2), channel_id=1, source_target_pairs={{0,4},{4,0},{8,12},{12,8},{1,5},{5,1},{9,13},{13,9},{2,6},{6,2},{1... | collective-permute-start | bytes 3145736 | tf_op jit(solution)/shard_map/ppermute | solution.py:419
  918.7 52.1 %all-to-all-start.4 = ((bf16[2,2048,512]{2,1,0:T(8,128)(2,1)}), bf16[2,2048,512]{2,1,0:T(8,128)(2,1)}, u32[]{:S(2)}, u32[]{:S(2)}) async-start(bf16[2,2048,512]{2,1,0:T(8,128)(2,1)} %bitcast.160), calls=%async_computation.6 | async-start | bytes 8388608 | tf_op jit(solution)/shard_map/all_to_all | solution.py:391
  970.8 111.0 %all-to-all-start.2 = ((bf16[2,2048,1160]{1,2,0:T(8,128)(2,1)}), bf16[2,2048,1160]{1,2,0:T(8,128)(2,1)}, u32[]{:S(2)}, u32[]{:S(2)}) async-start(bf16[2,2048,1160]{1,2,0:T(8,128)(2,1)} %bitcast.143), calls=%async_computation.4 | async-start | bytes 19005440 | tf_op jit(solution)/shard_map/all_to_all | solution.py:391
  979.5 329.0 %all-gather.18.cloned.1.call-start = ((), (), s32[]{:S(2)}) async-start(), calls=%async_computation.12 | async-start | bytes 5242880 | tf_op jit(solution)/shard_map/all_gather | solution.py:455
  1081.8 85.5 %all-to-all-start.5 = ((bf16[4,512,512]{2,1,0:T(8,128)(2,1)}), bf16[4,512,512]{2,1,0:T(8,128)(2,1)S(1)}, u32[]{:S(2)}, u32[]{:S(2)}) async-start(bf16[4,512,512]{2,1,0:T(8,128)(2,1)} %bitcast.153), calls=%async_computation.7 | async-start | bytes 4194304 | tf_op jit(solution)/shard_map/all_to_all | solution.py:392
  1167.3 109.7 %all-to-all-start.3 = ((bf16[4,512,1160]{1,2,0:T(8,128)(2,1)}), bf16[4,512,1160]{1,2,0:T(8,128)(2,1)}, u32[]{:S(2)}, u32[]{:S(2)}) async-start(bf16[4,512,1160]{1,2,0:T(8,128)(2,1)} %bitcast.146), calls=%async_computation.5 | async-start | bytes 9502720 | tf_op jit(solution)/shard_map/all_to_all | solution.py:392
  1172.4 136.0 %all-gather.20.cloned.1.call-start = ((), (), s32[]{:S(2)}) async-start(), calls=%async_computation.14 | async-start | bytes 5242880 | tf_op jit(solution)/shard_map/all_gather | solution.py:482
  1173.0 211.7 %all-reduce.13.cloned.1.call-start = ((), (), s32[]{:S(2)}) async-start(), calls=%async_computation.18 | async-start | bytes 155648 | tf_op jit(solution)/shard_map/psum | solution.py:501
  1316.4 78.5 %copy-start.1 = (f32[5,2048]{1,0:T(8,128)S(1)}, f32[5,2048]{1,0:T(8,128)}, u32[]{:S(2)}) copy-start(f32[5,2048]{1,0:T(8,128)} %param.16) | copy-start | bytes 122884
  (35 other events, 281.2 us)
Sparse Core Ops, SparseCore 0:
  22.7 139.2 all-gather.21
  163.5 122.7 all-gather.13
  288.4 128.6 all-gather.11
  418.5 105.9 all-gather.23
  526.5 56.7 all-gather.15
  584.7 105.9 all-gather.25
  754.2 202.5 reduce-scatter.2
  960.9 205.7 reduce-scatter.4
  1168.3 35.8 all-gather.17
  1205.6 34.4 all-gather.19
  1316.5 68.1 all-reduce.12

commit v3 on v2

--- a/solution.py
+++ b/solution.py
@@ -11,6 +11,8 @@
 N = 128
 BLOCK = 256
 EDGE = 8
+DEPTH = 3
+MESH = pl.DeviceIdType.MESH
 EPS = 1e-05
 HIGH = lax.Precision.HIGHEST
 F32 = jnp.float32
@@ -89,8 +91,8 @@
     return total
 
 
-def block_steps(raw_ref, head_ref):
-    dt = softplus(raw_ref[...] + head_ref[0:1, :])
+def block_steps(raw, head_ref):
+    dt = softplus(raw + head_ref[0:1, :])
     decay = -jnp.exp(head_ref[1:2, :])
     log_step = dt * decay
     lower = order_mask(False).astype(F32)
@@ -99,8 +101,12 @@
     return dt, decay, total, total_t
 
 
-def forward_body(conv_ref, raw_ref, gate_ref, up_ref, kernel_ref, head_ref, gain_ref, low_ref, ssd_ref, state_ref, sums_ref, state, buffer):
+def forward_body(
+    odd_ref, gate_ref, x_ref, own_ref, step_ref, other_ref, up_ref, kernel_ref, head_ref, gain_ref,
+    low_ref, ssd_ref, state_ref, sums_ref, state, buffer,
+):
     width = gate_ref.shape[1]
+    raw = step_ref[:, 0 : head_ref.shape[1]]
     first = pl.program_id(0) == 0
 
     @pl.when(first)
@@ -112,13 +118,16 @@
     def _():
         buffer[0:EDGE, :] = buffer[BLOCK : BLOCK + EDGE, :]
 
-    buffer[EDGE : EDGE + BLOCK, :] = conv_ref[...].astype(F32)
+    buffer[EDGE : EDGE + BLOCK, 0:width] = x_ref[...].astype(BF16).astype(F32)
+    buffer[EDGE : EDGE + BLOCK, width : width + N] = own_ref[...].astype(BF16).astype(F32)
+    buffer[EDGE : EDGE + BLOCK, width + N :] = other_ref[...].astype(BF16).astype(F32)
     before = convolve(buffer, kernel_ref, 0, buffer.shape[1])
     low_ref[...] = (before * sigmoid(before)).astype(BF16)
-    dt, _, total, total_t = block_steps(raw_ref, head_ref)
+    dt, _, total, total_t = block_steps(raw, head_ref)
     state_ref[0] = state[...]
-    inject = low_ref[:, width : width + N]
-    readout = low_ref[:, width + N : width + 2 * N]
+    odd = odd_ref[0, 0] == 1
+    own, other = low_ref[:, width : width + N], low_ref[:, width + N : width + 2 * N]
+    inject, readout = jnp.where(odd, other, own), jnp.where(odd, own, other)
     scores = dot_on(readout, inject, 1, 1)
     mask = order_mask(False)
     half = first_half(BLOCK)
@@ -154,19 +163,29 @@
     sums_ref[1:2, :] = dot_on(ones, cross, 1, 1, HIGH)[0:1, :]
 
 
-def mixer_forward(conv_input, raw_dt, gate_pre, grad_gated, kernel, heads, gain):
-    length, width = gate_pre.shape
-    wide = conv_input.shape[1]
+def proj_specs(width, index):
+    narrow = lambda place: pl.BlockSpec((BLOCK, N), lambda i: (index(i), 2 * width // N + place))
+    return [
+        pl.BlockSpec(memory_space=pltpu.SMEM),
+        pl.BlockSpec((BLOCK, width), lambda i: (index(i), 0)),
+        pl.BlockSpec((BLOCK, width), lambda i: (index(i), 1)),
+        narrow(0),
+        narrow(1),
+        narrow(2),
+    ]
+
+
+def mixer_forward(odd, proj, grad_gated, kernel, heads, gain):
+    length, width = grad_gated.shape
+    wide = width + 2 * N
     count = length // BLOCK
     rows = lambda i: (i, 0)
     whole = lambda i: (0, 0)
     return pl.pallas_call(
         forward_body,
         grid=(count,),
-        in_specs=[
-            pl.BlockSpec((BLOCK, wide), rows),
-            pl.BlockSpec((BLOCK, raw_dt.shape[1]), rows),
-            pl.BlockSpec((BLOCK, width), rows),
+        in_specs=proj_specs(width, lambda i: i)
+        + [
             pl.BlockSpec((BLOCK, width), rows),
             pl.BlockSpec(kernel.shape, whole),
             pl.BlockSpec(heads.shape, whole),
@@ -187,15 +206,16 @@
         scratch_shapes=[pltpu.VMEM((N, width), F32), pltpu.VMEM((BLOCK + EDGE, wide), F32)],
         compiler_params=pltpu.CompilerParams(vmem_limit_bytes=48 << 20),
         name="mixer_forward",
-    )(conv_input, raw_dt, gate_pre, grad_gated, kernel, heads, gain)
+    )(odd, proj, proj, proj, proj, proj, grad_gated, kernel, heads, gain)
 
 
 def backward_body(
-    conv_ref, edge_ref, low_ref, raw_ref, gate_ref, up_ref, ssd_ref, state_ref, norm_ref, kernel_ref, head_ref, gain_ref,
-    grad_gate_ref, grad_in_ref, grad_maps_ref, grad_dt_ref, grad_kernel_ref, grad_head_ref, grad_gain_ref,
+    odd_ref, gate_ref, x_ref, step_ref, edge_ref, low_ref, up_ref, ssd_ref, state_ref, norm_ref, kernel_ref, head_ref, gain_ref,
+    grad_ref, grad_step_ref, grad_own_ref, grad_other_ref, grad_kernel_ref, grad_head_ref, grad_gain_ref,
     adjoint, buffer, grads, next_state,
 ):
     width = gate_ref.shape[1]
+    raw = step_ref[:, 0 : head_ref.shape[1]]
     taps = kernel_ref.shape[0] - 1
     count = pl.num_programs(0)
     step = pl.program_id(0)
@@ -213,12 +233,13 @@
     def _():
         grads[BLOCK : BLOCK + EDGE, :] = grads[0:EDGE, :]
 
-    edge = edge_ref[edge_ref.shape[0] - EDGE :, 0:width].astype(F32)
-    buffer[0:EDGE, :] = jnp.where(step == count - 1, 0.0, edge)
-    buffer[EDGE : EDGE + BLOCK, :] = conv_ref[:, 0:width].astype(F32)
-    dt, decay, total, total_t = block_steps(raw_ref, head_ref)
-    inject = low_ref[:, width : width + N]
-    readout = low_ref[:, width + N : width + 2 * N]
+    last = step == count - 1
+    buffer[0:EDGE, :] = jnp.where(last, 0.0, edge_ref[...].astype(BF16).astype(F32))
+    buffer[EDGE : EDGE + BLOCK, :] = x_ref[...].astype(BF16).astype(F32)
+    dt, decay, total, total_t = block_steps(raw, head_ref)
+    odd = odd_ref[0, 0] == 1
+    own, other = low_ref[:, width : width + N], low_ref[:, width + N : width + 2 * N]
+    inject, readout = jnp.where(odd, other, own), jnp.where(odd, own, other)
     scores_t = dot_on(inject, readout, 1, 1)
     mask_t = order_mask(True)
     half = first_half(BLOCK)
@@ -240,7 +261,7 @@
         gated = ssd * gate
         grad_gain_ref[0:1, cols] += jnp.sum(up * gated * inverse, axis=0, keepdims=True)
         grad_pre = inverse * (up * gain_ref[0:1, cols]) - gated * pull
-        grad_gate_ref[:, cols] = (grad_pre * ssd * (sig * (1.0 + gate_pre * (1.0 - sig)))).astype(BF16)
+        grad_ref[:, cols] = (grad_pre * ssd * (sig * (1.0 + gate_pre * (1.0 - sig)))).astype(BF16)
         grad_ssd = grad_pre * gate
         grad_two = split(grad_ssd)
         total_p = over_pair(total, pair)
@@ -284,63 +305,73 @@
     ends = head_sums(jnp.concatenate(end_parts, axis=1))
     grad_log = dot_on(upper, row_grads, 1, 0, HIGH) + ends
     grad_dt = head_sums(jnp.concatenate(step_parts, axis=1)) + decay * grad_log
-    grad_raw = grad_dt * sigmoid(raw_ref[...] + head_ref[0:1, :])
-    grad_dt_ref[...] = grad_raw
+    grad_raw = grad_dt * sigmoid(raw + head_ref[0:1, :])
+    grad_step_ref[...] = jnp.zeros((BLOCK, N), BF16)
+    grad_step_ref[:, 0 : grad_raw.shape[1]] = grad_raw.astype(BF16)
     grad_head_ref[0:1, :] += jnp.sum(grad_raw, axis=0, keepdims=True)
     grad_head_ref[1:2, :] += decay * jnp.sum(dt * grad_log, axis=0, keepdims=True)
     grad_head_ref[2:3, :] += head_sums(jnp.concatenate(skip_parts, axis=1))
     scores_two = split(grad_scores_t)
-    grad_maps_ref[:, 0:N] = grad_inject + dot_two(scores_two, readout, 1, 0)
-    grad_maps_ref[:, N : 2 * N] = grad_readout + dot_two(scores_two, inject, 0, 0)
+    grad_inject = grad_inject + dot_two(scores_two, readout, 1, 0)
+    grad_readout = grad_readout + dot_two(scores_two, inject, 0, 0)
+    grad_own_ref[...] = jnp.where(odd, grad_readout, grad_inject)
+    grad_other_ref[...] = jnp.where(odd, grad_inject, grad_readout)
+    grad_ref[:, width : 2 * width] = convolve_back(buffer, grads, kernel_ref, grad_kernel_ref)
+
+
+def convolve_back(buffer, grads, kernel_ref, grad_kernel_ref):
+    taps = kernel_ref.shape[0] - 1
+    width = grads.shape[1]
     here = grads[0:BLOCK, :]
     grad_kernel_ref[taps : taps + 1, :] += jnp.sum(here, axis=0, keepdims=True)
-    total_in = jnp.zeros((BLOCK, width), F32)
+    total = jnp.zeros((BLOCK, width), F32)
     for tap in range(taps):
         low = EDGE - taps + 1 + tap
         grad_kernel_ref[tap : tap + 1, :] += jnp.sum(here * buffer[low : low + BLOCK, :], axis=0, keepdims=True)
         ahead = taps - 1 - tap
-        total_in = total_in + kernel_ref[tap : tap + 1, 0:width] * grads[ahead : ahead + BLOCK, :]
-    grad_in_ref[...] = total_in.astype(BF16)
-
-
-def mixer_backward(conv_input, low, raw_dt, gate_pre, grad_gated, ssd, states, norms, kernel, heads, gain):
-    length, width = gate_pre.shape
-    wide = conv_input.shape[1]
+        total = total + kernel_ref[tap : tap + 1, 0:width] * grads[ahead : ahead + BLOCK, :]
+    return total.astype(BF16)
+
+
+def mixer_backward(odd, proj, low, grad_gated, ssd, states, norms, kernel, heads, gain):
+    length, width = grad_gated.shape
+    wide = width + 2 * N
     count = length // BLOCK
-    edge = 16
-    back = lambda i: (count - 1 - i, 0)
+    place = lambda i: count - 1 - i
+    back = lambda i: (place(i), 0)
+    edge = lambda i: jnp.maximum(place(i) * (BLOCK // EDGE) - 1, 0)
     whole = lambda i: (0, 0)
+    specs = proj_specs(width, place)
     return pl.pallas_call(
         backward_body,
         grid=(count,),
-        in_specs=[
+        in_specs=specs[:3]
+        + [
+            specs[4],
+            pl.BlockSpec((EDGE, width), lambda i: (edge(i), 1)),
             pl.BlockSpec((BLOCK, wide), back),
-            pl.BlockSpec((edge, wide), lambda i: (jnp.maximum((count - 1 - i) * (BLOCK // edge) - 1, 0), 0)),
-            pl.BlockSpec((BLOCK, wide), back),
-            pl.BlockSpec((BLOCK, raw_dt.shape[1]), back),
             pl.BlockSpec((BLOCK, width), back),
             pl.BlockSpec((BLOCK, width), back),
-            pl.BlockSpec((BLOCK, width), back),
-            pl.BlockSpec((1, N, width), lambda i: (count - 1 - i, 0, 0)),
+            pl.BlockSpec((1, N, width), lambda i: (place(i), 0, 0)),
             pl.BlockSpec((BLOCK, norms.shape[1]), back),
             pl.BlockSpec(kernel.shape, whole),
             pl.BlockSpec(heads.shape, whole),
             pl.BlockSpec(gain.shape, whole),
         ],
         out_specs=[
-            pl.BlockSpec((BLOCK, width), back),
-            pl.BlockSpec((BLOCK, width), back),
-            pl.BlockSpec((BLOCK, 2 * N), back),
-            pl.BlockSpec((BLOCK, raw_dt.shape[1]), back),
+            pl.BlockSpec((BLOCK, 2 * width), back),
+            pl.BlockSpec((BLOCK, N), back),
+            pl.BlockSpec((BLOCK, N), back),
+            pl.BlockSpec((BLOCK, N), back),
             pl.BlockSpec((kernel.shape[0], width), whole),
             pl.BlockSpec(heads.shape, whole),
             pl.BlockSpec(gain.shape, whole),
         ],
         out_shape=[
-            jax.ShapeDtypeStruct((length, width), BF16),
-            jax.ShapeDtypeStruct((length, width), BF16),
-            jax.ShapeDtypeStruct((length, 2 * N), F32),
-            jax.ShapeDtypeStruct(raw_dt.shape, F32),
+            jax.ShapeDtypeStruct((length, 2 * width), BF16),
+            jax.ShapeDtypeStruct((length, N), BF16),
+            jax.ShapeDtypeStruct((length, N), F32),
+            jax.ShapeDtypeStruct((length, N), F32),
             jax.ShapeDtypeStruct((kernel.shape[0], width), F32),
             jax.ShapeDtypeStruct(heads.shape, F32),
             jax.ShapeDtypeStruct(gain.shape, F32),
@@ -353,7 +384,463 @@
         ],
         compiler_params=pltpu.CompilerParams(vmem_limit_bytes=56 << 20),
         name="mixer_backward",
-    )(conv_input, conv_input, low, raw_dt, gate_pre, grad_gated, ssd, states, norms, kernel, heads, gain)
+    )(odd, proj, proj, proj, proj, low, grad_gated, ssd, states, norms, kernel, heads, gain)
+
+
+def map_backward_body(own_ref, edge_ref, mine_ref, theirs_ref, step_ref, kernel_ref, grad_ref, grad_kernel_ref, buffer, grads):
+    step = pl.program_id(0)
+
+    @pl.when(step == 0)
+    def _():
+        grads[BLOCK : BLOCK + EDGE, :] = jnp.zeros((EDGE, N), F32)
+        grad_kernel_ref[...] = jnp.zeros_like(grad_kernel_ref)
+
+    @pl.when(step > 0)
+    def _():
+        grads[BLOCK : BLOCK + EDGE, :] = grads[0:EDGE, :]
+
+    last = step == pl.num_programs(0) - 1
+    buffer[0:EDGE, :] = jnp.where(last, 0.0, edge_ref[...].astype(BF16).astype(F32))
+    buffer[EDGE : EDGE + BLOCK, :] = own_ref[...].astype(BF16).astype(F32)
+    before = convolve(buffer, kernel_ref, 0, N)
+    sig = sigmoid(before)
+    grads[0:BLOCK, :] = (mine_ref[...] + theirs_ref[...]) * (sig * (1.0 + before * (1.0 - sig)))
+    grad_ref[:, 0:N] = convolve_back(buffer, grads, kernel_ref, grad_kernel_ref)
+    grad_ref[:, N : 2 * N] = step_ref[...]
+
+
+def map_backward(proj, mine, theirs, steps, kernel, column):
+    length = mine.shape[0]
+    count = length // BLOCK
+    place = lambda i: count - 1 - i
+    edge = lambda i: jnp.maximum(place(i) * (BLOCK // EDGE) - 1, 0)
+    back = lambda i: (place(i), 0)
+    whole = lambda i: (0, 0)
+    narrow = pl.BlockSpec((BLOCK, N), back)
+    return pl.pallas_call(
+        map_backward_body,
+        grid=(count,),
+        in_specs=[
+            pl.BlockSpec((BLOCK, N), lambda i: (place(i), column // N)),
+            pl.BlockSpec((EDGE, N), lambda i: (edge(i), column // N)),
+            narrow,
+            narrow,
+            narrow,
+            pl.BlockSpec(kernel.shape, whole),
+        ],
+        out_specs=[pl.BlockSpec((BLOCK, 2 * N), back), pl.BlockSpec(kernel.shape, whole)],
+        out_shape=[jax.ShapeDtypeStruct((length, 2 * N), BF16), jax.ShapeDtypeStruct(kernel.shape, F32)],
+        scratch_shapes=[pltpu.VMEM((BLOCK + EDGE, N), F32), pltpu.VMEM((BLOCK + EDGE, N), F32)],
+        name="map_backward",
+    )(proj, proj, mine, theirs, steps, kernel)
+
+
+def remote(src, dst, send, recv, device):
+    return pltpu.make_async_remote_copy(
+        src_ref=src, dst_ref=dst, send_sem=send, recv_sem=recv, device_id=device, device_id_type=MESH
+    )
+
+
+def gather_body(order, sizes, *refs):
+    nctx, ndp, ntp = sizes
+    ntok, nw = 2, (len(refs) - 9) // 2 - 2
+    toks, weights = refs[:ntok], refs[ntok : ntok + nw]
+    tok_outs = refs[ntok + nw : 2 * ntok + nw]
+    weight_outs = refs[2 * ntok + nw : 2 * ntok + 2 * nw]
+    z_send, z_recv, t_send, t_recv, w_send, w_recv, x_send, x_recv, own = refs[2 * ntok + 2 * nw :]
+    c, d, t = lax.axis_index("ctx"), lax.axis_index("dp"), lax.axis_index("tp")
+    near = t + 1 - 2 * lax.rem(t, 2)
+    far = lax.rem(t + 2, ntp)
+    length = toks[0].shape[0]
+    part = length // ntp
+
+    barrier = pltpu.get_barrier_semaphore()
+    peers = [{"ctx": lax.rem(c + s, nctx)} for s in range(1, nctx)]
+    peers += [{"dp": lax.rem(d + s, ndp)} for s in range(1, ndp)]
+    peers += [{"tp": near}, {"tp": far}]
+    for peer in peers:
+        pl.semaphore_signal(barrier, inc=1, device_id=peer, device_id_type=MESH)
+    pl.semaphore_wait(barrier, len(peers))
+
+    def rows(a, block, quarter):
+        return tok_outs[a].at[pl.ds(pl.multiple_of(block * length + quarter * part, 16), part), :]
+
+    def hop(a, j, side):
+        block = c - j if side == 0 else c + j
+        to = c + 1 if side == 0 else c - 1
+        valid = (block >= 0) & (to < nctx) if side == 0 else (block < nctx) & (to >= 0)
+        safe = jnp.clip(block, 0, nctx - 1)
+        source = toks[a].at[pl.ds(pl.multiple_of(t * part, 16), part), :] if j == 0 else rows(a, safe, t)
+        copy = remote(source, rows(a, safe, t), z_send.at[a, j, side], z_recv.at[a, safe], {"ctx": jnp.clip(to, 0, nctx - 1)})
+        return valid, copy
+
+    def arrival(j, side):
+        block = c - 1 - j if side == 0 else c + 1 + j
+        valid = block >= 0 if side == 0 else block < nctx
+        return valid, jnp.clip(block, 0, nctx - 1)
+
+    def tp_copy(a, block, kind):
+        quarter = t if kind < 2 else far
+        view = rows(a, block, quarter)
+        return remote(view, view, t_send.at[a, block, kind], t_recv.at[a, block, kind], {"tp": far if kind == 0 else near})
+
+    def tp_arrival(a, block, kind):
+        quarter = far if kind == 0 else (near if kind == 1 else lax.rem(near + 2, ntp))
+        view = rows(a, block, quarter)
+        return remote(view, view, t_send.at[a, block, kind], t_recv.at[a, block, kind], {"tp": near})
+
+    def w_copy(a, s):
+        to = lax.rem(c + s, nctx)
+        return remote(weights[a].at[to], weight_outs[a].at[d, c], w_send.at[a, s], w_recv.at[a, s], {"ctx": to})
+
+    def w_arrival(a, s):
+        view = weight_outs[a].at[d, lax.rem(c - s + nctx, nctx)]
+        return remote(view, view, w_send.at[a, s], w_recv.at[a, s], {"ctx": c})
+
+    def x_copy(a, s, e):
+        block = lax.rem(c - s + nctx, nctx)
+        source = weights[a].at[c] if s == 0 else weight_outs[a].at[d, block]
+        return remote(source, weight_outs[a].at[d, block], x_send.at[a, s, e], x_recv.at[a, s, e], {"dp": lax.rem(d + e, ndp)})
+
+    def x_arrival(a, s, e):
+        view = weight_outs[a].at[lax.rem(d - e + ndp, ndp), lax.rem(c - s + nctx, nctx)]
+        return remote(view, view, x_send.at[a, s, e], x_recv.at[a, s, e], {"dp": d})
+
+    def own_tok(a):
+        return pltpu.make_async_copy(toks[a], tok_outs[a].at[pl.ds(pl.multiple_of(c * length, 16), length), :], own.at[a])
+
+    def own_weight(a):
+        return pltpu.make_async_copy(weights[a].at[c], weight_outs[a].at[d, c], own.at[ntok + a])
+
+    def launch(step):
+        kind, a, j = step
+        if kind == "tok":
+            for side in (0, 1):
+                valid, copy = hop(a, j, side)
+
+                @pl.when(valid)
+                def _():
+                    copy.start()
+        else:
+            w_copy(a, j).start()
+
+    def settle(step):
+        kind, a, j = step
+        if kind == "tok":
+            for side in (0, 1):
+                valid, block = arrival(j, side)
+
+                @pl.when(valid)
+                def _():
+                    view = rows(a, block, t)
+                    remote(view, view, z_send.at[a, j, side], z_recv.at[a, block], {"ctx": c}).wait_recv()
+                    tp_copy(a, block, 0).start()
+                    tp_copy(a, block, 1).start()
+        else:
+            w_arrival(a, j).wait_recv()
+            for e in range(1, ndp):
+                x_copy(a, j, e).start()
+
+    def settle_far(step):
+        kind, a, j = step
+        if kind == "tok":
+            for side in (0, 1):
+                valid, block = arrival(j, side)
+
+                @pl.when(valid)
+                def _():
+                    tp_arrival(a, block, 0).wait_recv()
+                    tp_copy(a, block, 2).start()
+
+    for step in order[:DEPTH]:
+        launch(step)
+    for a in range(nw):
+        own_weight(a).start()
+        for e in range(1, ndp):
+            x_copy(a, 0, e).start()
+    for a in range(ntok):
+        own_tok(a).start()
+    for index, step in enumerate(order):
+        settle(step)
+        if index + DEPTH < len(order):
+            launch(order[index + DEPTH])
+        if index >= 2:
+            settle_far(order[index - 2])
+    for step in order[-2:]:
+        settle_far(step)
+    for kind, a, j in order:
+        if kind == "tok":
+            for side in (0, 1):
+                valid, copy = hop(a, j, side)
+                here, block = arrival(j, side)
+
+                @pl.when(valid)
+                def _():
+                    copy.wait_send()
+
+                @pl.when(here)
+                def _():
+                    for part_kind in range(3):
+                        tp_copy(a, block, part_kind).wait_send()
+                    tp_arrival(a, block, 1).wait_recv()
+                    tp_arrival(a, block, 2).wait_recv()
+        else:
+            w_copy(a, j).wait_send()
+            for e in range(1, ndp):
+                x_copy(a, j, e).wait_send()
+                x_arrival(a, j, e).wait_recv()
+    for a in range(nw):
+        own_weight(a).wait()
+        for e in range(1, ndp):
+            x_copy(a, 0, e).wait_send()
+            x_arrival(a, 0, e).wait_recv()
+    for a in range(ntok):
+        own_tok(a).wait()
+
+
+def gather_all(toks, weights, sizes):
+    nctx, ndp, ntp = sizes
+    turns = range(1, nctx)
+    nw = len(weights)
+    tok = lambda a, j: [("tok", a, j)] if j < nctx - 1 else []
+    per = lambda a: [("w", a, s) for s in turns]
+    order = tok(0, 0) + tok(1, 0) + per(0) + tok(0, 1) + tok(1, 1) + per(1)[:1] + tok(0, 2) + tok(1, 2) + per(1)[1:]
+    any_space = pl.BlockSpec(memory_space=pl.ANY)
+    length, model = toks[0].shape
+    out_shape = [jax.ShapeDtypeStruct((nctx * length, model), BF16) for _ in toks]
+    out_shape += [jax.ShapeDtypeStruct((ndp,) + w.shape, BF16) for w in weights]
+    dma = pltpu.SemaphoreType.DMA
+    return pl.pallas_call(
+        functools.partial(gather_body, order, sizes),
+        out_shape=out_shape,
+        in_specs=[any_space] * (len(toks) + nw),
+        out_specs=[any_space] * len(out_shape),
+        scratch_shapes=[
+            dma((2, nctx, 2)), dma((2, nctx)), dma((2, nctx, 3)), dma((2, nctx, 3)),
+            dma((nw, nctx)), dma((nw, nctx)), dma((nw, nctx, ndp)), dma((nw, nctx, ndp)), dma((2 + nw,)),
+        ],
+        compiler_params=pltpu.CompilerParams(collective_id=1, has_side_effects=True),
+        name="gather_inputs",
+    )(*toks, *weights)
+
+
+def add_rows(target, sources, rows, step):
+    def some(index, _):
+        here = pl.ds(pl.multiple_of(index * step, step), step)
+        total = sources[0][here, :].astype(F32)
+        for source in sources[1:]:
+            total = total + source[here, :].astype(F32)
+        target[here, :] = total.astype(target.dtype)
+        return 0
+
+    lax.fori_loop(0, rows // step, some, 0)
+
+
+def output_body(order, sizes, *refs):
+    nctx, ndp, ntp = sizes
+    nw = (len(refs) - 23) // 4
+    partial, grads = refs[0], refs[1 : 1 + nw]
+    sum_out, grad_outs = refs[1 + nw], refs[2 + nw : 2 + 2 * nw]
+    (near_in, far_out, far_in, z_out, z_in, held, acc, done) = refs[2 + 2 * nw : 10 + 2 * nw]
+    x_ins = refs[10 + 2 * nw : 10 + 3 * nw]
+    x_sums = refs[10 + 3 * nw : 10 + 4 * nw]
+    (near_s, near_r, far_s, far_r, z_s, z_r, x_s, x_r, w_s, w_r, fin_s, fin_r, local) = refs[10 + 4 * nw :]
+    c, d, t = lax.axis_index("ctx"), lax.axis_index("dp"), lax.axis_index("tp")
+    near = t + 1 - 2 * lax.rem(t, 2)
+    far = lax.rem(t + 2, ntp)
+    far_near = lax.rem(near + 2, ntp)
+    length = sum_out.shape[0]
+    part = length // ntp
+    wrap = lambda i: lax.rem(i + nctx, nctx)
+
+    barrier = pltpu.get_barrier_semaphore()
+    peers = [{"ctx": lax.rem(c + s, nctx)} for s in range(1, nctx)]
+    peers += [{"dp": lax.rem(d + e, ndp)} for e in range(1, ndp)]
+    peers += [{"tp": near}, {"tp": far}]
+    for peer in peers:
+        pl.semaphore_signal(barrier, inc=1, device_id=peer, device_id_type=MESH)
+    pl.semaphore_wait(barrier, len(peers))
+
+    def rows(s, quarter):
+        return partial.at[pl.ds(pl.multiple_of(wrap(c + s) * length + quarter * part, 16), part), :]
+
+    def near_copy(s, slot):
+        return remote(rows(s, near if slot == 0 else far_near), near_in.at[s, slot], near_s.at[s, slot], near_r.at[s, slot], {"tp": near})
+
+    def far_copy(s):
+        return remote(far_out.at[s], far_in.at[s], far_s.at[s], far_r.at[s], {"tp": far})
+
+    def z_copy(s):
+        return remote(z_out.at[s], z_in.at[s], z_s.at[s], z_r.at[s], {"ctx": wrap(c + s)})
+
+    def x_copy(a, s, e):
+        to = lax.rem(d + e, ndp)
+        return remote(grads[a].at[to, wrap(c + s)], x_ins[a].at[s, e - 1], x_s.at[a, s, e], x_r.at[a, s, e], {"dp": to})
+
+    def w_copy(a, s):
+        return remote(x_sums[a].at[s], grad_outs[a].at[c], w_s.at[a, s], w_r.at[a, s], {"ctx": wrap(c + s)})
+
+    def w_arrival(a, s):
+        view = grad_outs[a].at[wrap(c - s)]
+        return remote(view, view, w_s.at[a, s], w_r.at[a, s], {"ctx": c})
+
+    def load(s, quarter, slot):
+        return pltpu.make_async_copy(rows(s, quarter), held.at[slot], local.at[slot])
+
+    def load_grad(a, s):
+        return pltpu.make_async_copy(grads[a].at[d, wrap(c + s)], x_sums[a].at[s], local.at[2 + a * nctx + s])
+
+    def start_x(s):
+        for a in range(nw):
+            for e in range(1, ndp):
+                x_copy(a, s, e).start()
+
+    def near_sum(s):
+        load(s, far, 0).start()
+        near_copy(s, 1).wait_recv()
+        load(s, far, 0).wait()
+        add_rows(far_out.at[s], [held.at[0], near_in.at[s, 1]], part, 16)
+        far_copy(s).start()
+
+    def far_sum(s):
+        load(s, t, 1).start()
+        near_copy(s, 0).wait_recv()
+        far_copy(s).wait_recv()
+        load(s, t, 1).wait()
+        add_rows(acc if s == 0 else z_out.at[s], [held.at[1], near_in.at[s, 0], far_in.at[s]], part, 16)
+        if s > 0:
+            z_copy(s).start()
+
+    def grad_sum(s):
+        for a in range(nw):
+            load_grad(a, s).wait()
+            for e in range(1, ndp):
+                x_copy(a, s, e).wait_recv()
+            add_rows(x_sums[a].at[s], [x_sums[a].at[s]] + [x_ins[a].at[s, e - 1] for e in range(1, ndp)], x_sums[a].shape[1], 16)
+            if s > 0:
+                w_copy(a, s).start()
+            else:
+                pltpu.make_async_copy(x_sums[a].at[0], grad_outs[a].at[c], local.at[2 + nw * nctx + a]).start()
+
+    for s in order:
+        for slot in (1, 0):
+            near_copy(s, slot).start()
+        for a in range(nw):
+            load_grad(a, s).start()
+    ahead = 2
+    for s in order[:ahead]:
+        start_x(s)
+    for s in order[:ahead]:
+        near_sum(s)
+    for index, s in enumerate(order):
+        far_sum(s)
+        if index + ahead < nctx:
+            near_sum(order[index + ahead])
+        grad_sum(s)
+        if index + ahead < nctx:
+            start_x(order[index + ahead])
+    for s in range(1, nctx):
+        z_copy(s).wait_recv()
+    add_rows(done, [acc] + [z_in.at[s] for s in range(1, nctx)], part, 16)
+
+    def mine(quarter):
+        return sum_out.at[pl.ds(pl.multiple_of(quarter * part, 16), part), :]
+
+    finals = [
+        remote(done, mine(t), fin_s.at[0], fin_r.at[0], {"tp": far}),
+        remote(done, mine(t), fin_s.at[1], fin_r.at[1], {"tp": near}),
+        remote(mine(far), mine(far), fin_s.at[2], fin_r.at[2], {"tp": near}),
+    ]
+    keep = pltpu.make_async_copy(done, mine(t), local.at[0])
+    finals[0].start()
+    finals[1].start()
+    keep.start()
+    remote(mine(far), mine(far), fin_s.at[0], fin_r.at[0], {"tp": far}).wait_recv()
+    finals[2].start()
+    remote(mine(near), mine(near), fin_s.at[1], fin_r.at[1], {"tp": near}).wait_recv()
+    remote(mine(far_near), mine(far_near), fin_s.at[2], fin_r.at[2], {"tp": near}).wait_recv()
+    keep.wait()
+    for copy in finals:
+        copy.wait_send()
+    for s in order:
+        for slot in (1, 0):
+            near_copy(s, slot).wait_send()
+        far_copy(s).wait_send()
+        for a in range(nw):
+            for e in range(1, ndp):
+                x_copy(a, s, e).wait_send()
+            if s > 0:
+                w_copy(a, s).wait_send()
+                w_arrival(a, s).wait_recv()
+            else:
+                pltpu.make_async_copy(x_sums[a].at[0], grad_outs[a].at[c], local.at[2 + nw * nctx + a]).wait()
+        if s > 0:
+            z_copy(s).wait_send()
+
+
+def return_all(partial, grads, sizes):
+    nctx, ndp, ntp = sizes
+    length = partial.shape[0] // nctx
+    part, model = length // ntp, partial.shape[1]
+    nw = len(grads)
+    order = [nctx // 2] + [s for s in range(1, nctx) if s != nctx // 2] + [0]
+    any_space = pl.BlockSpec(memory_space=pl.ANY)
+    dma = pltpu.SemaphoreType.DMA
+    vmem = pltpu.VMEM
+    strip = lambda *lead: vmem(lead + (part, model), BF16)
+    return pl.pallas_call(
+        functools.partial(output_body, order, sizes),
+        out_shape=[jax.ShapeDtypeStruct((length, model), BF16)] + [jax.ShapeDtypeStruct(g.shape[1:], BF16) for g in grads],
+        in_specs=[any_space] * (1 + nw),
+        out_specs=[any_space] * (1 + nw),
+        scratch_shapes=[
+            strip(nctx, 2), strip(nctx), strip(nctx), strip(nctx), strip(nctx), strip(2), vmem((part, model), F32), strip(),
+        ]
+        + [vmem((nctx, max(ndp - 1, 1)) + g.shape[2:], BF16) for g in grads]
+        + [vmem((nctx,) + g.shape[2:], BF16) for g in grads]
+        + [
+            dma((nctx, 2)), dma((nctx, 2)), dma((nctx,)), dma((nctx,)), dma((nctx,)), dma((nctx,)),
+            dma((nw, nctx, ndp)), dma((nw, nctx, ndp)), dma((nw, nctx)), dma((nw, nctx)), dma((3,)), dma((3,)),
+            dma((2 + nw * nctx + nw,)),
+        ],
+        compiler_params=pltpu.CompilerParams(collective_id=2, has_side_effects=True, vmem_limit_bytes=60 << 20),
+        name="return_outputs",
+    )(partial, *grads)
+
+
+def small_body(sizes, value, gathered, send, recv, own):
+    nctx, ndp = sizes
+    c, d = lax.axis_index("ctx"), lax.axis_index("dp")
+    others = [(e, s) for e in range(ndp) for s in range(nctx) if e or s]
+    place = lambda e, s: {"dp": lax.rem(d + e, ndp), "ctx": lax.rem(c + s, nctx)}
+    barrier = pltpu.get_barrier_semaphore()
+    for e, s in others:
+        pl.semaphore_signal(barrier, inc=1, device_id=place(e, s), device_id_type=MESH)
+    pl.semaphore_wait(barrier, len(others))
+    keep = pltpu.make_async_copy(value, gathered.at[d, c], own)
+    keep.start()
+    for e, s in others:
+        remote(value, gathered.at[d, c], send.at[e, s], recv.at[e, s], place(e, s)).start()
+    for e, s in others:
+        view = gathered.at[lax.rem(d - e + ndp, ndp), lax.rem(c - s + nctx, nctx)]
+        remote(view, view, send.at[e, s], recv.at[e, s], place(e, s)).wait_recv()
+        remote(value, gathered.at[d, c], send.at[e, s], recv.at[e, s], place(e, s)).wait_send()
+    keep.wait()
+
+
+def gather_small(value, sizes):
+    nctx, ndp = sizes
+    vmem = pl.BlockSpec(memory_space=pltpu.VMEM)
+    dma = pltpu.SemaphoreType.DMA
+    return pl.pallas_call(
+        functools.partial(small_body, sizes),
+        out_shape=jax.ShapeDtypeStruct((ndp, nctx) + value.shape, F32),
+        in_specs=[vmem],
+        out_specs=vmem,
+        scratch_shapes=[dma((ndp, nctx)), dma((ndp, nctx)), dma],
+        compiler_params=pltpu.CompilerParams(collective_id=3, has_side_effects=True),
+        name="gather_small",
+    )(value)
 
 
 def dot_last(left_side, right_side):
@@ -362,35 +849,6 @@
 
 def dot_first(left_side, right_side):
     return lax.dot_general(left_side, right_side, (((0,), (0,)), ((), ())), preferred_element_type=F32)
-
-
-def conv_silu(padded, kernel):
-    tap_count = kernel.shape[0] - 1
-    length = padded.shape[0] - tap_count + 1
-    running = kernel[tap_count] + kernel[0] * padded[0:length]
-    for offset in range(1, tap_count):
-        running = running + kernel[offset] * padded[offset : offset + length]
-    return jax.nn.silu(running)
-
-
-def spread_rows(value):
-    part = value.shape[0] // lax.axis_size("tp")
-    mine = lax.dynamic_slice_in_dim(value, lax.axis_index("tp") * part, part, 0)
-    along = lax.all_gather(mine, "ctx", axis=0)
-    return lax.all_gather(along, "tp", axis=1).reshape(-1, value.shape[1])
-
-
-def fetch_weight(packed):
-    mine = lax.all_to_all(packed, "ctx", 0, 0, tiled=True)
-    return lax.all_gather(mine.reshape(-1, packed.shape[2]), "dp", axis=0, tiled=True)
-
-
-def return_grad(grad, rows):
-    ndp, nctx = lax.axis_size("dp"), lax.axis_size("ctx")
-    parts = grad.astype(BF16).reshape(ndp, nctx * rows, grad.shape[1])
-    summed = jnp.sum(lax.all_to_all(parts, "dp", 0, 0, tiled=True).astype(F32), axis=0)
-    back = lax.all_to_all(summed.astype(BF16).reshape(nctx, rows, grad.shape[1]), "ctx", 0, 0, tiled=True)
-    return back.astype(F32)
 
 
 def sum_rows(partial):
@@ -424,63 +882,52 @@
     normed = (hidden * rscale * norm_gain).astype(BF16)
 
     zx = zx_weight.reshape(rows, 2, nctx, width)
-    bc = jnp.repeat(bc_weight.reshape(rows, 2, groups, N), share, axis=2)
-    packed = jnp.concatenate(
-        [zx[:, 0], zx[:, 1], bc[:, 0], bc[:, 1], dt_weight.reshape(rows, nctx, heads)], axis=2
-    ).transpose(1, 0, 2)
-    weight_in = fetch_weight(packed)
-    weight_out = fetch_weight(out_weight.reshape(rows, nctx, width).transpose(1, 0, 2))
-    normed_all = spread_rows(normed)
-    cot_all = spread_rows(cot)
-
-    conv_width = width + 2 * N
+    maps = bc_weight.reshape(rows, 2, groups, N).transpose(0, 2, 1, 3)
+    own = maps.reshape(rows, nctx, N)
+    other = maps[:, :, ::-1].reshape(rows, nctx, N)
+    steps = jnp.pad(dt_weight.reshape(rows, nctx, heads), ((0, 0), (0, 0), (0, N - heads)))
+    packed_in = jnp.concatenate([zx[:, 0], zx[:, 1], own, steps, other], axis=2).transpose(1, 0, 2)
+    packed_out = out_weight.reshape(rows, nctx, width).transpose(1, 0, 2)
+    normed_all, cot_all, weight_in, weight_out = gather_all((normed, cot), (packed_in, packed_out), (nctx, ndp, ntp))
+    weight_in = weight_in.reshape(model_width, -1)
+    weight_out = weight_out.reshape(model_width, width)
+
     grad_gated = jnp.dot(cot_all, weight_out, preferred_element_type=F32)
-    gate_pre = jnp.dot(normed_all, weight_in[:, :width], preferred_element_type=F32)
-    conv_input = jnp.dot(normed_all, weight_in[:, width : width + conv_width], preferred_element_type=F32).astype(BF16)
-    raw_dt = jnp.dot(normed_all, weight_in[:, width + conv_width :], preferred_element_type=F32)
+    proj = jnp.dot(normed_all, weight_in, preferred_element_type=F32)
+    odd = lax.rem(ctx, 2)
     kernel_x = mine(conv_x.reshape(taps + 1, nctx, width).transpose(1, 0, 2))
-    kernel_bc = conv_bc.reshape(taps + 1, 2, groups, N)
-    kernel_bc = lax.dynamic_index_in_dim(kernel_bc, ctx // share, 2, False)
-    kernel = jnp.concatenate([kernel_x, kernel_bc.reshape(taps + 1, 2 * N)], axis=1)
+    kernel_maps = conv_bc.reshape(taps + 1, 2, groups, N).transpose(2, 1, 0, 3).reshape(nctx, taps + 1, N)
+    kernel_own = mine(kernel_maps)
+    kernel_other = lax.dynamic_index_in_dim(kernel_maps, ctx + 1 - 2 * odd, 0, False)
+    kernel = jnp.concatenate([kernel_x, kernel_own, kernel_other], axis=1)
+    odd = odd.astype(jnp.int32).reshape(1, 1)
     heads_mine = mine(head_params.reshape(3, nctx, heads).transpose(1, 0, 2))
     gain = mine(gate_gain.reshape(nctx, 1, width))
-    low, ssd, states, sums = mixer_forward(conv_input, raw_dt, gate_pre, grad_gated, kernel, heads_mine, gain)
+    low, ssd, states, sums = mixer_forward(odd, proj, grad_gated, kernel, heads_mine, gain)
     sums = (sums + partner(sums)) / group_width
     inverse = lax.rsqrt(sums[0] + EPS)
     norms = jnp.stack([inverse, inverse * inverse * inverse * sums[1]], axis=1)
+    gate_pre = proj[:, :width]
     gated_norm = (ssd * (gate_pre * jax.nn.sigmoid(gate_pre)) * norms[:, 0:1] * gain).astype(BF16)
     branch = sum_rows(dot_last(gated_norm, weight_out))
     part = length // ntp
     hidden_part = lax.dynamic_slice_in_dim(hidden, lax.axis_index("tp") * part, part, 0)
     mixed = lax.all_gather((hidden_part + branch).astype(BF16), "tp", axis=0, tiled=True)
-    grad_out = return_grad(dot_first(cot_all, gated_norm), rows)
-    grad_gate, grad_x, grad_maps, grad_dt, grad_kernel_x, grad_heads, gate_gain_grad = mixer_backward(
-        conv_input, low, raw_dt, gate_pre, grad_gated, ssd, states, norms, kernel, heads_mine, gain
+    grad_zx, grad_steps, grad_own, grad_other, grad_kernel_x, grad_heads, gate_gain_grad = mixer_backward(
+        odd, proj, low, grad_gated, ssd, states, norms, kernel, heads_mine, gain
     )
-
-    odd = ctx % 2
-    own_maps = lax.dynamic_slice_in_dim(grad_maps, odd * N, N, 1)
-    send_maps = lax.dynamic_slice_in_dim(grad_maps, (1 - odd) * N, N, 1)
-    own_maps = own_maps + partner(send_maps)
-    own_input = lax.dynamic_slice_in_dim(conv_input, width + odd * N, N, 1)
-    own_padded = jnp.concatenate([jnp.zeros((taps - 1, N), BF16), own_input], axis=0).astype(F32)
-    own_kernel = lax.dynamic_slice_in_dim(kernel, width + odd * N, N, 1)
-    _, conv_back = jax.vjp(conv_silu, own_padded, own_kernel)
-    grad_padded, grad_kernel_bc = conv_back(own_maps)
-    grad_kernel = jnp.concatenate([grad_kernel_x, grad_kernel_bc], axis=1)
-    grad_bc = grad_padded[taps - 1 :].astype(BF16)
-    grad_all = jnp.concatenate([grad_gate, grad_x, grad_bc, grad_dt.astype(BF16)], axis=1)
-    own_weight = jnp.concatenate(
-        [
-            weight_in[:, : 2 * width],
-            lax.dynamic_slice_in_dim(weight_in, 2 * width + odd * N, N, 1),
-            weight_in[:, 2 * width + 2 * N :],
-        ],
-        axis=1,
+    theirs = partner(grad_other)
+    grad_rest, grad_kernel_own = map_backward(proj, grad_own, theirs, grad_steps, kernel_own, 2 * width)
+    grad_all = jnp.concatenate([grad_zx, grad_rest], axis=1)
+    blocks = lambda grad: grad.astype(BF16).reshape(ndp, nctx, rows, -1)
+    weight_grads = (
+        blocks(dot_first(normed_all, grad_zx)),
+        blocks(dot_first(normed_all, grad_rest)),
+        blocks(dot_first(cot_all, gated_norm)),
     )
-    normed_part = sum_rows(dot_last(grad_all, own_weight))
-    grad_normed = lax.all_gather(normed_part.astype(BF16), "tp", axis=0, tiled=True).astype(F32)
-    grad_in = return_grad(dot_first(normed_all, grad_all), rows)
+    partial = dot_last(grad_all, weight_in[:, : grad_all.shape[1]]).astype(BF16)
+    grad_normed, back_zx, back_rest, back_out = return_all(partial, weight_grads, (nctx, ndp, ntp))
+    grad_normed = grad_normed.astype(F32)
 
     grad_hat = grad_normed * norm_gain
     norm_gain_grad = jnp.sum(grad_normed * hidden * rscale, axis=0)
@@ -489,24 +936,26 @@
     )
     tokens_grad = cot.astype(F32) + grad_hidden
 
-    zx_weight_grad = jnp.stack([grad_in[:, :, :width], grad_in[:, :, width : 2 * width]], axis=2)
-    zx_weight_grad = zx_weight_grad.transpose(1, 2, 0, 3).reshape(rows, 2, inner)
-    bc_weight_grad = grad_in[:, :, 2 * width : 2 * width + N].reshape(groups, 2, rows, N)
-    bc_weight_grad = bc_weight_grad.transpose(2, 1, 0, 3).reshape(rows, 2, groups * N)
-    dt_weight_grad = grad_in[:, :, 2 * width + N :].transpose(1, 0, 2).reshape(rows, nctx * heads)
-    out_weight_grad = grad_out.transpose(1, 0, 2).reshape(rows, inner)
-
-    small = jnp.concatenate([grad_kernel.reshape(-1), grad_heads.reshape(-1), gate_gain_grad.reshape(-1)])
-    table = lax.dynamic_update_slice(jnp.zeros((nctx, small.shape[0]), F32), small[None], (ctx, 0))
-    table, norm_gain_grad = lax.psum((table, norm_gain_grad), ("dp", "ctx"))
-    kernel_end = (taps + 1) * (width + N)
-    heads_end = kernel_end + 3 * heads
-    kernels = table[:, :kernel_end].reshape(nctx, taps + 1, width + N)
-    conv_x_grad = kernels[:, :, :width].transpose(1, 0, 2).reshape(taps + 1, inner)
-    conv_bc_grad = kernels[:, :, width:].reshape(groups, 2, taps + 1, N).transpose(2, 1, 0, 3)
-    conv_bc_grad = conv_bc_grad.reshape(taps + 1, 2, groups * N)
-    head_grad = table[:, kernel_end:heads_end].reshape(nctx, 3, heads).transpose(1, 0, 2).reshape(3, nctx * heads)
-    gate_gain_grad = table[:, heads_end:].reshape(inner)
+    zx_weight_grad = back_zx.astype(F32).reshape(nctx, rows, 2, width).transpose(1, 2, 0, 3).reshape(rows, 2, inner)
+    back_rest = back_rest.astype(F32)
+    bc_weight_grad = back_rest[:, :, :N].reshape(groups, 2, rows, N).transpose(2, 1, 0, 3).reshape(rows, 2, groups * N)
+    dt_weight_grad = back_rest[:, :, N : N + heads].transpose(1, 0, 2).reshape(rows, nctx * heads)
+    out_weight_grad = back_out.astype(F32).transpose(1, 0, 2).reshape(rows, inner)
+
+    pieces = (grad_kernel_x, grad_kernel_own, grad_heads, gate_gain_grad, norm_gain_grad)
+    small = jnp.concatenate([piece.reshape(-1) for piece in pieces])
+    lines = -(-small.shape[0] // (8 * N)) * 8
+    small = jnp.pad(small, (0, lines * N - small.shape[0])).reshape(lines, N)
+    table = jnp.sum(gather_small(small, (nctx, ndp)), axis=0).reshape(nctx, lines * N)
+    ends = [0]
+    for piece in pieces:
+        ends.append(ends[-1] + piece.size)
+    kernel_x, kernel_own, head_grad, gain_grad, norm_grad = [table[:, a:b] for a, b in zip(ends[:-1], ends[1:])]
+    conv_x_grad = kernel_x.reshape(nctx, taps + 1, width).transpose(1, 0, 2).reshape(taps + 1, inner)
+    conv_bc_grad = kernel_own.reshape(groups, 2, taps + 1, N).transpose(2, 1, 0, 3).reshape(taps + 1, 2, groups * N)
+    head_grad = head_grad.reshape(nctx, 3, heads).transpose(1, 0, 2).reshape(3, nctx * heads)
+    gate_gain_grad = gain_grad.reshape(inner)
+    norm_gain_grad = jnp.sum(norm_grad, axis=0)
     return (
         mixed.reshape(tokens.shape),
         tokens_grad.reshape(tokens.shape),

time: 1410 us -> 1080 us (0.77)
  waiting for transfers between devices: 927 us -> 103 us
  Pallas kernels: 71.3 us -> 690 us
  blocking collectives: 52.3 us -> 0 us
  starting transfers between devices: 35.2 us -> 1.17 us
  other arithmetic: 67.2 us -> 42.1 us
    pallas_call x2 -> x6, Pallas kernels: 71.3 us -> 690 us  [the longest x1 321 us: gather_all(): pl.pallas_call(functools.partial(gather_body, order, sizes), out_shape=ou...]
    all_to_all x5 -> x0, waiting for transfers between devices: 491 us -> none  [the longest x1 231 us: fetch_weight(): mine = lax.all_to_all(packed, 'ctx', 0, 0, tiled=True)]
    all_gather x7 -> x0, waiting for transfers between devices: 303 us -> none  [the longest x2 215 us: spread_rows(): return lax.all_gather(along, 'tp', axis=1).reshape(-1, value.shape[1])]
    reduce_scatter x2 -> x1, waiting for transfers between devices: 0.03 us -> 69.1 us  [sum_rows(): lax.psum_scatter(partial.astype(BF16), ('ctx', 'tp'), scatter_dimension=0...]
    psum x1 -> x0, waiting for transfers between devices: 59.9 us -> none  [shards(): table, norm_gain_grad = lax.psum((table, norm_gain_grad), ('dp', 'ctx'))]
    all_to_all x1 -> x0, blocking collectives: 52.3 us -> none  [fetch_weight(): mine = lax.all_to_all(packed, 'ctx', 0, 0, tiled=True)]
    ppermute x2, waiting for transfers between devices: 71 us -> 34.2 us  [partner(): return lax.ppermute(value, 'ctx', [(i, i ^ 1) for i in range(nctx)])]
    all_to_all x5 -> x0, starting transfers between devices: 31 us -> none  [the longest x2 14.4 us: return_grad(): lax.all_to_all(parts, 'dp', 0, 0, tiled=True).astype(F32)]
  transfers between devices with their start and end apart: 18 -> 4, of which waited for: 12 -> 3; matrix products, arithmetic and copies ran while one was open for 16% -> 14% of each run, Pallas kernels for 3% -> 32%
where the time goes in v3:
time: 1080 us
  Pallas kernels  690 us (64%)
  matrix products  134 us (12%)
  waiting for transfers between devices  103 us (10%)
  local copies, waits for them, and re-layouts  90 us (8%)
  other arithmetic  42.1 us (4%)
  between operations  15 us (1%)
    pallas_call x1, Pallas kernels, gather_all(): pl.pallas_call(functools.partial(gather_body, order, sizes), out_shape=ou...  321 us
    pallas_call x1, Pallas kernels, return_all(): pl.pallas_call(functools.partial(output_body, order, sizes), out_shape=[j...  271 us
    reduce_scatter x1, waiting for transfers between devices, sum_rows(): lax.psum_scatter(partial.astype(BF16), ('ctx', 'tp'), scatter_dimension=0...  69.1 us
    dot_general x3, matrix products, dot_first(): lax.dot_general(left_side, right_side, (((0,), (0,)), ((), ())), preferre...  48.4 us
    pallas_call x1, Pallas kernels, mixer_backward(): pl.pallas_call(backward_body, grid=(count,), in_specs=specs[:3] + [specs[...  44.8 us
    unnamed x72, local copies, waits for them, and re-layouts  41.6 us
    dot_general x2, matrix products, dot_last(): lax.dot_general(left_side, right_side, (((1,), (1,)), ((), ())), preferre...  41.2 us
    ppermute x2, waiting for transfers between devices, partner(): return lax.ppermute(value, 'ctx', [(i, i ^ 1) for i in range(nctx)])  34.2 us
  transfers between devices with their start and end apart: 4, of which 3 were waited for; matrix products, arithmetic and copies ran while one was open for 14% of the time, Pallas kernels for 32%

profile of v3, /device:TPU:0, one launch (start us, length us, event | category | flops | bytes accessed | tf_op | source)
XLA Modules:
  0.0 1075.6 jit_solution(5413137053573894892)
XLA Ops:
  8.0 11.1 %copy.71 = bf16[512,2,2048]{0,2,1:T(8,128)(2,1)} copy(bf16[512,2,2048]{2,1,0:T(2,128)(2,1)} %param.13) | data formatting | bytes 8388608 | tf_op args[2]
  52.8 320.9 %gather_inputs.1 = (bf16[2048,4096]{1,0:T(8,128)(2,1)}, bf16[2048,4096]{1,0:T(8,128)(2,1)}, bf16[2,4,512,1408]{3,2,1,0:T(8,128)(2,1)}, bf16[2,4,512,512]{3,2,1,0:T(8,128)(2,1)}) custom-call(bf16[512,4096]{1,0:T(8,128)(2,1)} %fusion.11.refs_0_, bf16[512,4096]{1,0:T(8,128)(2,1)} %bitcast.115, bf16[4,512,1408]{2,1,0:T(8,128)(2,1)} %bitcast.116, ...), custom_call_target="tpu_custom_call" | custom-call | tf_op jit(solution)/shard_map/gather_inputs/pallas_call | solution.py:613
  373.8 33.9 %fusion.22.gate_ref.x_ref.own_ref.step_ref.other_ref.edge_ref = f32[2048,1408]{1,0:T(8,128)} fusion(bf16[2048,4096]{1,0:T(8,128)(2,1)} %get-tuple-element.32, bf16[4096,1408]{1,0:T(8,128)(2,1)} %bitcast.149), kind=kOutput, calls=%fused_computation.60 | convolution fusion | flops 23622320128 | bytes 39845888 | tf_op jit(solution)/shard_map/dot_general | solution.py:896
  407.7 10.8 %fusion.23.up_ref = f32[2048,512]{1,0:T(8,128)} fusion(bf16[2048,4096]{1,0:T(8,128)(2,1)S(1)} %copy-done.26, bf16[4096,512]{1,0:T(8,128)(2,1)S(1)} %bitcast.151), kind=kOutput, calls=%fused_computation.61 | convolution fusion | flops 8589934592 | bytes 25165824 | tf_op jit(solution)/shard_map/dot_general | solution.py:895
  418.5 28.0 %mixer_forward.1 = (bf16[2048,768]{1,0:T(8,128)(2,1)S(1)}, f32[2048,512]{1,0:T(8,128)}, f32[8,128,512]{2,1,0:T(8,128)S(1)}, f32[2,2048]{1,0:T(2,128)S(1)}) custom-call(s32[1,1]{1,0:T(1,128)} %bitcast.1.odd_ref, f32[2048,1408]{1,0:T(8,128)} %fusion.22.gate_ref.x_ref.own_ref.step_ref.other_ref.edge_ref, ...), custom_call_target="tpu_custom_call" | custom-call | tf_op jit(solution)/shard_map/mixer_forward/pallas_call | solution.py:184
  457.6 11.7 %convolution_convert_fusion = bf16[2048,4096]{1,0:T(8,128)(2,1)} fusion(bf16[2048,512]{1,0:T(8,128)(2,1)S(1)} %multiply_convert_fusion, bf16[4096,512]{1,0:T(8,128)(2,1)S(1)} %bitcast.152), kind=kOutput, calls=%fused_computation | convolution fusion | flops 8598323200 | bytes 23068672 | tf_op jit(solution)/shard_map/dot_general | solution.py:847
  469.4 7.1 convert_element_type.45
  477.9 44.8 %mixer_backward.1 = (bf16[2048,1024]{1,0:T(8,128)(2,1)}, bf16[2048,128]{1,0:T(8,128)(2,1)}, f32[2048,128]{1,0:T(8,128)}, f32[2048,128]{1,0:T(8,128)}, f32[5,512]...) custom-call(s32[1,1]{1,0:T(1,128)} %bitcast.1.odd_ref, ...), custom_call_target="tpu_custom_call" | custom-call | tf_op jit(solution)/shard_map/mixer_backward/pallas_call | solution.py:345
  523.3 24.1 %convolution_convert_fusion.2 = bf16[4096,1024]{1,0:T(8,128)(2,1)} fusion(bf16[2048,4096]{1,0:T(8,128)(2,1)} %get-tuple-element.32, bf16[2048,1024]{1,0:T(8,128)(2,1)} %get-tuple-element.40), kind=kOutput, calls=%fused_computation.20 | convolution fusion | flops 17184063488 | bytes 29360128 | tf_op jit(solution)/shard_map/dot_general | solution.py:851
  547.4 14.3 %convolution_convert_fusion.3 = bf16[4096,512]{1,0:T(8,128)(2,1)} fusion(bf16[2048,4096]{1,0:T(8,128)(2,1)} %get-tuple-element.34, bf16[2048,512]{1,0:T(8,128)(2,1)S(1)} %multiply_convert_fusion), kind=kOutput, calls=%fused_computation.21 | convolution fusion | flops 8592031744 | bytes 23068672 | tf_op jit(solution)/shard_map/dot_general | solution.py:851
  561.8 31.1 %collective-permute-done.1.theirs_ref = f32[2048,128]{1,0:T(8,128)S(1)} collective-permute-done((f32[2048,128]{1,0:T(8,128)}, f32[2048,128]{1,0:T(8,128)S(1)}, u32[]{:S(2)}, u32[]{:S(2)}) %collective-permute-start.1) | collective-permute-done | bytes 1048608 | tf_op jit(solution)/shard_map/ppermute | solution.py:877
  593.8 6.6 map_backward.1
  600.4 69.1 %reduce-scatter.2.cloned.1.call-done = bf16[128,4096]{1,0:T(8,128)(2,1)} async-done(((bf16[2048,4096]{1,0:T(8,128)(2,1)}), bf16[128,4096]{1,0:T(8,128)(2,1)}) %reduce-scatter.2.cloned.1.call-update) | async-done | bytes 1048592 | tf_op jit(solution)/shard_map/reduce_scatter | solution.py:855
  672.6 29.5 %convolution_convert_fusion.1.refs_0_ = bf16[2048,4096]{1,0:T(8,128)(2,1)} fusion(bf16[4096,1408]{1,0:T(8,128)(2,1)} %bitcast.150, bf16[2048,256]{1,0:T(8,128)(2,1)} %get-tuple-element.44, bf16[2048,1024]{1,0:T(8,128)(2,1)} %get-tuple-element.40), kind=kOutput, calls=%fused_computation.1 | convolution fusion | flops 21493710848 | bytes 32505856 | tf_op jit(solution)/shard_map/dot_general | solution.py:847
  702.1 10.1 convolution_convert_fusion.4
  712.2 270.8 %return_outputs.1 = (bf16[512,4096]{1,0:T(8,128)(2,1)}, bf16[4,512,1024]{2,1,0:T(8,128)(2,1)}, bf16[4,512,256]{2,1,0:T(8,128)(2,1)}, bf16[4,512,512]{2,1,0:T(8,128)(2,1)}) custom-call(bf16[2048,4096]{1,0:T(8,128)(2,1)} %convolution_convert_fusion.1.refs_0_, bf16[2,4,512,1024]{3,2,1,0:T(8,128)(2,1)} %bitcast.119, bf16[2,4,512,256]{3,2,1,0:T(8,128)(2,1)} %bitcast.127, ...), custom_call_target="tpu_custom_call" | custom-call | tf_op jit(solution)/shard_map/return_outputs/pallas_call | solution.py:791
  983.0 7.5 fusion.8
  991.2 18.5 %gather_small.1 = f32[2,4,64,128]{3,2,1,0:T(8,128)} custom-call(f32[64,128]{1,0:T(8,128)} %pad_bitcast_fusion.value), custom_call_target="tpu_custom_call" | custom-call | tf_op jit(solution)/shard_map/gather_small/pallas_call | solution.py:835
  1012.0 11.5 %reshape.263 = f32[4,512,2,512]{3,2,1,0:T(2,128)} reshape(bf16[4,512,1024]{2,1,0:T(8,128)(2,1)} %get-tuple-element.50) | data formatting | bytes 12582912 | tf_op jit(solution)/shard_map/reshape | solution.py:939
  1023.5 8.5 copy.91
  1034.6 5.2 copy.86
  1039.8 5.7 copy.87
  1055.2 8.4 fusion.5
  1063.6 4.7 copy.106
  (126 shorter events, 66.8 us)
Async XLA Ops:
  7.2 36.8 %copy-start = (f32[5,2048]{1,0:T(8,128)S(1)}, f32[5,2048]{1,0:T(8,128)}, u32[]{:S(2)}) copy-start(f32[5,2048]{1,0:T(8,128)} %param.16) | copy-start | bytes 122884
  7.2 662.3 %reduce-scatter.2.cloned.1.call-start = ((), (), s32[]{:S(2)}) async-start(), calls=%async_computation.1 | async-start | bytes 17825792 | tf_op jit(solution)/shard_map/reduce_scatter | solution.py:855
  32.2 11.7 %copy-start.24 = (f32[2048]{0:T(1024)S(1)}, f32[2048]{0:T(1024)}, u32[]{:S(2)}) copy-start(f32[2048]{0:T(1024)} %param.19) | copy-start | bytes 24580
  32.2 11.7 %copy-start.25 = (f32[3,32]{1,0:T(4,128)S(1)}, f32[3,32]{1,0:T(4,128)}, u32[]{:S(2)}) copy-start(f32[3,32]{1,0:T(4,128)} %param.18) | copy-start | bytes 1156
  35.9 13.3 %copy-start.17 = (f32[512]{0:T(512)}, f32[512]{0:T(512)S(1)}, u32[]{:S(2)}) copy-start(f32[512]{0:T(512)S(1)} %get-tuple-element.97) | copy-start | bytes 6148
  39.8 9.4 copy-start.13
  44.0 374.5 %copy-start.6 = (f32[1,512]{1,0:T(1,128)}, f32[1,512]{1,0:T(1,128)S(1)}, u32[]{:S(2)}) copy-start(f32[1,512]{1,0:T(1,128)S(1)} %fusion.36.gain_ref) | copy-start | bytes 6148
  44.1 374.4 %copy-start.5 = (f32[3,1,8]{2,0,1:T(4,128)}, f32[3,1,8]{2,0,1:T(4,128)S(1)}, u32[]{:S(2)}) copy-start(f32[3,1,8]{2,0,1:T(4,128)S(1)} %copy.99) | copy-start | bytes 292
  44.1 374.4 %copy-start.15 = (f32[5,128]{1,0:T(8,128)}, f32[5,128]{1,0:T(8,128)S(1)}, u32[]{:S(2)}) copy-start(f32[5,128]{1,0:T(8,128)S(1)} %get-tuple-element.94.kernel_ref) | copy-start | bytes 7684
  373.8 33.9 %copy-start.26 = (bf16[2048,4096]{1,0:T(8,128)(2,1)S(1)}, bf16[2048,4096]{1,0:T(8,128)(2,1)}, u32[]{:S(2)}) copy-start(bf16[2048,4096]{1,0:T(8,128)(2,1)} %get-tuple-element.34) | copy-start | bytes 50331652
  373.8 33.9 %copy-start.27 = (bf16[2,4,512,512]{3,2,1,0:T(8,128)(2,1)S(1)}, bf16[2,4,512,512]{3,2,1,0:T(8,128)(2,1)}, u32[]{:S(2)}) copy-start(bf16[2,4,512,512]{3,2,1,0:T(8,128)(2,1)} %get-tuple-element.35) | copy-start | bytes 12582916
  418.5 28.1 %copy-start.4 = (f32[5,768]{1,0:T(8,128)}, f32[5,768]{1,0:T(8,128)S(1)}, u32[]{:S(2)}) copy-start(f32[5,768]{1,0:T(8,128)S(1)} %pad_maximum_fusion.kernel_ref) | copy-start | bytes 46084
  449.6 3.7 collective-permute-start
  469.4 594.2 %all-gather.2.cloned.1.call-start = ((), (), s32[]{:S(2)}) async-start(), calls=%async_computation.2 | async-start | bytes 5242880 | tf_op jit(solution)/shard_map/all_gather | solution.py:915
  522.8 70.1 %collective-permute-start.1 = (f32[2048,128]{1,0:T(8,128)}, f32[2048,128]{1,0:T(8,128)S(1)}, u32[]{:S(2)}, u32[]{:S(2)}) collective-permute-start(f32[2048,128]{1,0:T(8,128)} %get-tuple-element.42), channel_id=1, source_target_pairs={{0,4},{4,0},{8,12},{12,8},{1,5},{5,1},{9,13},{13,9},{2,6},{6,2},{1... | collective-permute-start | bytes 3145736 | tf_op jit(solution)/shard_map/ppermute | solution.py:877
  547.4 14.3 %copy-start.19 = (f32[5,512]{1,0:T(8,128)S(1)}, f32[5,512]{1,0:T(8,128)}, u32[]{:S(2)}) copy-start(f32[5,512]{1,0:T(8,128)} %get-tuple-element.46) | copy-start | bytes 30724
  547.4 14.3 %copy-start.23 = (f32[3,8]{1,0:T(4,128)S(1)}, f32[3,8]{1,0:T(4,128)}, u32[]{:S(2)}) copy-start(f32[3,8]{1,0:T(4,128)} %get-tuple-element.48) | copy-start | bytes 292
  672.6 29.5 %copy-start.28 = (bf16[2048,256]{1,0:T(8,128)(2,1)S(1)}, bf16[2048,256]{1,0:T(8,128)(2,1)}, u32[]{:S(2)}) copy-start(bf16[2048,256]{1,0:T(8,128)(2,1)} %get-tuple-element.44) | copy-start | bytes 3145732
  712.2 270.8 %copy-start.14 = (f32[4096]{0:T(1024)S(1)}, f32[4096]{0:T(1024)}, u32[]{:S(2)}) copy-start(f32[4096]{0:T(1024)} %param.12) | copy-start | bytes 49156
  712.2 270.9 %copy-start.18 = (f32[512]{0:T(512)S(1)}, f32[512]{0:T(512)}, u32[]{:S(2)}) copy-start(f32[512]{0:T(512)} %copy-done.17) | copy-start | bytes 6148
  983.0 27.8 %copy-start.8 = (bf16[4,512,256]{2,1,0:T(8,128)(2,1)S(1)}, bf16[4,512,256]{2,1,0:T(8,128)(2,1)}, u32[]{:S(2)}) copy-start(bf16[4,512,256]{2,1,0:T(8,128)(2,1)} %get-tuple-element.51) | copy-start | bytes 3145732
  1039.8 11.6 %copy-start.9 = (f32[4,512,128]{2,1,0:T(8,128)S(1)}, f32[4,512,128]{2,1,0:T(8,128)}, u32[]{:S(2)}) copy-start(f32[4,512,128]{2,1,0:T(8,128)} %slice.59) | copy-start | bytes 3145732
  1045.5 9.6 copy-start.20
  1055.2 13.1 %copy-start.1 = (f32[5,2048]{1,0:T(8,128)S(1)}, f32[5,2048]{1,0:T(8,128)}, u32[]{:S(2)}) copy-start(f32[5,2048]{1,0:T(8,128)} %param.16) | copy-start | bytes 122884
  (9 other events, 44.4 us)
Sparse Core Ops, SparseCore 0:
  469.5 199.9 reduce-scatter.1
  672.7 33.4 all-gather.1

commit v4 on v3

--- a/solution.py
+++ b/solution.py
@@ -441,13 +441,13 @@
     )
 
 
-def gather_body(order, sizes, *refs):
+def gather_body(order, sizes, parts, *refs):
     nctx, ndp, ntp = sizes
-    ntok, nw = 2, (len(refs) - 9) // 2 - 2
-    toks, weights = refs[:ntok], refs[ntok : ntok + nw]
-    tok_outs = refs[ntok + nw : 2 * ntok + nw]
-    weight_outs = refs[2 * ntok + nw : 2 * ntok + 2 * nw]
-    z_send, z_recv, t_send, t_recv, w_send, w_recv, x_send, x_recv, own = refs[2 * ntok + 2 * nw :]
+    ntok, nin, nw = 2, parts[-1][0] + 1, parts[-1][2] + 1
+    toks, weights = refs[:ntok], refs[ntok : ntok + nin]
+    tok_outs = refs[ntok + nin : 2 * ntok + nin]
+    weight_outs = refs[2 * ntok + nin : 2 * ntok + nin + nw]
+    z_send, z_recv, t_send, t_recv, w_send, w_recv, x_send, x_recv, own = refs[2 * ntok + nin + nw :]
     c, d, t = lax.axis_index("ctx"), lax.axis_index("dp"), lax.axis_index("tp")
     near = t + 1 - 2 * lax.rem(t, 2)
     far = lax.rem(t + 2, ntp)
@@ -461,6 +461,17 @@
     for peer in peers:
         pl.semaphore_signal(barrier, inc=1, device_id=peer, device_id_type=MESH)
     pl.semaphore_wait(barrier, len(peers))
+
+    def piece(p, to):
+        array, column, _, _, width = parts[p]
+        return weights[array].at[:, pl.ds(pl.multiple_of(column(to), N), width)]
+
+    def landing(p, block):
+        _, _, out, start, width = parts[p]
+        return weight_outs[out].at[d, block, :, start : start + width]
+
+    def of(out):
+        return [p for p in range(len(parts)) if parts[p][2] == out]
 
     def rows(a, block, quarter):
         return tok_outs[a].at[pl.ds(pl.multiple_of(block * length + quarter * part, 16), part), :]
@@ -489,18 +500,17 @@
         view = rows(a, block, quarter)
         return remote(view, view, t_send.at[a, block, kind], t_recv.at[a, block, kind], {"tp": near})
 
-    def w_copy(a, s):
+    def w_copy(p, s):
         to = lax.rem(c + s, nctx)
-        return remote(weights[a].at[to], weight_outs[a].at[d, c], w_send.at[a, s], w_recv.at[a, s], {"ctx": to})
-
-    def w_arrival(a, s):
+        return remote(piece(p, to), landing(p, c), w_send.at[p, s], w_recv.at[p, s], {"ctx": to})
+
+    def w_arrival(p, s):
+        view = landing(p, lax.rem(c - s + nctx, nctx))
+        return remote(view, view, w_send.at[p, s], w_recv.at[p, s], {"ctx": c})
+
+    def x_copy(a, s, e):
         view = weight_outs[a].at[d, lax.rem(c - s + nctx, nctx)]
-        return remote(view, view, w_send.at[a, s], w_recv.at[a, s], {"ctx": c})
-
-    def x_copy(a, s, e):
-        block = lax.rem(c - s + nctx, nctx)
-        source = weights[a].at[c] if s == 0 else weight_outs[a].at[d, block]
-        return remote(source, weight_outs[a].at[d, block], x_send.at[a, s, e], x_recv.at[a, s, e], {"dp": lax.rem(d + e, ndp)})
+        return remote(view, view, x_send.at[a, s, e], x_recv.at[a, s, e], {"dp": lax.rem(d + e, ndp)})
 
     def x_arrival(a, s, e):
         view = weight_outs[a].at[lax.rem(d - e + ndp, ndp), lax.rem(c - s + nctx, nctx)]
@@ -509,8 +519,8 @@
     def own_tok(a):
         return pltpu.make_async_copy(toks[a], tok_outs[a].at[pl.ds(pl.multiple_of(c * length, 16), length), :], own.at[a])
 
-    def own_weight(a):
-        return pltpu.make_async_copy(weights[a].at[c], weight_outs[a].at[d, c], own.at[ntok + a])
+    def own_piece(p):
+        return pltpu.make_async_copy(piece(p, c), landing(p, c), own.at[ntok + p])
 
     def launch(step):
         kind, a, j = step
@@ -522,7 +532,8 @@
                 def _():
                     copy.start()
         else:
-            w_copy(a, j).start()
+            for p in of(a):
+                w_copy(p, j).start()
 
     def settle(step):
         kind, a, j = step
@@ -537,7 +548,8 @@
                     tp_copy(a, block, 0).start()
                     tp_copy(a, block, 1).start()
         else:
-            w_arrival(a, j).wait_recv()
+            for p in of(a):
+                w_arrival(p, j).wait_recv()
             for e in range(1, ndp):
                 x_copy(a, j, e).start()
 
@@ -554,8 +566,11 @@
 
     for step in order[:DEPTH]:
         launch(step)
+    for p in range(len(parts)):
+        own_piece(p).start()
+    for p in range(len(parts)):
+        own_piece(p).wait()
     for a in range(nw):
-        own_weight(a).start()
         for e in range(1, ndp):
             x_copy(a, 0, e).start()
     for a in range(ntok):
@@ -585,12 +600,12 @@
                     tp_arrival(a, block, 1).wait_recv()
                     tp_arrival(a, block, 2).wait_recv()
         else:
-            w_copy(a, j).wait_send()
+            for p in of(a):
+                w_copy(p, j).wait_send()
             for e in range(1, ndp):
                 x_copy(a, j, e).wait_send()
                 x_arrival(a, j, e).wait_recv()
     for a in range(nw):
-        own_weight(a).wait()
         for e in range(1, ndp):
             x_copy(a, 0, e).wait_send()
             x_arrival(a, 0, e).wait_recv()
@@ -598,26 +613,28 @@
         own_tok(a).wait()
 
 
-def gather_all(toks, weights, sizes):
+def gather_all(toks, weights, parts, sizes):
     nctx, ndp, ntp = sizes
     turns = range(1, nctx)
-    nw = len(weights)
+    nw = parts[-1][2] + 1
+    widths = [sum(p[4] for p in parts if p[2] == out) for out in range(nw)]
+    shard_rows = weights[0].shape[0]
     tok = lambda a, j: [("tok", a, j)] if j < nctx - 1 else []
     per = lambda a: [("w", a, s) for s in turns]
     order = tok(0, 0) + tok(1, 0) + per(0) + tok(0, 1) + tok(1, 1) + per(1)[:1] + tok(0, 2) + tok(1, 2) + per(1)[1:]
     any_space = pl.BlockSpec(memory_space=pl.ANY)
     length, model = toks[0].shape
     out_shape = [jax.ShapeDtypeStruct((nctx * length, model), BF16) for _ in toks]
-    out_shape += [jax.ShapeDtypeStruct((ndp,) + w.shape, BF16) for w in weights]
+    out_shape += [jax.ShapeDtypeStruct((ndp, nctx, shard_rows, width), BF16) for width in widths]
     dma = pltpu.SemaphoreType.DMA
     return pl.pallas_call(
-        functools.partial(gather_body, order, sizes),
+        functools.partial(gather_body, order, sizes, parts),
         out_shape=out_shape,
-        in_specs=[any_space] * (len(toks) + nw),
+        in_specs=[any_space] * (len(toks) + len(weights)),
         out_specs=[any_space] * len(out_shape),
         scratch_shapes=[
             dma((2, nctx, 2)), dma((2, nctx)), dma((2, nctx, 3)), dma((2, nctx, 3)),
-            dma((nw, nctx)), dma((nw, nctx)), dma((nw, nctx, ndp)), dma((nw, nctx, ndp)), dma((2 + nw,)),
+            dma((len(parts), nctx)), dma((len(parts), nctx)), dma((nw, nctx, ndp)), dma((nw, nctx, ndp)), dma((2 + len(parts),)),
         ],
         compiler_params=pltpu.CompilerParams(collective_id=1, has_side_effects=True),
         name="gather_inputs",
@@ -636,15 +653,15 @@
     lax.fori_loop(0, rows // step, some, 0)
 
 
-def output_body(order, sizes, *refs):
+def output_body(order, sizes, nw, parts, *refs):
     nctx, ndp, ntp = sizes
-    nw = (len(refs) - 23) // 4
-    partial, grads = refs[0], refs[1 : 1 + nw]
-    sum_out, grad_outs = refs[1 + nw], refs[2 + nw : 2 + 2 * nw]
-    (near_in, far_out, far_in, z_out, z_in, held, acc, done) = refs[2 + 2 * nw : 10 + 2 * nw]
-    x_ins = refs[10 + 2 * nw : 10 + 3 * nw]
-    x_sums = refs[10 + 3 * nw : 10 + 4 * nw]
-    (near_s, near_r, far_s, far_r, z_s, z_r, x_s, x_r, w_s, w_r, fin_s, fin_r, local) = refs[10 + 4 * nw :]
+    nout = len(parts)
+    partial, small, grads = refs[0], refs[1], refs[2 : 2 + nw]
+    sum_out, small_out, grad_outs = refs[2 + nw], refs[3 + nw], refs[4 + nw : 4 + nw + nout]
+    rest = refs[4 + nw + nout :]
+    (near_in, far_out, far_in, z_out, z_in, held, acc, done) = rest[:8]
+    x_ins, x_sums = rest[8 : 8 + nw], rest[8 + nw : 8 + 2 * nw]
+    (near_s, near_r, far_s, far_r, z_s, z_r, x_s, x_r, w_s, w_r, fin_s, fin_r, local, small_s, small_r) = rest[8 + 2 * nw :]
     c, d, t = lax.axis_index("ctx"), lax.axis_index("dp"), lax.axis_index("tp")
     near = t + 1 - 2 * lax.rem(t, 2)
     far = lax.rem(t + 2, ntp)
@@ -654,13 +671,20 @@
     wrap = lambda i: lax.rem(i + nctx, nctx)
 
     barrier = pltpu.get_barrier_semaphore()
-    peers = [{"ctx": lax.rem(c + s, nctx)} for s in range(1, nctx)]
-    peers += [{"dp": lax.rem(d + e, ndp)} for e in range(1, ndp)]
-    peers += [{"tp": near}, {"tp": far}]
+    others = [(e, s) for e in range(ndp) for s in range(nctx) if e or s]
+    place = lambda e, s: {"dp": lax.rem(d + e, ndp), "ctx": lax.rem(c + s, nctx)}
+    peers = [place(e, s) for e, s in others] + [{"tp": near}, {"tp": far}]
     for peer in peers:
         pl.semaphore_signal(barrier, inc=1, device_id=peer, device_id_type=MESH)
     pl.semaphore_wait(barrier, len(peers))
 
+    def small_copy(e, s):
+        return remote(small, small_out.at[d, c], small_s.at[e, s], small_r.at[e, s], place(e, s))
+
+    def small_arrival(e, s):
+        view = small_out.at[lax.rem(d - e + ndp, ndp), wrap(c - s)]
+        return remote(view, view, small_s.at[e, s], small_r.at[e, s], place(e, s))
+
     def rows(s, quarter):
         return partial.at[pl.ds(pl.multiple_of(wrap(c + s) * length + quarter * part, 16), part), :]
 
@@ -677,12 +701,25 @@
         to = lax.rem(d + e, ndp)
         return remote(grads[a].at[to, wrap(c + s)], x_ins[a].at[s, e - 1], x_s.at[a, s, e], x_r.at[a, s, e], {"dp": to})
 
-    def w_copy(a, s):
-        return remote(x_sums[a].at[s], grad_outs[a].at[c], w_s.at[a, s], w_r.at[a, s], {"ctx": wrap(c + s)})
-
-    def w_arrival(a, s):
-        view = grad_outs[a].at[wrap(c - s)]
-        return remote(view, view, w_s.at[a, s], w_r.at[a, s], {"ctx": c})
+    def piece(p, s):
+        a, start, width, _, _ = parts[p]
+        return x_sums[a].at[s, :, start : start + width]
+
+    def landing(p, block):
+        _, _, width, out, split_columns = parts[p]
+        if split_columns:
+            return grad_outs[out].at[:, pl.ds(pl.multiple_of(block * width, N), width)]
+        return grad_outs[out].at[block]
+
+    def w_copy(p, s):
+        return remote(piece(p, s), landing(p, c), w_s.at[p, s], w_r.at[p, s], {"ctx": wrap(c + s)})
+
+    def w_arrival(p, s):
+        view = landing(p, wrap(c - s))
+        return remote(view, view, w_s.at[p, s], w_r.at[p, s], {"ctx": c})
+
+    def w_own(p):
+        return pltpu.make_async_copy(piece(p, 0), landing(p, c), local.at[2 + nw * nctx + p])
 
     def load(s, quarter, slot):
         return pltpu.make_async_copy(rows(s, quarter), held.at[slot], local.at[slot])
@@ -717,10 +754,11 @@
             for e in range(1, ndp):
                 x_copy(a, s, e).wait_recv()
             add_rows(x_sums[a].at[s], [x_sums[a].at[s]] + [x_ins[a].at[s, e - 1] for e in range(1, ndp)], x_sums[a].shape[1], 16)
+        for p in range(nout):
             if s > 0:
-                w_copy(a, s).start()
+                w_copy(p, s).start()
             else:
-                pltpu.make_async_copy(x_sums[a].at[0], grad_outs[a].at[c], local.at[2 + nw * nctx + a]).start()
+                w_own(p).start()
 
     for s in order:
         for slot in (1, 0):
@@ -730,6 +768,10 @@
     ahead = 2
     for s in order[:ahead]:
         start_x(s)
+    for e, s in others:
+        small_copy(e, s).start()
+    small_own = pltpu.make_async_copy(small, small_out.at[d, c], local.at[2 + nw * nctx + nout])
+    small_own.start()
     for s in order[:ahead]:
         near_sum(s)
     for index, s in enumerate(order):
@@ -769,30 +811,37 @@
         for a in range(nw):
             for e in range(1, ndp):
                 x_copy(a, s, e).wait_send()
+        for p in range(nout):
             if s > 0:
-                w_copy(a, s).wait_send()
-                w_arrival(a, s).wait_recv()
+                w_copy(p, s).wait_send()
+                w_arrival(p, s).wait_recv()
             else:
-                pltpu.make_async_copy(x_sums[a].at[0], grad_outs[a].at[c], local.at[2 + nw * nctx + a]).wait()
+                w_own(p).wait()
         if s > 0:
             z_copy(s).wait_send()
-
-
-def return_all(partial, grads, sizes):
+    for e, s in others:
+        small_copy(e, s).wait_send()
+        small_arrival(e, s).wait_recv()
+    small_own.wait()
+
+
+def return_all(partial, small, grads, parts, sizes):
     nctx, ndp, ntp = sizes
     length = partial.shape[0] // nctx
     part, model = length // ntp, partial.shape[1]
-    nw = len(grads)
+    nw, nout = len(grads), len(parts)
+    outs = [(nctx,) + grads[p[0]].shape[2:] if not p[4] else (grads[0].shape[2], nctx * p[2]) for p in parts]
     order = [nctx // 2] + [s for s in range(1, nctx) if s != nctx // 2] + [0]
     any_space = pl.BlockSpec(memory_space=pl.ANY)
     dma = pltpu.SemaphoreType.DMA
     vmem = pltpu.VMEM
     strip = lambda *lead: vmem(lead + (part, model), BF16)
     return pl.pallas_call(
-        functools.partial(output_body, order, sizes),
-        out_shape=[jax.ShapeDtypeStruct((length, model), BF16)] + [jax.ShapeDtypeStruct(g.shape[1:], BF16) for g in grads],
-        in_specs=[any_space] * (1 + nw),
-        out_specs=[any_space] * (1 + nw),
+        functools.partial(output_body, order, sizes, nw, parts),
+        out_shape=[jax.ShapeDtypeStruct((length, model), BF16), jax.ShapeDtypeStruct((ndp, nctx) + small.shape, F32)]
+        + [jax.ShapeDtypeStruct(out, BF16) for out in outs],
+        in_specs=[any_space] * (2 + nw),
+        out_specs=[any_space] * (2 + nout),
         scratch_shapes=[
             strip(nctx, 2), strip(nctx), strip(nctx), strip(nctx), strip(nctx), strip(2), vmem((part, model), F32), strip(),
         ]
@@ -800,12 +849,12 @@
         + [vmem((nctx,) + g.shape[2:], BF16) for g in grads]
         + [
             dma((nctx, 2)), dma((nctx, 2)), dma((nctx,)), dma((nctx,)), dma((nctx,)), dma((nctx,)),
-            dma((nw, nctx, ndp)), dma((nw, nctx, ndp)), dma((nw, nctx)), dma((nw, nctx)), dma((3,)), dma((3,)),
-            dma((2 + nw * nctx + nw,)),
+            dma((nw, nctx, ndp)), dma((nw, nctx, ndp)), dma((nout, nctx)), dma((nout, nctx)), dma((3,)), dma((3,)),
+            dma((2 + nw * nctx + nout + 1,)), dma((ndp, nctx)), dma((ndp, nctx)),
         ],
         compiler_params=pltpu.CompilerParams(collective_id=2, has_side_effects=True, vmem_limit_bytes=60 << 20),
         name="return_outputs",
-    )(partial, *grads)
+    )(partial, small, *grads)
 
 
 def small_body(sizes, value, gathered, send, recv, own):
@@ -862,7 +911,8 @@
     ctx = lax.axis_index("ctx")
     rows = dt_weight.shape[0]
     inner = conv_x.shape[1]
-    groups = bc_weight.shape[2] // N
+    pair_width = bc_weight.shape[2]
+    groups = pair_width // N
     share = nctx // groups
     assert share == 2 and groups * share == nctx
     width = inner // nctx
@@ -881,14 +931,18 @@
     rscale = lax.rsqrt(jnp.mean(hidden * hidden, axis=-1, keepdims=True) + EPS)
     normed = (hidden * rscale * norm_gain).astype(BF16)
 
-    zx = zx_weight.reshape(rows, 2, nctx, width)
-    maps = bc_weight.reshape(rows, 2, groups, N).transpose(0, 2, 1, 3)
-    own = maps.reshape(rows, nctx, N)
-    other = maps[:, :, ::-1].reshape(rows, nctx, N)
-    steps = jnp.pad(dt_weight.reshape(rows, nctx, heads), ((0, 0), (0, 0), (0, N - heads)))
-    packed_in = jnp.concatenate([zx[:, 0], zx[:, 1], own, steps, other], axis=2).transpose(1, 0, 2)
-    packed_out = out_weight.reshape(rows, nctx, width).transpose(1, 0, 2)
-    normed_all, cot_all, weight_in, weight_out = gather_all((normed, cot), (packed_in, packed_out), (nctx, ndp, ntp))
+    steps = jnp.pad(dt_weight.reshape(rows, nctx, heads), ((0, 0), (0, 0), (0, N - heads))).reshape(rows, nctx * N)
+    map_at = lambda which: lambda to: (lax.rem(to + which, 2) * groups + to // share) * N
+    parts = (
+        (0, lambda to: to * width, 0, 0, width),
+        (0, lambda to: inner + to * width, 0, width, width),
+        (1, map_at(0), 0, 2 * width, N),
+        (2, lambda to: to * N, 0, 2 * width + N, N),
+        (1, map_at(1), 0, 2 * width + 2 * N, N),
+        (3, lambda to: to * width, 1, 0, width),
+    )
+    sources = (zx_weight.reshape(rows, 2 * inner), bc_weight.reshape(rows, 2 * pair_width), steps, out_weight)
+    normed_all, cot_all, weight_in, weight_out = gather_all((normed, cot), sources, parts, (nctx, ndp, ntp))
     weight_in = weight_in.reshape(model_width, -1)
     weight_out = weight_out.reshape(model_width, width)
 
@@ -910,9 +964,6 @@
     gate_pre = proj[:, :width]
     gated_norm = (ssd * (gate_pre * jax.nn.sigmoid(gate_pre)) * norms[:, 0:1] * gain).astype(BF16)
     branch = sum_rows(dot_last(gated_norm, weight_out))
-    part = length // ntp
-    hidden_part = lax.dynamic_slice_in_dim(hidden, lax.axis_index("tp") * part, part, 0)
-    mixed = lax.all_gather((hidden_part + branch).astype(BF16), "tp", axis=0, tiled=True)
     grad_zx, grad_steps, grad_own, grad_other, grad_kernel_x, grad_heads, gate_gain_grad = mixer_backward(
         odd, proj, low, grad_gated, ssd, states, norms, kernel, heads_mine, gain
     )
@@ -926,7 +977,23 @@
         blocks(dot_first(cot_all, gated_norm)),
     )
     partial = dot_last(grad_all, weight_in[:, : grad_all.shape[1]]).astype(BF16)
-    grad_normed, back_zx, back_rest, back_out = return_all(partial, weight_grads, (nctx, ndp, ntp))
+    pieces = (grad_kernel_x, grad_kernel_own, grad_heads, gate_gain_grad)
+    small = jnp.concatenate([piece.reshape(-1) for piece in pieces])
+    lines = -(-small.shape[0] // (8 * N)) * 8
+    small = jnp.pad(small, (0, lines * N - small.shape[0])).reshape(lines, N)
+    out_parts = (
+        (0, 0, width, 0, True),
+        (0, width, width, 1, True),
+        (1, 0, 2 * N, 2, False),
+        (2, 0, width, 3, True),
+    )
+    grad_normed, table, back_z, back_x, back_rest, back_out = return_all(
+        partial, small, weight_grads, out_parts, (nctx, ndp, ntp)
+    )
+    grad_normed, branch = lax.optimization_barrier((grad_normed, branch))
+    part = length // ntp
+    hidden_part = lax.dynamic_slice_in_dim(hidden, lax.axis_index("tp") * part, part, 0)
+    mixed = lax.all_gather((hidden_part + branch).astype(BF16), "tp", axis=0, tiled=True)
     grad_normed = grad_normed.astype(F32)
 
     grad_hat = grad_normed * norm_gain
@@ -936,26 +1003,22 @@
     )
     tokens_grad = cot.astype(F32) + grad_hidden
 
-    zx_weight_grad = back_zx.astype(F32).reshape(nctx, rows, 2, width).transpose(1, 2, 0, 3).reshape(rows, 2, inner)
+    zx_weight_grad = jnp.stack([back_z, back_x], axis=1).astype(F32)
     back_rest = back_rest.astype(F32)
     bc_weight_grad = back_rest[:, :, :N].reshape(groups, 2, rows, N).transpose(2, 1, 0, 3).reshape(rows, 2, groups * N)
     dt_weight_grad = back_rest[:, :, N : N + heads].transpose(1, 0, 2).reshape(rows, nctx * heads)
-    out_weight_grad = back_out.astype(F32).transpose(1, 0, 2).reshape(rows, inner)
-
-    pieces = (grad_kernel_x, grad_kernel_own, grad_heads, gate_gain_grad, norm_gain_grad)
-    small = jnp.concatenate([piece.reshape(-1) for piece in pieces])
-    lines = -(-small.shape[0] // (8 * N)) * 8
-    small = jnp.pad(small, (0, lines * N - small.shape[0])).reshape(lines, N)
-    table = jnp.sum(gather_small(small, (nctx, ndp)), axis=0).reshape(nctx, lines * N)
+    out_weight_grad = back_out.astype(F32)
+
+    table = jnp.sum(table, axis=0).reshape(nctx, lines * N)
     ends = [0]
     for piece in pieces:
         ends.append(ends[-1] + piece.size)
-    kernel_x, kernel_own, head_grad, gain_grad, norm_grad = [table[:, a:b] for a, b in zip(ends[:-1], ends[1:])]
+    kernel_x, kernel_own, head_grad, gain_grad = [table[:, a:b] for a, b in zip(ends[:-1], ends[1:])]
     conv_x_grad = kernel_x.reshape(nctx, taps + 1, width).transpose(1, 0, 2).reshape(taps + 1, inner)
     conv_bc_grad = kernel_own.reshape(groups, 2, taps + 1, N).transpose(2, 1, 0, 3).reshape(taps + 1, 2, groups * N)
     head_grad = head_grad.reshape(nctx, 3, heads).transpose(1, 0, 2).reshape(3, nctx * heads)
     gate_gain_grad = gain_grad.reshape(inner)
-    norm_gain_grad = jnp.sum(norm_grad, axis=0)
+    norm_gain_grad = jnp.sum(gather_small(norm_gain_grad.reshape(-1, N), (nctx, ndp)), axis=(0, 1)).reshape(model_width)
     return (
         mixed.reshape(tokens.shape),
         tokens_grad.reshape(tokens.shape),

time: 1080 us -> 972 us (0.900)
  waiting for transfers between devices: 103 us -> 33.4 us
  local copies, waits for them, and re-layouts: 90 us -> 42.5 us
    reduce_scatter x1, waiting for transfers between devices: 69.1 us -> 0.02 us  [sum_rows(): lax.psum_scatter(partial.astype(BF16), ('ctx', 'tp'), scatter_dimension=0...]
    reshape x6 -> x0, local copies, waits for them, and re-layouts: 29.8 us -> none  [the longest x2 20 us: shards(): back_zx.astype(F32).reshape(nctx, rows, 2, width).transpose(1, 2, 0, 3)]
    unnamed x72 -> x63, local copies, waits for them, and re-layouts: 41.6 us -> 27 us
  transfers between devices with their start and end apart: 4 -> 4, of which waited for: 3 -> 2; matrix products, arithmetic and copies ran while one was open for 14% -> 14% of each run, Pallas kernels for 32% -> 35%
where the time goes in v4:
time: 972 us; the launch traced here: 966 us
  Pallas kernels  690 us (71%)
  matrix products  135 us (14%)
  other arithmetic  48.9 us (5%)
  local copies, waits for them, and re-layouts  42.5 us (4%)
  waiting for transfers between devices  33.4 us (3%)
  between operations  14.6 us (2%)
    pallas_call x1, Pallas kernels, gather_all(): pl.pallas_call(functools.partial(gather_body, order, sizes, parts), out_s...  322 us
    pallas_call x1, Pallas kernels, return_all(): pl.pallas_call(functools.partial(output_body, order, sizes, nw, parts), o...  271 us
    dot_general x3, matrix products, dot_first(): lax.dot_general(left_side, right_side, (((0,), (0,)), ((), ())), preferre...  51.1 us
    pallas_call x1, Pallas kernels, mixer_backward(): pl.pallas_call(backward_body, grid=(count,), in_specs=specs[:3] + [specs[...  44.9 us
    dot_general x2, matrix products, dot_last(): lax.dot_general(left_side, right_side, (((1,), (1,)), ((), ())), preferre...  39.5 us
    dot_general x1, matrix products, shards(): proj = jnp.dot(normed_all, weight_in, preferred_element_type=F32)  34.1 us
    ppermute x2, waiting for transfers between devices, partner(): return lax.ppermute(value, 'ctx', [(i, i ^ 1) for i in range(nctx)])  33.3 us
    pallas_call x1, Pallas kernels, mixer_forward(): pl.pallas_call(forward_body, grid=(count,), in_specs=proj_specs(width, la...  28 us
  transfers between devices with their start and end apart: 4, of which 2 were waited for; matrix products, arithmetic and copies ran while one was open for 14% of the time, Pallas kernels for 35%

profile of v4, /device:TPU:0, one launch (start us, length us, event | category | flops | bytes accessed | tf_op | source)
XLA Modules:
  0.0 965.8 jit_solution(16435631693322722913)
XLA Ops:
  9.5 3.2 fusion.9
  13.4 4.4 copy.65
  20.2 5.8 fusion.11.refs_0_
  26.0 322.4 %gather_inputs.1 = (bf16[2048,4096]{1,0:T(8,128)(2,1)}, bf16[2048,4096]{1,0:T(8,128)(2,1)}, bf16[2,4,512,1408]{3,2,1,0:T(8,128)(2,1)}, bf16[2,4,512,512]{3,2,1,0:T(8,128)(2,1)}) custom-call(bf16[512,4096]{1,0:T(8,128)(2,1)} %fusion.11.refs_0_, bf16[512,4096]{1,0:T(8,128)(2,1)} %bitcast.105, bf16[512,4096]{1,0:T(8,128)(2,1)} %bitcast.104, ...), custom_call_target="tpu_custom_call" | custom-call | tf_op jit(solution)/shard_map/gather_inputs/pallas_call | solution.py:630
  348.4 34.1 %fusion.21.gate_ref.x_ref.own_ref.step_ref.other_ref.edge_ref = f32[2048,1408]{1,0:T(8,128)} fusion(bf16[2048,4096]{1,0:T(8,128)(2,1)} %get-tuple-element.36, bf16[4096,1408]{1,0:T(8,128)(2,1)} %bitcast.140), kind=kOutput, calls=%fused_computation.53 | convolution fusion | flops 23622320128 | bytes 39845888 | tf_op jit(solution)/shard_map/dot_general | solution.py:950
  382.4 10.3 %fusion.22.up_ref = f32[2048,512]{1,0:T(8,128)} fusion(bf16[2048,4096]{1,0:T(8,128)(2,1)S(1)} %copy-done.24, bf16[4096,512]{1,0:T(8,128)(2,1)S(1)} %bitcast.142), kind=kOutput, calls=%fused_computation.54 | convolution fusion | flops 8589934592 | bytes 25165824 | tf_op jit(solution)/shard_map/dot_general | solution.py:949
  392.8 28.0 %mixer_forward.1 = (bf16[2048,768]{1,0:T(8,128)(2,1)S(1)}, f32[2048,512]{1,0:T(8,128)}, f32[8,128,512]{2,1,0:T(8,128)S(1)}, f32[2,2048]{1,0:T(2,128)S(1)}) custom-call(s32[1,1]{1,0:T(1,128)} %bitcast.1.odd_ref, f32[2048,1408]{1,0:T(8,128)} %fusion.21.gate_ref.x_ref.own_ref.step_ref.other_ref.edge_ref, ...), custom_call_target="tpu_custom_call" | custom-call | tf_op jit(solution)/shard_map/mixer_forward/pallas_call | solution.py:184
  427.6 4.2 multiply_convert_fusion
  431.8 11.8 %convolution_convert_fusion = bf16[2048,4096]{1,0:T(8,128)(2,1)} fusion(bf16[2048,512]{1,0:T(8,128)(2,1)S(1)} %multiply_convert_fusion, bf16[4096,512]{1,0:T(8,128)(2,1)S(1)} %bitcast.143), kind=kOutput, calls=%fused_computation | convolution fusion | flops 8598323200 | bytes 23068672 | tf_op jit(solution)/shard_map/dot_general | solution.py:896
  443.7 7.1 convert_element_type.49
  452.1 44.9 %mixer_backward.1 = (bf16[2048,1024]{1,0:T(8,128)(2,1)}, bf16[2048,128]{1,0:T(8,128)(2,1)}, f32[2048,128]{1,0:T(8,128)}, f32[2048,128]{1,0:T(8,128)}, f32[5,512]...) custom-call(s32[1,1]{1,0:T(1,128)} %bitcast.1.odd_ref, ...), custom_call_target="tpu_custom_call" | custom-call | tf_op jit(solution)/shard_map/mixer_backward/pallas_call | solution.py:345
  497.6 24.1 %convolution_convert_fusion.2 = bf16[4096,1024]{1,0:T(8,128)(2,1)} fusion(bf16[2048,4096]{1,0:T(8,128)(2,1)} %get-tuple-element.36, bf16[2048,1024]{1,0:T(8,128)(2,1)} %get-tuple-element.44), kind=kOutput, calls=%fused_computation.20 | convolution fusion | flops 17184063488 | bytes 29360128 | tf_op jit(solution)/shard_map/dot_general | solution.py:900
  521.7 14.5 %convolution_convert_fusion.3 = bf16[4096,512]{1,0:T(8,128)(2,1)} fusion(bf16[2048,4096]{1,0:T(8,128)(2,1)} %get-tuple-element.38, bf16[2048,512]{1,0:T(8,128)(2,1)S(1)} %multiply_convert_fusion), kind=kOutput, calls=%fused_computation.21 | convolution fusion | flops 8592031744 | bytes 23068672 | tf_op jit(solution)/shard_map/dot_general | solution.py:900
  536.3 30.8 %collective-permute-done.1.theirs_ref = f32[2048,128]{1,0:T(8,128)S(1)} collective-permute-done((f32[2048,128]{1,0:T(8,128)}, f32[2048,128]{1,0:T(8,128)S(1)}, u32[]{:S(2)}, u32[]{:S(2)}) %collective-permute-start.1) | collective-permute-done | bytes 1048608 | tf_op jit(solution)/shard_map/ppermute | solution.py:927
  568.1 6.6 map_backward.1
  576.1 12.5 %convolution_convert_fusion.4 = bf16[4096,256]{1,0:T(8,128)(2,1)} fusion(bf16[2048,4096]{1,0:T(8,128)(2,1)} %get-tuple-element.36, bf16[2048,256]{1,0:T(8,128)(2,1)} %get-tuple-element.48), kind=kOutput, calls=%fused_computation.25 | convolution fusion | flops 4296015872 | bytes 19922944 | tf_op jit(solution)/shard_map/dot_general | solution.py:900
  588.6 27.8 %convolution_convert_fusion.1.refs_0_ = bf16[2048,4096]{1,0:T(8,128)(2,1)} fusion(bf16[4096,1408]{1,0:T(8,128)(2,1)} %bitcast.141, bf16[2048,256]{1,0:T(8,128)(2,1)S(1)} %copy-done.26, bf16[2048,1024]{1,0:T(8,128)(2,1)} %get-tuple-element.44), kind=kOutput, calls=%fused_computation.1 | convolution fusion | flops 21493710848 | bytes 32505856 | tf_op jit(solution)/shard_map/dot_general | solution.py:896
  616.3 270.8 %return_outputs.1 = (bf16[512,4096]{1,0:T(8,128)(2,1)}, f32[2,4,32,128]{3,2,1,0:T(8,128)}, bf16[512,2048]{1,0:T(8,128)(2,1)}, bf16[512,2048]{1,0:T(8,128)(2,1)},...) custom-call(bf16[2048,4096]{1,0:T(8,128)(2,1)} %convolution_convert_fusion.1.refs_0_, ...), custom_call_target="tpu_custom_call" | custom-call | tf_op jit(solution)/shard_map/return_outputs/pallas_call | solution.py:839
  888.7 2.9 fusion.16
  895.8 11.2 %copy.63 = f32[512,2,2048]{2,1,0:T(2,128)} copy(f32[512,2,2048]{2,0,1:T(8,128)S(1)} %maximum_convert_fusion) | data formatting | bytes 16777216
  918.5 8.0 fusion.8
  926.5 17.6 %gather_small.1 = f32[2,4,32,128]{3,2,1,0:T(8,128)} custom-call(f32[32,128]{1,0:T(8,128)} %bitcast.125), custom_call_target="tpu_custom_call" | custom-call | tf_op jit(solution)/shard_map/gather_small/pallas_call | solution.py:884
  945.7 8.4 fusion.5
  954.1 4.7 copy.77
  (111 shorter events, 35.1 us)
Async XLA Ops:
  7.2 880.0 %reduce-scatter.2.cloned.1.call-start = ((), (), s32[]{:S(2)}) async-start(), calls=%async_computation.1 | async-start | bytes 17825792 | tf_op jit(solution)/shard_map/reduce_scatter | solution.py:904
  8.7 384.1 %copy-start.6 = (f32[1,512]{1,0:T(1,128)}, f32[1,512]{1,0:T(1,128)S(1)}, u32[]{:S(2)}) copy-start(f32[1,512]{1,0:T(1,128)S(1)} %fusion.35.gain_ref) | copy-start | bytes 6148
  9.5 383.3 %copy-start.5 = (f32[3,1,8]{2,0,1:T(4,128)}, f32[3,1,8]{2,0,1:T(4,128)S(1)}, u32[]{:S(2)}) copy-start(f32[3,1,8]{2,0,1:T(4,128)S(1)} %copy.75) | copy-start | bytes 292
  12.7 5.0 copy-start.17
  13.3 6.8 copy-start.18
  13.4 5.9 copy-start.12
  13.4 6.8 copy-start.13
  20.1 372.6 %copy-start.16 = (f32[5,128]{1,0:T(8,128)}, f32[5,128]{1,0:T(8,128)S(1)}, u32[]{:S(2)}) copy-start(f32[5,128]{1,0:T(8,128)S(1)} %get-tuple-element.109.kernel_ref) | copy-start | bytes 7684
  348.4 34.1 %copy-start.24 = (bf16[2048,4096]{1,0:T(8,128)(2,1)S(1)}, bf16[2048,4096]{1,0:T(8,128)(2,1)}, u32[]{:S(2)}) copy-start(bf16[2048,4096]{1,0:T(8,128)(2,1)} %get-tuple-element.38) | copy-start | bytes 50331652
  348.4 34.1 %copy-start.25 = (bf16[2,4,512,512]{3,2,1,0:T(8,128)(2,1)S(1)}, bf16[2,4,512,512]{3,2,1,0:T(8,128)(2,1)}, u32[]{:S(2)}) copy-start(bf16[2,4,512,512]{3,2,1,0:T(8,128)(2,1)} %get-tuple-element.39) | copy-start | bytes 12582916
  392.7 28.0 %copy-start.4 = (f32[5,768]{1,0:T(8,128)}, f32[5,768]{1,0:T(8,128)S(1)}, u32[]{:S(2)}) copy-start(f32[5,768]{1,0:T(8,128)S(1)} %pad_maximum_fusion.kernel_ref) | copy-start | bytes 46084
  423.8 3.7 collective-permute-start
  443.6 510.4 %all-gather.2.cloned.1.call-start = ((), (), s32[]{:S(2)}) async-start(), calls=%async_computation.2 | async-start | bytes 5242880 | tf_op jit(solution)/shard_map/all_gather | solution.py:996
  497.0 70.1 %collective-permute-start.1 = (f32[2048,128]{1,0:T(8,128)}, f32[2048,128]{1,0:T(8,128)S(1)}, u32[]{:S(2)}, u32[]{:S(2)}) collective-permute-start(f32[2048,128]{1,0:T(8,128)} %get-tuple-element.46), channel_id=1, source_target_pairs={{0,4},{4,0},{8,12},{12,8},{1,5},{5,1},{9,13},{13,9},{2,6},{6,2},{1... | collective-permute-start | bytes 3145736 | tf_op jit(solution)/shard_map/ppermute | solution.py:927
  521.7 14.5 %copy-start.20 = (f32[5,512]{1,0:T(8,128)S(1)}, f32[5,512]{1,0:T(8,128)}, u32[]{:S(2)}) copy-start(f32[5,512]{1,0:T(8,128)} %get-tuple-element.49) | copy-start | bytes 30724
  521.7 14.5 %copy-start.23 = (f32[3,8]{1,0:T(4,128)S(1)}, f32[3,8]{1,0:T(4,128)}, u32[]{:S(2)}) copy-start(f32[3,8]{1,0:T(4,128)} %get-tuple-element.51) | copy-start | bytes 292
  568.1 6.6 copy-start.22
  576.1 12.5 %copy-start.26 = (bf16[2048,256]{1,0:T(8,128)(2,1)S(1)}, bf16[2048,256]{1,0:T(8,128)(2,1)}, u32[]{:S(2)}) copy-start(bf16[2048,256]{1,0:T(8,128)(2,1)} %get-tuple-element.48) | copy-start | bytes 3145732
  895.7 11.3 %copy-start.10 = (bf16[512,2048]{1,0:T(8,128)(2,1)S(1)}, bf16[512,2048]{1,0:T(8,128)(2,1)}, u32[]{:S(2)}) copy-start(bf16[512,2048]{1,0:T(8,128)(2,1)} %get-tuple-element.60) | copy-start | bytes 6291460
  907.0 5.8 copy-start.9
  909.6 8.9 copy-start.14
  909.6 8.9 copy-start.19
  913.6 32.1 %copy-start.21 = (f32[512]{0:T(512)S(1)}, f32[512]{0:T(512)}, u32[]{:S(2)}) copy-start(f32[512]{0:T(512)} %get-tuple-element.111) | copy-start | bytes 6148
  945.7 13.1 %copy-start.1 = (f32[5,2048]{1,0:T(8,128)S(1)}, f32[5,2048]{1,0:T(8,128)}, u32[]{:S(2)}) copy-start(f32[5,2048]{1,0:T(8,128)} %param.16) | copy-start | bytes 122884
  (7 other events, 17.4 us)
Sparse Core Ops, SparseCore 0:
  443.7 202.7 reduce-scatter.1
  891.8 41.7 all-gather.1

commit v5 on v4

--- a/solution.py
+++ b/solution.py
@@ -857,7 +857,7 @@
     )(partial, small, *grads)
 
 
-def small_body(sizes, value, gathered, send, recv, own):
+def small_body(sizes, value, total, gathered, send, recv):
     nctx, ndp = sizes
     c, d = lax.axis_index("ctx"), lax.axis_index("dp")
     others = [(e, s) for e in range(ndp) for s in range(nctx) if e or s]
@@ -866,29 +866,32 @@
     for e, s in others:
         pl.semaphore_signal(barrier, inc=1, device_id=place(e, s), device_id_type=MESH)
     pl.semaphore_wait(barrier, len(others))
-    keep = pltpu.make_async_copy(value, gathered.at[d, c], own)
-    keep.start()
+    gathered[d, c] = value[...]
     for e, s in others:
         remote(value, gathered.at[d, c], send.at[e, s], recv.at[e, s], place(e, s)).start()
     for e, s in others:
         view = gathered.at[lax.rem(d - e + ndp, ndp), lax.rem(c - s + nctx, nctx)]
         remote(view, view, send.at[e, s], recv.at[e, s], place(e, s)).wait_recv()
         remote(value, gathered.at[d, c], send.at[e, s], recv.at[e, s], place(e, s)).wait_send()
-    keep.wait()
-
-
-def gather_small(value, sizes):
+    running = jnp.zeros(value.shape, F32)
+    for e in range(ndp):
+        for s in range(nctx):
+            running = running + gathered[e, s]
+    total[...] = running
+
+
+def sum_small(value, sizes):
     nctx, ndp = sizes
     vmem = pl.BlockSpec(memory_space=pltpu.VMEM)
     dma = pltpu.SemaphoreType.DMA
     return pl.pallas_call(
         functools.partial(small_body, sizes),
-        out_shape=jax.ShapeDtypeStruct((ndp, nctx) + value.shape, F32),
+        out_shape=jax.ShapeDtypeStruct(value.shape, F32),
         in_specs=[vmem],
         out_specs=vmem,
-        scratch_shapes=[dma((ndp, nctx)), dma((ndp, nctx)), dma],
+        scratch_shapes=[pltpu.VMEM((ndp, nctx) + value.shape, F32), dma((ndp, nctx)), dma((ndp, nctx))],
         compiler_params=pltpu.CompilerParams(collective_id=3, has_side_effects=True),
-        name="gather_small",
+        name="sum_small",
     )(value)
 
 
@@ -992,8 +995,8 @@
     )
     grad_normed, branch = lax.optimization_barrier((grad_normed, branch))
     part = length // ntp
-    hidden_part = lax.dynamic_slice_in_dim(hidden, lax.axis_index("tp") * part, part, 0)
-    mixed = lax.all_gather((hidden_part + branch).astype(BF16), "tp", axis=0, tiled=True)
+    token_part = lax.dynamic_slice_in_dim(tokens.reshape(length, model_width), lax.axis_index("tp") * part, part, 0)
+    mixed = lax.all_gather((token_part.astype(F32) + branch).astype(BF16), "tp", axis=0, tiled=True)
     grad_normed = grad_normed.astype(F32)
 
     grad_hat = grad_normed * norm_gain
@@ -1018,7 +1021,7 @@
     conv_bc_grad = kernel_own.reshape(groups, 2, taps + 1, N).transpose(2, 1, 0, 3).reshape(taps + 1, 2, groups * N)
     head_grad = head_grad.reshape(nctx, 3, heads).transpose(1, 0, 2).reshape(3, nctx * heads)
     gate_gain_grad = gain_grad.reshape(inner)
-    norm_gain_grad = jnp.sum(gather_small(norm_gain_grad.reshape(-1, N), (nctx, ndp)), axis=(0, 1)).reshape(model_width)
+    norm_gain_grad = sum_small(norm_gain_grad.reshape(-1, N), (nctx, ndp)).reshape(model_width)
     return (
         mixed.reshape(tokens.shape),
         tokens_grad.reshape(tokens.shape),

time: 972 us -> 968 us (level)
    unnamed x63 -> x66, local copies, waits for them, and re-layouts: 27 us -> 27.4 us
  transfers between devices with their start and end apart: 4 -> 4, of which waited for: 2 -> 2; matrix products, arithmetic and copies ran while one was open for 14% -> 13% of each run, Pallas kernels for 35% -> 36%
where the time goes in v5:
time: 968 us; the launch traced here: 962 us
  Pallas kernels  693 us (72%)
  matrix products  135 us (14%)
  local copies, waits for them, and re-layouts  43 us (4%)
  other arithmetic  40.1 us (4%)
  waiting for transfers between devices  34.7 us (4%)
  between operations  14.6 us (2%)
    pallas_call x1, Pallas kernels, gather_all(): pl.pallas_call(functools.partial(gather_body, order, sizes, parts), out_s...  322 us
    pallas_call x1, Pallas kernels, return_all(): pl.pallas_call(functools.partial(output_body, order, sizes, nw, parts), o...  272 us
    dot_general x3, matrix products, dot_first(): lax.dot_general(left_side, right_side, (((0,), (0,)), ((), ())), preferre...  51 us
    pallas_call x1, Pallas kernels, mixer_backward(): pl.pallas_call(backward_body, grid=(count,), in_specs=specs[:3] + [specs[...  44.2 us
    dot_general x2, matrix products, dot_last(): lax.dot_general(left_side, right_side, (((1,), (1,)), ((), ())), preferre...  39.7 us
    ppermute x2, waiting for transfers between devices, partner(): return lax.ppermute(value, 'ctx', [(i, i ^ 1) for i in range(nctx)])  34.6 us
    dot_general x1, matrix products, shards(): proj = jnp.dot(normed_all, weight_in, preferred_element_type=F32)  34.1 us
    pallas_call x1, Pallas kernels, mixer_forward(): pl.pallas_call(forward_body, grid=(count,), in_specs=proj_specs(width, la...  28 us
  transfers between devices with their start and end apart: 4, of which 2 were waited for; matrix products, arithmetic and copies ran while one was open for 13% of the time, Pallas kernels for 36%

profile of v5, /device:TPU:0, one launch (start us, length us, event | category | flops | bytes accessed | tf_op | source)
XLA Modules:
  0.0 962.0 jit_solution(2293386956574404467)
XLA Ops:
  9.5 3.2 fusion.5
  13.4 4.4 copy.65
  20.2 5.8 fusion.7.refs_0_
  26.0 322.4 %gather_inputs.1 = (bf16[2048,4096]{1,0:T(8,128)(2,1)}, bf16[2048,4096]{1,0:T(8,128)(2,1)}, bf16[2,4,512,1408]{3,2,1,0:T(8,128)(2,1)}, bf16[2,4,512,512]{3,2,1,0:T(8,128)(2,1)}) custom-call(bf16[512,4096]{1,0:T(8,128)(2,1)} %fusion.7.refs_0_, bf16[512,4096]{1,0:T(8,128)(2,1)} %bitcast.95, bf16[512,4096]{1,0:T(8,128)(2,1)} %bitcast.94, ...), custom_call_target="tpu_custom_call" | custom-call | tf_op jit(solution)/shard_map/gather_inputs/pallas_call | solution.py:630
  348.4 34.1 %fusion.20.gate_ref.x_ref.own_ref.step_ref.other_ref.edge_ref = f32[2048,1408]{1,0:T(8,128)} fusion(bf16[2048,4096]{1,0:T(8,128)(2,1)} %get-tuple-element.36, bf16[4096,1408]{1,0:T(8,128)(2,1)} %bitcast.130), kind=kOutput, calls=%fused_computation.53 | convolution fusion | flops 23622320128 | bytes 39845888 | tf_op jit(solution)/shard_map/dot_general | solution.py:953
  382.4 10.3 %fusion.21.up_ref = f32[2048,512]{1,0:T(8,128)} fusion(bf16[2048,4096]{1,0:T(8,128)(2,1)S(1)} %copy-done.25, bf16[4096,512]{1,0:T(8,128)(2,1)S(1)} %bitcast.132), kind=kOutput, calls=%fused_computation.54 | convolution fusion | flops 8589934592 | bytes 25165824 | tf_op jit(solution)/shard_map/dot_general | solution.py:952
  392.8 28.0 %mixer_forward.1 = (bf16[2048,768]{1,0:T(8,128)(2,1)S(1)}, f32[2048,512]{1,0:T(8,128)}, f32[8,128,512]{2,1,0:T(8,128)S(1)}, f32[2,2048]{1,0:T(2,128)S(1)}) custom-call(s32[1,1]{1,0:T(1,128)} %bitcast.1.odd_ref, f32[2048,1408]{1,0:T(8,128)} %fusion.20.gate_ref.x_ref.own_ref.step_ref.other_ref.edge_ref, ...), custom_call_target="tpu_custom_call" | custom-call | tf_op jit(solution)/shard_map/mixer_forward/pallas_call | solution.py:184
  427.6 4.2 multiply_convert_fusion
  431.9 11.8 %convolution_convert_fusion = bf16[2048,4096]{1,0:T(8,128)(2,1)} fusion(bf16[2048,512]{1,0:T(8,128)(2,1)S(1)} %multiply_convert_fusion, bf16[4096,512]{1,0:T(8,128)(2,1)S(1)} %bitcast.133), kind=kOutput, calls=%fused_computation.5 | convolution fusion | flops 8598323200 | bytes 23068672 | tf_op jit(solution)/shard_map/dot_general | solution.py:899
  445.1 44.2 %mixer_backward.1 = (bf16[2048,1024]{1,0:T(8,128)(2,1)}, bf16[2048,128]{1,0:T(8,128)(2,1)}, f32[2048,128]{1,0:T(8,128)}, f32[2048,128]{1,0:T(8,128)}, f32[5,512]...) custom-call(s32[1,1]{1,0:T(1,128)} %bitcast.1.odd_ref, ...), custom_call_target="tpu_custom_call" | custom-call | tf_op jit(solution)/shard_map/mixer_backward/pallas_call | solution.py:345
  489.7 24.1 %convolution_convert_fusion.2 = bf16[4096,1024]{1,0:T(8,128)(2,1)} fusion(bf16[2048,4096]{1,0:T(8,128)(2,1)} %get-tuple-element.36, bf16[2048,1024]{1,0:T(8,128)(2,1)} %get-tuple-element.44), kind=kOutput, calls=%fused_computation.20 | convolution fusion | flops 17184063488 | bytes 29360128 | tf_op jit(solution)/shard_map/dot_general | solution.py:903
  513.8 14.2 %convolution_convert_fusion.3 = bf16[4096,512]{1,0:T(8,128)(2,1)} fusion(bf16[2048,4096]{1,0:T(8,128)(2,1)} %get-tuple-element.38, bf16[2048,512]{1,0:T(8,128)(2,1)S(1)} %multiply_convert_fusion), kind=kOutput, calls=%fused_computation.21 | convolution fusion | flops 8592031744 | bytes 23068672 | tf_op jit(solution)/shard_map/dot_general | solution.py:903
  528.1 32.2 %collective-permute-done.1.theirs_ref = f32[2048,128]{1,0:T(8,128)S(1)} collective-permute-done((f32[2048,128]{1,0:T(8,128)}, f32[2048,128]{1,0:T(8,128)S(1)}, u32[]{:S(2)}, u32[]{:S(2)}) %collective-permute-start.1) | collective-permute-done | bytes 1048608 | tf_op jit(solution)/shard_map/ppermute | solution.py:930
  561.2 6.6 map_backward.1
  569.2 12.7 %convolution_convert_fusion.4 = bf16[4096,256]{1,0:T(8,128)(2,1)} fusion(bf16[2048,4096]{1,0:T(8,128)(2,1)} %get-tuple-element.36, bf16[2048,256]{1,0:T(8,128)(2,1)} %get-tuple-element.48), kind=kOutput, calls=%fused_computation.25 | convolution fusion | flops 4296015872 | bytes 19922944 | tf_op jit(solution)/shard_map/dot_general | solution.py:903
  581.9 28.0 %convolution_convert_fusion.1.refs_0_ = bf16[2048,4096]{1,0:T(8,128)(2,1)} fusion(bf16[4096,1408]{1,0:T(8,128)(2,1)} %bitcast.131, bf16[2048,256]{1,0:T(8,128)(2,1)S(1)} %copy-done.27, bf16[2048,1024]{1,0:T(8,128)(2,1)} %get-tuple-element.44), kind=kOutput, calls=%fused_computation.6 | convolution fusion | flops 21493710848 | bytes 32505856 | tf_op jit(solution)/shard_map/dot_general | solution.py:899
  609.9 271.9 %return_outputs.1 = (bf16[512,4096]{1,0:T(8,128)(2,1)}, f32[2,4,32,128]{3,2,1,0:T(8,128)}, bf16[512,2048]{1,0:T(8,128)(2,1)}, bf16[512,2048]{1,0:T(8,128)(2,1)},...) custom-call(bf16[2048,4096]{1,0:T(8,128)(2,1)} %convolution_convert_fusion.1.refs_0_, ...), custom_call_target="tpu_custom_call" | custom-call | tf_op jit(solution)/shard_map/return_outputs/pallas_call | solution.py:839
  887.2 2.8 maximum_convert_fusion
  890.0 11.1 %copy.63 = f32[512,2,2048]{2,1,0:T(2,128)} copy(f32[512,2,2048]{2,0,1:T(8,128)S(1)} %maximum_convert_fusion) | data formatting | bytes 16777216
  901.1 2.5 convert_element_type.68
  912.6 8.2 fusion.11
  920.9 20.3 %sum_small.1 = f32[32,128]{1,0:T(8,128)} custom-call(f32[32,128]{1,0:T(8,128)} %bitcast.115), custom_call_target="tpu_custom_call" | custom-call | tf_op jit(solution)/shard_map/sum_small/pallas_call | solution.py:887
  941.2 8.4 fusion.4
  949.6 4.7 copy.78
  (112 shorter events, 31.3 us)
Async XLA Ops:
  7.2 874.6 %reduce-scatter.2.cloned.1.call-start = ((), (), s32[]{:S(2)}) async-start(), calls=%async_computation.1 | async-start | bytes 17825792 | tf_op jit(solution)/shard_map/reduce_scatter | solution.py:907
  8.7 384.1 %copy-start.6 = (f32[1,512]{1,0:T(1,128)}, f32[1,512]{1,0:T(1,128)S(1)}, u32[]{:S(2)}) copy-start(f32[1,512]{1,0:T(1,128)S(1)} %fusion.34.gain_ref) | copy-start | bytes 6148
  9.5 383.3 %copy-start.5 = (f32[3,1,8]{2,0,1:T(4,128)}, f32[3,1,8]{2,0,1:T(4,128)S(1)}, u32[]{:S(2)}) copy-start(f32[3,1,8]{2,0,1:T(4,128)S(1)} %copy.75) | copy-start | bytes 292
  12.7 5.0 copy-start.18
  13.4 6.8 copy-start.19
  13.4 5.9 copy-start.12
  13.4 6.8 copy-start.13
  20.1 372.6 %copy-start.17 = (f32[5,128]{1,0:T(8,128)}, f32[5,128]{1,0:T(8,128)S(1)}, u32[]{:S(2)}) copy-start(f32[5,128]{1,0:T(8,128)S(1)} %get-tuple-element.109.kernel_ref) | copy-start | bytes 7684
  348.4 34.1 %copy-start.25 = (bf16[2048,4096]{1,0:T(8,128)(2,1)S(1)}, bf16[2048,4096]{1,0:T(8,128)(2,1)}, u32[]{:S(2)}) copy-start(bf16[2048,4096]{1,0:T(8,128)(2,1)} %get-tuple-element.38) | copy-start | bytes 50331652
  348.4 34.1 %copy-start.26 = (bf16[2,4,512,512]{3,2,1,0:T(8,128)(2,1)S(1)}, bf16[2,4,512,512]{3,2,1,0:T(8,128)(2,1)}, u32[]{:S(2)}) copy-start(bf16[2,4,512,512]{3,2,1,0:T(8,128)(2,1)} %get-tuple-element.39) | copy-start | bytes 12582916
  392.7 28.1 %copy-start.4 = (f32[5,768]{1,0:T(8,128)}, f32[5,768]{1,0:T(8,128)S(1)}, u32[]{:S(2)}) copy-start(f32[5,768]{1,0:T(8,128)S(1)} %pad_maximum_fusion.kernel_ref) | copy-start | bytes 46084
  423.8 3.7 collective-permute-start
  443.6 506.0 %all-gather.2.cloned.1.call-start = ((), (), s32[]{:S(2)}) async-start(), calls=%async_computation.2 | async-start | bytes 5242880 | tf_op jit(solution)/shard_map/all_gather | solution.py:999
  489.3 71.0 %collective-permute-start.1 = (f32[2048,128]{1,0:T(8,128)}, f32[2048,128]{1,0:T(8,128)S(1)}, u32[]{:S(2)}, u32[]{:S(2)}) collective-permute-start(f32[2048,128]{1,0:T(8,128)} %get-tuple-element.46), channel_id=1, source_target_pairs={{0,4},{4,0},{8,12},{12,8},{1,5},{5,1},{9,13},{13,9},{2,6},{6,2},{1... | collective-permute-start | bytes 3145736 | tf_op jit(solution)/shard_map/ppermute | solution.py:930
  513.8 14.3 %copy-start.21 = (f32[5,512]{1,0:T(8,128)S(1)}, f32[5,512]{1,0:T(8,128)}, u32[]{:S(2)}) copy-start(f32[5,512]{1,0:T(8,128)} %get-tuple-element.49) | copy-start | bytes 30724
  513.8 14.3 %copy-start.24 = (f32[3,8]{1,0:T(4,128)S(1)}, f32[3,8]{1,0:T(4,128)}, u32[]{:S(2)}) copy-start(f32[3,8]{1,0:T(4,128)} %get-tuple-element.51) | copy-start | bytes 292
  561.2 6.6 copy-start.23
  569.2 12.7 %copy-start.27 = (bf16[2048,256]{1,0:T(8,128)(2,1)S(1)}, bf16[2048,256]{1,0:T(8,128)(2,1)}, u32[]{:S(2)}) copy-start(bf16[2048,256]{1,0:T(8,128)(2,1)} %get-tuple-element.48) | copy-start | bytes 3145732
  890.0 11.1 %copy-start.10 = (bf16[512,2048]{1,0:T(8,128)(2,1)S(1)}, bf16[512,2048]{1,0:T(8,128)(2,1)}, u32[]{:S(2)}) copy-start(bf16[512,2048]{1,0:T(8,128)(2,1)} %get-tuple-element.60) | copy-start | bytes 6291460
  901.1 5.8 copy-start.9
  903.6 9.0 copy-start.14
  903.6 9.0 copy-start.20
  907.7 33.5 %copy-start.22 = (f32[512]{0:T(512)S(1)}, f32[512]{0:T(512)}, u32[]{:S(2)}) copy-start(f32[512]{0:T(512)} %get-tuple-element.111) | copy-start | bytes 6148
  941.2 13.7 %copy-start.1 = (f32[5,2048]{1,0:T(8,128)S(1)}, f32[5,2048]{1,0:T(8,128)}, u32[]{:S(2)}) copy-start(f32[5,2048]{1,0:T(8,128)} %param.16) | copy-start | bytes 122884
  (8 other events, 21.3 us)
Sparse Core Ops, SparseCore 0:
  443.8 203.5 reduce-scatter.1
  886.0 45.4 all-gather.1

commit v6 on v5

--- a/solution.py
+++ b/solution.py
@@ -1006,7 +1006,8 @@
     )
     tokens_grad = cot.astype(F32) + grad_hidden
 
-    zx_weight_grad = jnp.stack([back_z, back_x], axis=1).astype(F32)
+    upper = lax.broadcasted_iota(jnp.int32, (rows, 2, inner), 1) == 0
+    zx_weight_grad = jnp.where(upper, back_z[:, None, :], back_x[:, None, :]).astype(F32)
     back_rest = back_rest.astype(F32)
     bc_weight_grad = back_rest[:, :, :N].reshape(groups, 2, rows, N).transpose(2, 1, 0, 3).reshape(rows, 2, groups * N)
     dt_weight_grad = back_rest[:, :, N : N + heads].transpose(1, 0, 2).reshape(rows, nctx * heads)

time: 968 us -> 965 us (level)
  local copies, waits for them, and re-layouts: 43 us -> 31.9 us
    unnamed x66 -> x67, local copies, waits for them, and re-layouts: 27.4 us -> 16.4 us
where the time goes in v6:
time: 965 us; the launch traced here: 958 us
  Pallas kernels  693 us (72%)
  matrix products  135 us (14%)
  other arithmetic  47.7 us (5%)
  waiting for transfers between devices  34.5 us (4%)
  local copies, waits for them, and re-layouts  31.9 us (3%)
  between operations  14.6 us (2%)
    pallas_call x1, Pallas kernels, gather_all(): pl.pallas_call(functools.partial(gather_body, order, sizes, parts), out_s...  322 us
    pallas_call x1, Pallas kernels, return_all(): pl.pallas_call(functools.partial(output_body, order, sizes, nw, parts), o...  272 us
    dot_general x3, matrix products, dot_first(): lax.dot_general(left_side, right_side, (((0,), (0,)), ((), ())), preferre...  51 us
    pallas_call x1, Pallas kernels, mixer_backward(): pl.pallas_call(backward_body, grid=(count,), in_specs=specs[:3] + [specs[...  44.2 us
    dot_general x2, matrix products, dot_last(): lax.dot_general(left_side, right_side, (((1,), (1,)), ((), ())), preferre...  39.8 us
    ppermute x2, waiting for transfers between devices, partner(): return lax.ppermute(value, 'ctx', [(i, i ^ 1) for i in range(nctx)])  34.5 us
    dot_general x1, matrix products, shards(): proj = jnp.dot(normed_all, weight_in, preferred_element_type=F32)  34.1 us
    pallas_call x1, Pallas kernels, mixer_forward(): pl.pallas_call(forward_body, grid=(count,), in_specs=proj_specs(width, la...  28 us
  transfers between devices with their start and end apart: 4, of which 2 were waited for; matrix products, arithmetic and copies ran while one was open for 13% of the time, Pallas kernels for 36%

profile of v6, /device:TPU:0, one launch (start us, length us, event | category | flops | bytes accessed | tf_op | source)
XLA Modules:
  0.0 958.2 jit_solution(13233175638147563846)
XLA Ops:
  9.5 3.2 fusion.5
  13.4 4.4 copy.61
  20.2 5.8 fusion.7.refs_0_
  26.0 322.4 %gather_inputs.1 = (bf16[2048,4096]{1,0:T(8,128)(2,1)}, bf16[2048,4096]{1,0:T(8,128)(2,1)}, bf16[2,4,512,1408]{3,2,1,0:T(8,128)(2,1)}, bf16[2,4,512,512]{3,2,1,0:T(8,128)(2,1)}) custom-call(bf16[512,4096]{1,0:T(8,128)(2,1)} %fusion.7.refs_0_, bf16[512,4096]{1,0:T(8,128)(2,1)} %bitcast.93, bf16[512,4096]{1,0:T(8,128)(2,1)} %bitcast.92, ...), custom_call_target="tpu_custom_call" | custom-call | tf_op jit(solution)/shard_map/gather_inputs/pallas_call | solution.py:630
  348.4 34.1 %fusion.21.gate_ref.x_ref.own_ref.step_ref.other_ref.edge_ref = f32[2048,1408]{1,0:T(8,128)} fusion(bf16[2048,4096]{1,0:T(8,128)(2,1)} %get-tuple-element.36, bf16[4096,1408]{1,0:T(8,128)(2,1)} %bitcast.126), kind=kOutput, calls=%fused_computation.55 | convolution fusion | flops 23622320128 | bytes 39845888 | tf_op jit(solution)/shard_map/dot_general | solution.py:953
  382.4 10.3 %fusion.22.up_ref = f32[2048,512]{1,0:T(8,128)} fusion(bf16[2048,4096]{1,0:T(8,128)(2,1)S(1)} %copy-done.26, bf16[4096,512]{1,0:T(8,128)(2,1)S(1)} %bitcast.128), kind=kOutput, calls=%fused_computation.56 | convolution fusion | flops 8589934592 | bytes 25165824 | tf_op jit(solution)/shard_map/dot_general | solution.py:952
  392.8 28.0 %mixer_forward.1 = (bf16[2048,768]{1,0:T(8,128)(2,1)S(1)}, f32[2048,512]{1,0:T(8,128)}, f32[8,128,512]{2,1,0:T(8,128)S(1)}, f32[2,2048]{1,0:T(2,128)S(1)}) custom-call(s32[1,1]{1,0:T(1,128)} %bitcast.1.odd_ref, f32[2048,1408]{1,0:T(8,128)} %fusion.21.gate_ref.x_ref.own_ref.step_ref.other_ref.edge_ref, ...), custom_call_target="tpu_custom_call" | custom-call | tf_op jit(solution)/shard_map/mixer_forward/pallas_call | solution.py:184
  425.1 2.5 collective-permute-done
  427.6 4.2 multiply_convert_fusion
  431.8 11.7 %convolution_convert_fusion = bf16[2048,4096]{1,0:T(8,128)(2,1)} fusion(bf16[2048,512]{1,0:T(8,128)(2,1)S(1)} %multiply_convert_fusion, bf16[4096,512]{1,0:T(8,128)(2,1)S(1)} %bitcast.129), kind=kOutput, calls=%fused_computation.5 | convolution fusion | flops 8598323200 | bytes 23068672 | tf_op jit(solution)/shard_map/dot_general | solution.py:899
  445.0 44.2 %mixer_backward.1 = (bf16[2048,1024]{1,0:T(8,128)(2,1)}, bf16[2048,128]{1,0:T(8,128)(2,1)}, f32[2048,128]{1,0:T(8,128)}, f32[2048,128]{1,0:T(8,128)}, f32[5,512]...) custom-call(s32[1,1]{1,0:T(1,128)} %bitcast.1.odd_ref, ...), custom_call_target="tpu_custom_call" | custom-call | tf_op jit(solution)/shard_map/mixer_backward/pallas_call | solution.py:345
  489.8 24.1 %convolution_convert_fusion.2 = bf16[4096,1024]{1,0:T(8,128)(2,1)} fusion(bf16[2048,4096]{1,0:T(8,128)(2,1)} %get-tuple-element.36, bf16[2048,1024]{1,0:T(8,128)(2,1)} %get-tuple-element.44), kind=kOutput, calls=%fused_computation.21 | convolution fusion | flops 17184063488 | bytes 29360128 | tf_op jit(solution)/shard_map/dot_general | solution.py:903
  513.8 14.2 %convolution_convert_fusion.3 = bf16[4096,512]{1,0:T(8,128)(2,1)} fusion(bf16[2048,4096]{1,0:T(8,128)(2,1)} %get-tuple-element.38, bf16[2048,512]{1,0:T(8,128)(2,1)S(1)} %multiply_convert_fusion), kind=kOutput, calls=%fused_computation.22 | convolution fusion | flops 8592031744 | bytes 23068672 | tf_op jit(solution)/shard_map/dot_general | solution.py:903
  528.2 32.0 %collective-permute-done.1.theirs_ref = f32[2048,128]{1,0:T(8,128)S(1)} collective-permute-done((f32[2048,128]{1,0:T(8,128)}, f32[2048,128]{1,0:T(8,128)S(1)}, u32[]{:S(2)}, u32[]{:S(2)}) %collective-permute-start.1) | collective-permute-done | bytes 1048608 | tf_op jit(solution)/shard_map/ppermute | solution.py:930
  561.1 6.6 map_backward.1
  569.1 12.7 %convolution_convert_fusion.4 = bf16[4096,256]{1,0:T(8,128)(2,1)} fusion(bf16[2048,4096]{1,0:T(8,128)(2,1)} %get-tuple-element.36, bf16[2048,256]{1,0:T(8,128)(2,1)} %get-tuple-element.48), kind=kOutput, calls=%fused_computation.26 | convolution fusion | flops 4296015872 | bytes 19922944 | tf_op jit(solution)/shard_map/dot_general | solution.py:903
  581.8 28.0 %convolution_convert_fusion.1.refs_0_ = bf16[2048,4096]{1,0:T(8,128)(2,1)} fusion(bf16[4096,1408]{1,0:T(8,128)(2,1)} %bitcast.127, bf16[2048,256]{1,0:T(8,128)(2,1)S(1)} %copy-done.28, bf16[2048,1024]{1,0:T(8,128)(2,1)} %get-tuple-element.44), kind=kOutput, calls=%fused_computation.6 | convolution fusion | flops 21493710848 | bytes 32505856 | tf_op jit(solution)/shard_map/dot_general | solution.py:899
  609.8 272.3 %return_outputs.1 = (bf16[512,4096]{1,0:T(8,128)(2,1)}, f32[2,4,32,128]{3,2,1,0:T(8,128)}, bf16[512,2048]{1,0:T(8,128)(2,1)}, bf16[512,2048]{1,0:T(8,128)(2,1)},...) custom-call(bf16[2048,4096]{1,0:T(8,128)(2,1)} %convolution_convert_fusion.1.refs_0_, ...), custom_call_target="tpu_custom_call" | custom-call | tf_op jit(solution)/shard_map/return_outputs/pallas_call | solution.py:839
  887.5 4.2 convert_element_type.68
  900.7 11.0 %fusion.15 = f32[512,2,2048]{2,1,0:T(2,128)} fusion(pred[2]{0:T(512)(128)(4,1)S(1)} %iota_compare_fusion, bf16[512,2048]{1,0:T(8,128)(2,1)} %get-tuple-element.57, bf16[512,2048]{1,0:T(8,128)(2,1)} %get-tuple-element.56), kind=kLoop, calls=%fused_computation.27 | loop fusion | flops 4194304 | bytes 12582914 | tf_op jit(solution)/shard_map/convert_element_type | solution.py:1010
  911.7 6.0 fusion.11
  917.7 19.6 %sum_small.1 = f32[32,128]{1,0:T(8,128)} custom-call(f32[32,128]{1,0:T(8,128)} %bitcast.111), custom_call_target="tpu_custom_call" | custom-call | tf_op jit(solution)/shard_map/sum_small/pallas_call | solution.py:887
  937.4 8.4 fusion.4
  945.8 4.7 copy.74
  (114 shorter events, 28.8 us)
Async XLA Ops:
  7.2 874.9 %reduce-scatter.2.cloned.1.call-start = ((), (), s32[]{:S(2)}) async-start(), calls=%async_computation.1 | async-start | bytes 17825792 | tf_op jit(solution)/shard_map/reduce_scatter | solution.py:907
  8.7 384.1 %copy-start.6 = (f32[1,512]{1,0:T(1,128)}, f32[1,512]{1,0:T(1,128)S(1)}, u32[]{:S(2)}) copy-start(f32[1,512]{1,0:T(1,128)S(1)} %fusion.35.gain_ref) | copy-start | bytes 6148
  9.5 383.3 %copy-start.5 = (f32[3,1,8]{2,0,1:T(4,128)}, f32[3,1,8]{2,0,1:T(4,128)S(1)}, u32[]{:S(2)}) copy-start(f32[3,1,8]{2,0,1:T(4,128)S(1)} %copy.71) | copy-start | bytes 292
  13.4 6.8 copy-start.20
  13.4 5.9 copy-start.13
  13.4 6.8 copy-start.14
  20.2 372.6 %copy-start.18 = (f32[5,128]{1,0:T(8,128)}, f32[5,128]{1,0:T(8,128)S(1)}, u32[]{:S(2)}) copy-start(f32[5,128]{1,0:T(8,128)S(1)} %get-tuple-element.65.kernel_ref) | copy-start | bytes 7684
  348.4 34.1 %copy-start.26 = (bf16[2048,4096]{1,0:T(8,128)(2,1)S(1)}, bf16[2048,4096]{1,0:T(8,128)(2,1)}, u32[]{:S(2)}) copy-start(bf16[2048,4096]{1,0:T(8,128)(2,1)} %get-tuple-element.38) | copy-start | bytes 50331652
  348.4 34.1 %copy-start.27 = (bf16[2,4,512,512]{3,2,1,0:T(8,128)(2,1)S(1)}, bf16[2,4,512,512]{3,2,1,0:T(8,128)(2,1)}, u32[]{:S(2)}) copy-start(bf16[2,4,512,512]{3,2,1,0:T(8,128)(2,1)} %get-tuple-element.39) | copy-start | bytes 12582916
  392.8 28.0 %copy-start.4 = (f32[5,768]{1,0:T(8,128)}, f32[5,768]{1,0:T(8,128)S(1)}, u32[]{:S(2)}) copy-start(f32[5,768]{1,0:T(8,128)S(1)} %pad_maximum_fusion.kernel_ref) | copy-start | bytes 46084
  423.8 3.7 collective-permute-start
  443.6 502.1 %all-gather.2.cloned.1.call-start = ((), (), s32[]{:S(2)}) async-start(), calls=%async_computation.2 | async-start | bytes 5242880 | tf_op jit(solution)/shard_map/all_gather | solution.py:999
  489.3 70.9 %collective-permute-start.1 = (f32[2048,128]{1,0:T(8,128)}, f32[2048,128]{1,0:T(8,128)S(1)}, u32[]{:S(2)}, u32[]{:S(2)}) collective-permute-start(f32[2048,128]{1,0:T(8,128)} %get-tuple-element.46), channel_id=1, source_target_pairs={{0,4},{4,0},{8,12},{12,8},{1,5},{5,1},{9,13},{13,9},{2,6},{6,2},{1... | collective-permute-start | bytes 3145736 | tf_op jit(solution)/shard_map/ppermute | solution.py:930
  513.8 14.3 %copy-start.22 = (f32[5,512]{1,0:T(8,128)S(1)}, f32[5,512]{1,0:T(8,128)}, u32[]{:S(2)}) copy-start(f32[5,512]{1,0:T(8,128)} %get-tuple-element.49) | copy-start | bytes 30724
  513.8 14.3 %copy-start.25 = (f32[3,8]{1,0:T(4,128)S(1)}, f32[3,8]{1,0:T(4,128)}, u32[]{:S(2)}) copy-start(f32[3,8]{1,0:T(4,128)} %get-tuple-element.51) | copy-start | bytes 292
  561.1 6.6 copy-start.24
  569.1 12.7 %copy-start.28 = (bf16[2048,256]{1,0:T(8,128)(2,1)S(1)}, bf16[2048,256]{1,0:T(8,128)(2,1)}, u32[]{:S(2)}) copy-start(bf16[2048,256]{1,0:T(8,128)(2,1)} %get-tuple-element.48) | copy-start | bytes 3145732
  887.5 7.4 copy-start.11
  900.7 11.0 %copy-start.7 = (bf16[1,512,4096]{2,1,0:T(8,128)(2,1)S(1)}, bf16[1,512,4096]{2,1,0:T(8,128)(2,1)}, u32[]{:S(2)}) copy-start(bf16[1,512,4096]{2,1,0:T(8,128)(2,1)} %param.11) | copy-start | bytes 12582916
  900.7 11.0 %copy-start.8 = (bf16[512,4096]{1,0:T(8,128)(2,1)S(1)}, bf16[512,4096]{1,0:T(8,128)(2,1)}, u32[]{:S(2)}) copy-start(bf16[512,4096]{1,0:T(8,128)(2,1)} %get-tuple-element.55) | copy-start | bytes 12582916
  900.7 11.0 %copy-start.15 = (f32[4096]{0:T(1024)S(1)}, f32[4096]{0:T(1024)}, u32[]{:S(2)}) copy-start(f32[4096]{0:T(1024)} %param.12) | copy-start | bytes 49156
  900.7 11.0 %copy-start.21 = (f32[512]{0:T(512)S(1)}, f32[512]{0:T(512)}, u32[]{:S(2)}) copy-start(f32[512]{0:T(512)} %copy-done.20) | copy-start | bytes 6148
  911.6 25.7 %copy-start.23 = (f32[512]{0:T(512)S(1)}, f32[512]{0:T(512)}, u32[]{:S(2)}) copy-start(f32[512]{0:T(512)} %get-tuple-element.67) | copy-start | bytes 6148
  945.7 5.4 copy-start.1
  (9 other events, 23.3 us)
Sparse Core Ops, SparseCore 0:
  443.7 203.3 reduce-scatter.1
  886.3 44.8 all-gather.1
